TPU v7x, 32 devices: a whole 2x2x4 slice. The times are simulated.
32 devices in a mesh: rows: 8 (over z, y), modes: 4 (over x, core).
Axes of the slice: x: 2, y: 2, z: 4, core: 2. Of those that a mesh axis runs over, the one named last changes fastest.
Arguments:
- mode_slab: bfloat16 [4096, 512], P('rows', 'modes'), may hold values from -25 to 25
- mass_diag: float32 [4096], P('rows'), may hold values from 9.5 to 19
- mass_gain: float32 [4096], P('rows'), may hold values from 0.5 to 1.5
- band_coef: float32 [4], replicated, may hold values from 0.2 to 0.5
- band_offsets: int32 [4], replicated, may hold values from 1 to 64, as said below
- boundary_blocks: int32 [16, 4], P('rows'), may hold values from 0 to 31, as said below
- boundary_counts: int32 [16], P('rows'), may hold values from 2 to 4, as said below
- boundary_modes: bfloat16 [16, 512, 512], P('rows'), may hold values from -0.5 to 0.5
Outputs:
- projected: bfloat16 [16, 512, 512], P('rows', 'modes')
Inputs may be any that keep to these rules, and one draw needn't show every extreme that they name: `band_offsets`: the offsets are distinct and one of them equals 64. `boundary_blocks`: entries of one component are distinct. For component c with e = c // 2, every entry b (used or not) satisfies (b - e * 4 + 512 // 256) mod (32) < 8. Among the used entries of the components of each index e of rows, one is the block just below e's rows and one the block just above them, counted cyclically. `boundary_counts`: some component uses all 4 blocks.
All inputs are finite; a program needn't handle non-finite values.
Results may differ from a plain program's by a relative error of at most 0.0035.
The roundings to bfloat16 on the way count: a program that leaves them out, or rounds other values in their place, can miss the bound.
Values may be sent and summed in bfloat16 or wider, within the bound.
No kernel may reach another device: no remote copies, remote signals or barrier semaphores. Data moves between devices by JAX's collectives and lax.ppermute only.
A program may use at most 64 MiB of HBM per device.

v0:
```python
import jax
import jax.numpy as jnp
from jax import lax
from jax.sharding import PartitionSpec as P

CB = 512
BLOCK = 128
BMAX = 4
NOFF = 4
BAND = 64


def padded_2(block, sides, width, periodic):
    for axis, dim in sides:
        count = lax.axis_size(axis)
        forward = [(i, i + 1) for i in range(count - 1)]
        if periodic:
            forward.append((count - 1, 0))
        backward = [(target, source) for source, target in forward]
        low = lax.ppermute(
            lax.slice_in_dim(block, block.shape[dim] - width, None, axis=dim), axis, forward
        )
        high = lax.ppermute(lax.slice_in_dim(block, 0, width, axis=dim), axis, backward)
        block = jnp.concatenate([low, block, high], axis=dim)
    return block


def local(
    mode_slab,
    mass_diag,
    mass_gain,
    band_coef,
    band_offsets,
    boundary_blocks,
    boundary_counts,
    boundary_modes,
):
    rows_dev, mode_cols = mode_slab.shape
    per_dev = rows_dev // BLOCK
    rim_rows = per_dev // 2 * BLOCK
    slab_float = mode_slab.astype(jnp.float32)
    scaled = (mass_gain[:, None] * slab_float).astype(jnp.bfloat16)
    padded = padded_2(scaled, (("rows", 0),), BAND, False)
    neighbour = jnp.zeros((rows_dev, mode_cols), jnp.float32)
    for j in range(NOFF):
        offset = band_offsets[j]
        upward = lax.dynamic_slice_in_dim(padded, BAND + offset, rows_dev, 0)
        downward = lax.dynamic_slice_in_dim(padded, BAND - offset, rows_dev, 0)
        neighbour = neighbour + band_coef[j] * (
            upward.astype(jnp.float32) + downward.astype(jnp.float32)
        )
    mass_image = (mass_diag[:, None] * slab_float + mass_gain[:, None] * neighbour).astype(
        jnp.bfloat16
    )
    every_mode = lax.all_gather(mass_image, "modes", axis=1, tiled=True)
    full_order = every_mode.shape[1]
    total_rows = rows_dev * lax.axis_size("rows")
    partial_value = (
        lax.dot_general(
            every_mode, mode_slab, (((0,), (0,)), ((), ())), preferred_element_type=jnp.float32
        )
        / total_rows
    )
    column_block = lax.psum(partial_value, "rows")
    gram_matrix = lax.all_gather(column_block, "modes", axis=1, tiled=True)
    lower_factor = jnp.linalg.cholesky(gram_matrix)
    first_column = lax.axis_index("modes") * mode_cols
    unit_columns = (
        lax.broadcasted_iota(jnp.int32, (full_order, mode_cols), 0)
        == lax.broadcasted_iota(jnp.int32, (full_order, mode_cols), 1) + first_column
    ).astype(jnp.float32)
    inverse = jax.scipy.linalg.solve_triangular(
        lower_factor, unit_columns, lower=True, trans=1
    ).astype(jnp.bfloat16)
    mass_basis = jnp.dot(every_mode, inverse, preferred_element_type=jnp.float32).astype(
        jnp.bfloat16
    )
    extended = padded_2(mass_basis, (("rows", 0),), rim_rows, True)
    total_blocks = per_dev * lax.axis_size("rows")
    window_start = lax.axis_index("rows") * per_dev - per_dev // 2
    local_blocks = jnp.mod(boundary_blocks - window_start, total_blocks)
    owned = boundary_modes.shape[0]
    shaped = boundary_modes.reshape(owned, BMAX, BLOCK, CB)
    row_index = local_blocks[:, :, None] * BLOCK + jnp.arange(BLOCK, dtype=jnp.int32)[None, None, :]
    picked = jnp.take(extended, row_index, axis=0)
    in_use = jnp.arange(BMAX, dtype=jnp.int32)[None, :] < boundary_counts[:, None]
    picked = jnp.where(in_use[:, :, None, None], picked, jnp.zeros_like(picked))
    result = jnp.einsum("csbk,csbm->ckm", picked, shaped, preferred_element_type=jnp.float32)
    return result.astype(jnp.bfloat16)


def solution(mesh):
    in_specs = (
        P("rows", "modes"),
        P("rows"),
        P("rows"),
        P(),
        P(),
        P("rows", None),
        P("rows"),
        P("rows", None, None),
    )
    out_specs = P("rows", "modes", None)
    return jax.shard_map(local, mesh=mesh, in_specs=in_specs, out_specs=out_specs, check_vma=False)
```

profile of v0, /device:TPU:0, one launch (start us, length us, event | category | flops | bytes accessed | tf_op | source)
XLA Modules:
  0.0 294.4 jit_solution(5894387732189599143)
XLA Ops:
  6.5 1.1 fusion.4
  7.7 4.9 %collective-permute-start = (bf16[64,128]{1,0:T(8,128)(2,1)S(1)}, bf16[64,128]{1,0:T(8,128)(2,1)S(1)}, u32[]{:S(2)}, u32[]{:S(2)}) collective-permute-start(bf16[64,128]{1,0:T(8,128)(2,1)S(1)} %get-tuple-element.25), channel_id=1, source_target_pairs={{0,4},{4,8},{8,12},{12,16},{16,20},{20,24},{24,28},{1,5},{5,9},{9,... | collective-permute-start | bytes 49160 | tf_op jit(solution)/shard_map/ppermute | solution.py:20
  12.6 1.3 collective-permute-start.1
  13.9 0.7 fusion.59
  14.6 0.6 fusion.58
  25.6 0.8 copy-done.6
  26.4 2.8 fusion.3
  29.2 7.2 %all_gather.6 = bf16[512,512]{1,0:T(8,128)(2,1)S(1)} all-gather(bf16[512,128]{1,0:T(8,128)(2,1)S(1)} %fusion.3), channel_id=1, replica_groups=mesh['rows'=8,'modes'=4] {'modes'}, dimensions={1}, use_global_device_ids=true | all-gather | bytes 655360 | tf_op jit(solution)/shard_map/all_gather | solution.py:55
  36.4 0.8 copy-done.4
  37.3 1.0 convolution_multiply_fusion
  38.3 72.4 %all-reduce.3.cloned.1.call-done = f32[512,128]{0,1:T(8,128)} async-done(((f32[512,128]{0,1:T(8,128)}), f32[512,128]{0,1:T(8,128)}) %all-reduce.3.cloned.1.call-update) | async-done | bytes 262160 | tf_op jit(solution)/shard_map/psum | solution.py:64
  110.7 0.6 iota_multiply_fusion
  111.3 0.7 copy-done.12
  112.1 0.7 fusion.44
  112.8 15.5 %all-gather.2.cloned.1.call-done = f32[512,512]{0,1:T(8,128)} async-done(((f32[512,128]{0,1:T(8,128)}), f32[512,512]{0,1:T(8,128)}) %all-gather.2.cloned.1.call-update) | async-done | bytes 1048592 | tf_op jit(solution)/shard_map/all_gather | solution.py:65
  128.4 1.6 copy.13
  130.3 1.0 copy-done.2
  131.3 11.7 %cholesky.104 = f32[128,128]{1,0:T(8,128)S(1)} custom-call(f32[128,128]{1,0:T(8,128)S(1)} %cholesky.266), custom_call_target="Cholesky" | custom-call | tf_op jit(solution)/shard_map/jit(cholesky)/cholesky | solution.py:66
  143.1 9.8 %custom-call.31 = f32[1,128,128]{1,2,0:T(8,128)S(1)} custom-call(f32[1,128,128]{2,1,0:T(8,128)S(1)} %get-tuple-element.36), custom_call_target="InvertDiagBlocksLowerTriangular" | custom-call | tf_op jit(solution)/shard_map/jit(cholesky)/cholesky | solution.py:66
  153.6 0.7 copy-done.7
  154.3 11.7 %cholesky.217 = f32[128,128]{1,0:T(8,128)S(1)} custom-call(f32[128,128]{1,0:T(8,128)S(1)} %cholesky.270), custom_call_target="Cholesky" | custom-call | tf_op jit(solution)/shard_map/jit(cholesky)/cholesky | solution.py:66
  166.1 9.9 %custom-call.32 = f32[1,128,128]{1,2,0:T(8,128)S(1)} custom-call(f32[1,128,128]{2,1,0:T(8,128)S(1)} %get-tuple-element.33), custom_call_target="InvertDiagBlocksLowerTriangular" | custom-call | tf_op jit(solution)/shard_map/jit(cholesky)/cholesky | solution.py:66
  176.0 1.2 convolution_dynamic-update-slice_fusion
  177.6 0.6 cholesky.275
  178.2 13.2 %cholesky.238 = f32[128,128]{1,0:T(8,128)} custom-call(f32[128,128]{1,0:T(8,128)} %cholesky.275), custom_call_target="Cholesky" | custom-call | tf_op jit(solution)/shard_map/jit(cholesky)/cholesky | solution.py:66
  191.4 1.5 select_reduce_fusion.1
  192.9 0.7 compare_reduce_fusion.1
  193.6 11.3 %custom-call.33 = f32[1,128,128]{1,2,0:T(8,128)} custom-call(f32[1,128,128]{2,1,0:T(8,128)} %get-tuple-element.30), custom_call_target="InvertDiagBlocksLowerTriangular" | custom-call | tf_op jit(solution)/shard_map/jit(cholesky)/cholesky | solution.py:66
  204.8 1.0 convolution_dynamic-update-slice_fusion.1
  206.3 11.7 %cholesky.255 = f32[128,128]{1,0:T(8,128)S(1)} custom-call(f32[128,128]{1,0:T(8,128)S(1)} %convolution_subtract_fusion.5), custom_call_target="Cholesky" | custom-call | tf_op jit(solution)/shard_map/jit(cholesky)/cholesky | solution.py:66
  218.2 0.7 compare_reduce_fusion
  218.9 0.7 compare_reduce_fusion.2
  222.8 9.9 %while.1 = (s32[]{:T(128)}, f32[512,512]{1,0:T(8,128)S(1)}, s32[4,2]{0,1:T(2,128)S(1)}, f32[4,128,128]{2,1,0:T(8,128)}, s32[]{:T(128)}) while((s32[]{:T(128)}, f32[512,512]{1,0:T(8,128)S(1)}, s32[4,2]{0,1:T(2,128)S(1)}, f32[4,128,128]{2,1,0:T(8,128)}, s32[]{:T(128)}) %tuple.39), condition=%wide.while_cond, body=%wide.while_body.sunk | while | flops 2 | bytes 132705 | solution.py:72
  222.8 0.5 fusion.73
  223.4 1.9 bitcast_dynamic-update-slice_fusion.2
  225.3 0.5 fusion.73
  225.8 1.9 bitcast_dynamic-update-slice_fusion.2
  227.8 0.5 fusion.73
  228.3 1.9 bitcast_dynamic-update-slice_fusion.2
  230.2 0.5 fusion.73
  230.8 1.9 bitcast_dynamic-update-slice_fusion.2
  232.6 40.1 %custom-call.34 = f32[4,128,128]{1,2,0:T(8,128)S(1)} custom-call(f32[4,128,128]{2,1,0:T(8,128)} %get-tuple-element.12), custom_call_target="InvertDiagBlocksLowerTriangular" | custom-call | tf_op jit(solution)/shard_map/jit(_solve_triangular)/triangular_solve | solution.py:72
  272.8 0.9 fusion.60
  275.9 1.5 collective-permute-start.2
  277.4 3.3 %collective-permute-start.3 = (bf16[256,128]{1,0:T(8,128)(2,1)S(1)}, bf16[256,128]{1,0:T(8,128)(2,1)S(1)}, u32[]{:S(2)}, u32[]{:S(2)}) collective-permute-start(bf16[256,128]{1,0:T(8,128)(2,1)S(1)} %get-tuple-element.24), channel_id=1, source_target_pairs={{4,0},{8,4},{12,8},{16,12},{20,16},{24,20},{28,24},{0,28},{5,1},{9... | collective-permute-start | bytes 196616 | tf_op jit(solution)/shard_map/ppermute | solution.py:23
  280.8 2.2 collective-permute-done.2
  283.1 3.2 %gather_fusion = bf16[1024,128]{1,0:T(8,128)(2,1)S(1)} fusion(bf16[1024,128]{1,0:T(8,128)(2,1)S(1)} %pad_maximum_fusion, s32[1024]{0:T(1024)S(1)} %broadcast_clamp_fusion), kind=kCustom, calls=%fused_computation | custom fusion | bytes 528384 | tf_op jit(solution)/shard_map/jit(_take)/gather | solution.py:85
  286.5 1.1 fusion
  (68 shorter events, 5.9 us)
Async XLA Ops:
  6.5 280.0 %copy-start = (bf16[2,512,512]{2,1,0:T(8,128)(2,1)S(1)}, bf16[2,512,512]{2,1,0:T(8,128)(2,1)}, u32[]{:S(2)}) copy-start(bf16[2,512,512]{2,1,0:T(8,128)(2,1)} %param.15) | copy-start | bytes 3145732
  6.5 104.1 %all-reduce.3.cloned.1.call-start = ((), (), s32[]{:S(2)}) async-start(), calls=%async_computation | async-start | bytes 524288 | tf_op jit(solution)/shard_map/psum | solution.py:64
  7.7 6.2 %copy-start.9 = (s32[4]{0:T(128)S(1)}, s32[4]{0:T(128)}, u32[]{:S(2)}) copy-start(s32[4]{0:T(128)} %param.12) | copy-start | bytes 52
  7.7 17.8 %collective-permute-start = (bf16[64,128]{1,0:T(8,128)(2,1)S(1)}, bf16[64,128]{1,0:T(8,128)(2,1)S(1)}, u32[]{:S(2)}, u32[]{:S(2)}) collective-permute-start(bf16[64,128]{1,0:T(8,128)(2,1)S(1)} %get-tuple-element.25), channel_id=1, source_target_pairs={{0,4},{4,8},{8,12},{12,16},{16,20},{20,24},{24,28},{1,5},{5,9},{9,... | collective-permute-start | bytes 49160 | tf_op jit(solution)/shard_map/ppermute | solution.py:20
  12.6 12.9 %collective-permute-start.1 = (bf16[64,128]{1,0:T(8,128)(2,1)S(1)}, bf16[64,128]{1,0:T(8,128)(2,1)S(1)}, u32[]{:S(2)}, u32[]{:S(2)}) collective-permute-start(bf16[64,128]{1,0:T(8,128)(2,1)S(1)} %get-tuple-element.26), channel_id=1, source_target_pairs={{4,0},{8,4},{12,8},{16,12},{20,16},{24,20},{28,24},{5,1},{9,5},{13... | collective-permute-start | bytes 49160 | tf_op jit(solution)/shard_map/ppermute | solution.py:23
  13.9 0.7 copy-start.10
  25.5 0.9 copy-start.6
  25.6 0.9 copy-start.11
  25.6 0.8 copy-start.8
  36.4 0.8 copy-start.4
  38.3 90.1 %all-gather.2.cloned.1.call-start = ((), (), s32[]{:S(2)}) async-start(), calls=%async_computation.1 | async-start | bytes 1310720 | tf_op jit(solution)/shard_map/all_gather | solution.py:65
  111.3 0.7 copy-start.12
  128.4 1.7 copy-start.1
  130.2 1.0 copy-start.2
  131.2 21.7 %copy-start.3 = (f32[512,512]{1,0:T(8,128)S(1)}, f32[512,512]{1,0:T(8,128)}, u32[]{:S(2)}) copy-start(f32[512,512]{1,0:T(8,128)} %copy-done.2) | copy-start | bytes 3145732
  153.6 0.7 copy-start.7
  222.1 0.7 copy-start.14
  274.5 1.0 copy-start.5
  275.9 4.8 %copy-start.13 = (s32[2]{0:T(128)S(1)}, s32[2]{0:T(128)}, u32[]{:S(2)}) copy-start(s32[2]{0:T(128)} %param.14) | copy-start | bytes 28
  275.9 7.1 %collective-permute-start.2 = (bf16[256,128]{1,0:T(8,128)(2,1)S(1)}, bf16[256,128]{1,0:T(8,128)(2,1)S(1)}, u32[]{:S(2)}, u32[]{:S(2)}) collective-permute-start(bf16[256,128]{1,0:T(8,128)(2,1)S(1)} %get-tuple-element.23), channel_id=1, source_target_pairs={{0,4},{4,8},{8,12},{12,16},{16,20},{20,24},{24,28},{28,0},{1,5},{5... | collective-permute-start | bytes 196616 | tf_op jit(solution)/shard_map/ppermute | solution.py:20
  277.4 5.7 %collective-permute-start.3 = (bf16[256,128]{1,0:T(8,128)(2,1)S(1)}, bf16[256,128]{1,0:T(8,128)(2,1)S(1)}, u32[]{:S(2)}, u32[]{:S(2)}) collective-permute-start(bf16[256,128]{1,0:T(8,128)(2,1)S(1)} %get-tuple-element.24), channel_id=1, source_target_pairs={{4,0},{8,4},{12,8},{16,12},{20,16},{24,20},{28,24},{0,28},{5,1},{9... | collective-permute-start | bytes 196616 | tf_op jit(solution)/shard_map/ppermute | solution.py:23
Sparse Core Ops, SparseCore 0:
  38.4 72.2 all-reduce.2
  112.3 15.9 all-gather.1
where the time goes:
time: 295 us; the launch traced here: 294 us
  other arithmetic  129 us (44%)
  waiting for transfers between devices  90.3 us (31%)
  between operations  26.6 us (9%)
  local copies, waits for them, and re-layouts  21.7 us (7%)
  starting transfers between devices  11 us (4%)
  matrix products  8.59 us (3%)
  blocking collectives  7.2 us (2%)
    another operation x14, other arithmetic, local(): lower_factor = jnp.linalg.cholesky(gram_matrix)  83.2 us
    psum x1, waiting for transfers between devices, local(): column_block = lax.psum(partial_value, 'rows')  72.4 us
    another operation x3, other arithmetic, local(): jax.scipy.linalg.solve_triangular(lower_factor, unit_columns, lower=True,...  40.8 us
    all_gather x1, waiting for transfers between devices, local(): gram_matrix = lax.all_gather(column_block, 'modes', axis=1, tiled=True)  15.5 us
    another operation x12, local copies, waits for them, and re-layouts  9.85 us
    all_gather x1, blocking collectives, local(): every_mode = lax.all_gather(mass_image, 'modes', axis=1, tiled=True)  7.2 us
    ppermute x2, starting transfers between devices, padded_2(): lax.ppermute(lax.slice_in_dim(block, block.shape[dim] - width, None, axis...  6.39 us
  transfers between devices with their start and end apart: 6, of which 4 were waited for; matrix products, arithmetic and copies ran while one was open for 1% of the time, Pallas kernels for 0%

commit v1 on v0

v1 whole, which is shorter than its diff:
```python
import jax
import jax.numpy as jnp
from jax import lax
from jax.experimental import pallas as pl
from jax.experimental.pallas import tpu as pltpu
from jax.sharding import PartitionSpec as P

BLOCK = 128
BMAX = 4
NOFF = 4
BAND = 64

f32 = jnp.float32
bf16 = jnp.bfloat16
VMEM = pl.BlockSpec(memory_space=pltpu.VMEM)
SMEM = pl.BlockSpec(memory_space=pltpu.SMEM)


def halves(x):
    top = x.astype(bf16)
    rest = x - top.astype(f32)
    middle = rest.astype(bf16)
    return top, middle, (rest - middle.astype(f32)).astype(bf16)


def dot(a, b, dims=((1,), (0,))):
    return lax.dot_general(a, b, (dims, ((), ())), preferred_element_type=f32)


def dot_f32(a, b, dims=((1,), (0,))):
    return lax.dot_general(
        a, b, (dims, ((), ())), precision=lax.Precision.HIGHEST, preferred_element_type=f32
    )


def image_kernel(scale, where_ref, coef_ref, offset_ref, gathered, diag_ref, gain_ref, image, share, scaled, blocks):
    modes = gathered.shape[0]
    rows = diag_ref.shape[0]
    size = BLOCK
    wide = size + 2 * BAND
    row = lax.broadcasted_iota(jnp.int32, (size, wide), 0)
    column = lax.broadcasted_iota(jnp.int32, (size, wide), 1)
    distance = jnp.abs(column - row - BAND)
    band = jnp.zeros((size, wide), f32)
    for j in range(NOFF):
        band = band + jnp.where(distance == offset_ref[j], coef_ref[j], 0.0)
    parts = halves(band)
    for m in range(modes):
        lanes = slice(m * size, (m + 1) * size)
        scaled[0:BAND, lanes] = gathered[m, 0:BAND, :]
        scaled[BAND + rows :, lanes] = gathered[m, BAND + rows :, :]
        slab = gathered[m, BAND : BAND + rows, :].astype(f32)
        scaled[BAND : BAND + rows, lanes] = (gain_ref[...] * slab).astype(bf16)
    for i in range(rows // size):
        rows_in = scaled[i * size : i * size + wide, :]
        neighbour = dot(parts[0], rows_in) + dot(parts[1], rows_in) + dot(parts[2], rows_in)
        here = slice(i * size, (i + 1) * size)
        for m in range(modes):
            lanes = slice(m * size, (m + 1) * size)
            slab = gathered[m, BAND + i * size : BAND + (i + 1) * size, :].astype(f32)
            image[here, lanes] = (
                diag_ref[here, :] * slab + gain_ref[here, :] * neighbour[:, lanes]
            ).astype(bf16)
    for s in range(blocks.shape[0] // size):
        i, j = where_ref[2 * s], where_ref[2 * s + 1]
        image_i = image[:, pl.ds(pl.multiple_of(i * size, size), size)]
        image_j = image[:, pl.ds(pl.multiple_of(j * size, size), size)]
        slab_i = gathered[i, BAND : BAND + rows, :]
        slab_j = gathered[j, BAND : BAND + rows, :]
        over_rows = ((0,), (0,))
        blocks[s * size : (s + 1) * size, :] = (
            dot(image_i, slab_j, over_rows) + dot(slab_i, image_j, over_rows)
        ) * scale
    start = where_ref[2 * (blocks.shape[0] // size)]
    share[...] = blocks[pl.ds(pl.multiple_of(start, 8), share.shape[0]), :]


def lanes_of(x, t):
    return jnp.broadcast_to(x[:, t : t + 1], (8, BLOCK))


def rows_of(x, t):
    return jnp.broadcast_to(x[t : t + 1, :], (8, BLOCK))


def inverse_factor(square):
    panels = BLOCK // 8
    sub = lax.broadcasted_iota(jnp.int32, (8, BLOCK), 0)
    lane = lax.broadcasted_iota(jnp.int32, (8, BLOCK), 1)
    left = [square[8 * p : 8 * p + 8, :] for p in range(panels)]
    right = [(lane == sub + 8 * p).astype(f32) for p in range(panels)]
    result = []
    for p in range(panels):
        has_next = p + 1 < panels
        a, b = left[p], right[p]
        own = [lanes_of(a, 8 * p + t) for t in range(8)]
        if has_next:
            c, d = left[p + 1], right[p + 1]
            below = [lanes_of(c, 8 * p + t) for t in range(8)]
        pivots = jnp.ones((8, BLOCK), f32)
        inverses = jnp.ones((8, BLOCK), f32)
        for t in range(8):
            pivot = rows_of(own[t], t)
            inverse = 1.0 / pivot
            pivots = jnp.where(sub == t, pivot, pivots)
            inverses = jnp.where(sub == t, inverse, inverses)
            a_row, b_row = rows_of(a, t), rows_of(b, t)
            if has_next:
                g = below[t] * inverse
            if t < 7:
                f = jnp.where(sub > t, own[t] * inverse, 0.0)
                for u in range(t + 1, 8):
                    u_row = rows_of(own[u], t)
                    own[u] = own[u] - f * u_row
                    if has_next:
                        below[u] = below[u] - g * u_row
                a = a - f * a_row
                b = b - f * b_row
            if has_next:
                c = c - g * a_row
                d = d - g * b_row
        result.append(b * lax.rsqrt(pivots))
        if has_next:
            left[p + 1], right[p + 1] = c, d
        if p + 2 < panels:
            across = jnp.transpose(a * inverses)
            a_rows = [rows_of(a, t) for t in range(8)]
            b_rows = [rows_of(b, t) for t in range(8)]
            for i in range(p + 2, panels):
                factors = across[8 * i : 8 * i + 8, :]
                for t in range(8):
                    f = lanes_of(factors, t)
                    left[i] = left[i] - f * a_rows[t]
                    right[i] = right[i] - f * b_rows[t]
    return jnp.concatenate(result, axis=0)


def factor_kernel(which_ref, gram, inverse, schur, solved):
    count = inverse.shape[1] // BLOCK
    size = BLOCK
    place = lambda i, j: (i * (i + 1) // 2 + j) * size
    across = ((1,), (1,))
    schur[...] = gram[...]
    solved[...] = jnp.zeros(solved.shape, f32)
    for k in range(count):
        w = inverse_factor(schur[place(k, k) : place(k, k) + size, :])
        here = slice(k * size, (k + 1) * size)
        if k:
            solved[here, : k * size] = -dot_f32(w, solved[here, : k * size])
        solved[here, here] = w
        lower = [None] * count
        for i in range(k + 1, count):
            lower[i] = dot_f32(schur[place(i, k) : place(i, k) + size, :], w, across)
        for i in range(k + 1, count):
            for j in range(k + 1, i + 1):
                at = slice(place(i, j), place(i, j) + size)
                schur[at, :] = schur[at, :] - dot_f32(lower[i], lower[j], across)
        for i in range(k + 1, count):
            there = slice(i * size, (i + 1) * size)
            done = (k + 1) * size
            solved[there, :done] = solved[there, :done] + dot_f32(lower[i], solved[here, :done])
    mine = pl.multiple_of(which_ref[0] * size, size)
    inverse[...] = solved[pl.ds(mine, size), :].astype(bf16)


def project_kernel(blocks_ref, counts_ref, low, own, high, inverse, shapes, out, basis, picked):
    size = BLOCK
    across = ((1,), (1,))
    at = 0
    for part in (low, own, high):
        for i in range(part.shape[0] // size):
            rows = part[i * size : (i + 1) * size, :]
            basis[at] = dot(rows, inverse[...], across).astype(bf16)
            at += 1
    for c in range(out.shape[0]):
        for s in range(BMAX):
            rows = basis[blocks_ref[BMAX * c + s]]
            picked[s * size : (s + 1) * size, :] = jnp.where(s < counts_ref[c], rows, jnp.zeros_like(rows))
        out[c] = dot(picked[...], shapes[c], ((0,), (0,))).astype(bf16)


def sum_over_rows(value):
    count = lax.axis_size("rows")
    if count & (count - 1):
        return lax.psum(value, "rows")
    step = 1
    while step < count:
        value = value + lax.ppermute(value, "rows", [(i, i ^ step) for i in range(count)])
        step *= 2
    return value


def local(
    mode_slab,
    mass_diag,
    mass_gain,
    band_coef,
    band_offsets,
    boundary_blocks,
    boundary_counts,
    boundary_modes,
):
    rows_dev, mode_cols = mode_slab.shape
    modes = lax.axis_size("modes")
    row_devices = lax.axis_size("rows")
    order = mode_cols * modes
    count = order // BLOCK
    per_dev = rows_dev // BLOCK
    rim_rows = per_dev // 2 * BLOCK
    total_rows = rows_dev * row_devices
    up = [(i, i + 1) for i in range(row_devices - 1)]
    down = [(i + 1, i) for i in range(row_devices - 1)]

    def scaled_edge(rows):
        return (mass_gain[rows, None] * mode_slab[rows, :].astype(f32)).astype(bf16)

    low = lax.ppermute(scaled_edge(slice(rows_dev - BAND, rows_dev)), "rows", up)
    high = lax.ppermute(scaled_edge(slice(0, BAND)), "rows", down)
    gathered = lax.all_gather(jnp.concatenate([low, mode_slab, high], axis=0), "modes", axis=0)

    lower = [(i, j) for i in range(count) for j in range(i + 1)]
    share_rows = len(lower) * BLOCK // modes
    taken = -(-(share_rows + BLOCK // 2) // BLOCK)
    table = []
    for m in range(modes):
        first = m * share_rows // BLOCK
        first = min(first, len(lower) - taken)
        entries = [v for s in range(taken) for v in lower[first + s]]
        table.append(entries + [m * share_rows - first * BLOCK])
    mode_index = lax.axis_index("modes")
    where = jnp.asarray(table, jnp.int32)[mode_index]

    image, share = pl.pallas_call(
        lambda *refs: image_kernel(0.5 / total_rows, *refs),
        out_shape=(
            jax.ShapeDtypeStruct((rows_dev, order), bf16),
            jax.ShapeDtypeStruct((share_rows, BLOCK), f32),
        ),
        in_specs=[SMEM, SMEM, SMEM, VMEM, VMEM, VMEM],
        out_specs=(VMEM, VMEM),
        scratch_shapes=[
            pltpu.VMEM((rows_dev + 2 * BAND, order), bf16),
            pltpu.VMEM((taken * BLOCK, BLOCK), f32),
        ],
        name="image",
    )(where, band_coef, band_offsets, gathered, mass_diag[:, None], mass_gain[:, None])

    share = sum_over_rows(share)
    image, share = lax.optimization_barrier((image, share))
    around = [(i, (i + 1) % row_devices) for i in range(row_devices)]
    back = [(target, source) for source, target in around]
    rim_low = lax.ppermute(image[rows_dev - rim_rows :, :], "rows", around)
    rim_high = lax.ppermute(image[:rim_rows, :], "rows", back)
    gram = lax.all_gather(share, "modes", axis=0).reshape(len(lower) * BLOCK, BLOCK)

    inverse = pl.pallas_call(
        factor_kernel,
        out_shape=jax.ShapeDtypeStruct((BLOCK, order), bf16),
        in_specs=[SMEM, VMEM],
        out_specs=VMEM,
        scratch_shapes=[
            pltpu.VMEM((len(lower) * BLOCK, BLOCK), f32),
            pltpu.VMEM((order, order), f32),
        ],
        name="factor",
    )(mode_index.reshape(1).astype(jnp.int32), gram)

    total_blocks = per_dev * row_devices
    window_start = lax.axis_index("rows") * per_dev - per_dev // 2
    local_blocks = jnp.mod(boundary_blocks - window_start, total_blocks).reshape(-1)
    owned, _, width = boundary_modes.shape
    window = per_dev + 2 * (per_dev // 2)
    return pl.pallas_call(
        project_kernel,
        out_shape=jax.ShapeDtypeStruct((owned, mode_cols, width), bf16),
        in_specs=[SMEM, SMEM, VMEM, VMEM, VMEM, VMEM, VMEM],
        out_specs=VMEM,
        scratch_shapes=[
            pltpu.VMEM((window, BLOCK, BLOCK), bf16),
            pltpu.VMEM((BMAX * BLOCK, BLOCK), bf16),
        ],
        name="project",
    )(local_blocks, boundary_counts, rim_low, image, rim_high, inverse, boundary_modes)


def solution(mesh):
    in_specs = (
        P("rows", "modes"),
        P("rows"),
        P("rows"),
        P(),
        P(),
        P("rows", None),
        P("rows"),
        P("rows", None, None),
    )
    out_specs = P("rows", "modes", None)
    return jax.shard_map(local, mesh=mesh, in_specs=in_specs, out_specs=out_specs, check_vma=False)
```

time: 295 us -> 87 us (0.29)
  other arithmetic: 129 us -> 1.81 us
  waiting for transfers between devices: 90.3 us -> 17.6 us
  Pallas kernels: 0 us -> 29.5 us
  between operations: 26.6 us -> 0.1 us
  local copies, waits for them, and re-layouts: 21.7 us -> 5.76 us
  blocking collectives: 7.2 us -> 15.9 us
  matrix products: 8.59 us -> 0 us
  starting transfers between devices: 11 us -> 15.9 us
    another operation x17 -> x0, other arithmetic: 124 us -> none  [the longest x14 83.2 us: local(): lower_factor = jnp.linalg.cholesky(gram_matrix)]
    psum x1 -> x0, waiting for transfers between devices: 72.4 us -> none  [local(): column_block = lax.psum(partial_value, 'rows')]
    pallas_call x0 -> x3, Pallas kernels: none -> 29.5 us  [the longest x1 23.1 us: local(): pl.pallas_call(factor_kernel, out_shape=jax.ShapeDtypeStruct((BLOCK, orde...]
    all_gather x1 -> x0, waiting for transfers between devices: 15.5 us -> none  [local(): gram_matrix = lax.all_gather(column_block, 'modes', axis=1, tiled=True)]
    ppermute x4 -> x7, waiting for transfers between devices: 2.34 us -> 17.6 us  [the longest x3 16.2 us: sum_over_rows(): lax.ppermute(value, 'rows', [(i, i ^ step) for i in range(count)])]
    another operation x17 -> x0, local copies, waits for them, and re-layouts: 10.6 us -> none
    all_gather x1 -> x2, blocking collectives: 7.2 us -> 15.9 us  [the longest x1 8.33 us: local(): lax.all_gather(jnp.concatenate([low, mode_slab, high], axis=0), 'modes',...]
    another operation x13 -> x0, matrix products: 6.26 us -> none  [the longest x6 3.61 us: local(): lower_factor = jnp.linalg.cholesky(gram_matrix)]
  transfers between devices with their start and end apart: 6 -> 7, of which waited for: 4 -> 4; matrix products, arithmetic and copies ran while one was open for 1% -> 4% of each run, Pallas kernels for 0% -> 27%
where the time goes in v1:
time: 87 us; the launch traced here: 86.6 us
  Pallas kernels  29.5 us (34%)
  waiting for transfers between devices  17.6 us (20%)
  starting transfers between devices  15.9 us (18%)
  blocking collectives  15.9 us (18%)
  local copies, waits for them, and re-layouts  5.76 us (7%)
  other arithmetic  1.81 us (2%)
    pallas_call x1, Pallas kernels, local(): pl.pallas_call(factor_kernel, out_shape=jax.ShapeDtypeStruct((BLOCK, orde...  23.1 us
    ppermute x3, waiting for transfers between devices, sum_over_rows(): lax.ppermute(value, 'rows', [(i, i ^ step) for i in range(count)])  16.2 us
    all_gather x1, blocking collectives, local(): lax.all_gather(jnp.concatenate([low, mode_slab, high], axis=0), 'modes',...  8.33 us
    all_gather x1, blocking collectives, local(): lax.all_gather(share, 'modes', axis=0).reshape(len(lower) * BLOCK, BLOCK)  7.55 us
    ppermute x3, starting transfers between devices, sum_over_rows(): lax.ppermute(value, 'rows', [(i, i ^ step) for i in range(count)])  6.52 us
    ppermute x1, starting transfers between devices, local(): lax.ppermute(scaled_edge(slice(rows_dev - BAND, rows_dev)), 'rows', up)  4.87 us
    pallas_call x1, Pallas kernels, local(): pl.pallas_call(lambda *refs: image_kernel(0.5 / total_rows, *refs), out_s...  3.27 us
    ppermute x1, starting transfers between devices, local(): rim_high = lax.ppermute(image[:rim_rows, :], 'rows', back)  3.2 us
  transfers between devices with their start and end apart: 7, of which 4 were waited for; matrix products, arithmetic and copies ran while one was open for 4% of the time, Pallas kernels for 27%

profile of v1, /device:TPU:0, one launch (start us, length us, event | category | flops | bytes accessed | tf_op | source)
XLA Modules:
  0.0 86.6 jit_solution(17637180137008517363)
XLA Ops:
  0.0 0.8 fusion.2
  0.8 0.8 multiply_convert_fusion.1
  1.6 4.9 %collective-permute-start = (bf16[64,128]{1,0:T(8,128)(2,1)S(1)}, bf16[64,128]{1,0:T(8,128)(2,1)S(1)}, u32[]{:S(2)}, u32[]{:S(2)}) collective-permute-start(bf16[64,128]{1,0:T(8,128)(2,1)S(1)} %get-tuple-element.15), channel_id=1, source_target_pairs={{0,4},{4,8},{8,12},{12,16},{16,20},{20,24},{24,28},{1,5},{5,9},{9,... | collective-permute-start | bytes 49160 | tf_op jit(solution)/shard_map/ppermute | solution.py:217
  6.5 1.3 %collective-permute-start.1 = (bf16[64,128]{1,0:T(8,128)(2,1)S(1)}, bf16[64,128]{1,0:T(8,128)(2,1)S(1)}, u32[]{:S(2)}, u32[]{:S(2)}) collective-permute-start(bf16[64,128]{1,0:T(8,128)(2,1)S(1)} %get-tuple-element.16), channel_id=1, source_target_pairs={{4,0},{8,4},{12,8},{16,12},{20,16},{24,20},{28,24},{5,1},{9,5},{13... | collective-permute-start | bytes 49160 | tf_op jit(solution)/shard_map/ppermute | solution.py:218
  7.8 0.0 copy-start.5
  7.8 1.2 %dynamic-slice_bitcast_fusion.refs_0_ = s32[7]{0:T(128)} fusion(s32[4,7]{1,0:T(4,128)} %constant.32.clone, s32[]{:T(128)S(6)} %select_n.11), kind=kLoop, calls=%fused_computation.7 | loop fusion | bytes 60 | tf_op jit(solution)/shard_map/squeeze | solution.py:231
  9.0 0.0 copy-done.5
  9.0 0.0 copy-start.4
  9.0 0.9 copy.10.refs_4_
  9.9 0.0 copy-done.4
  9.9 0.0 copy-start.3
  9.9 0.9 copy.11.refs_5_
  10.7 0.0 collective-permute-done
  10.7 1.4 %collective-permute-done.1 = bf16[64,128]{1,0:T(8,128)(2,1)S(1)} collective-permute-done((bf16[64,128]{1,0:T(8,128)(2,1)S(1)}, bf16[64,128]{1,0:T(8,128)(2,1)S(1)}, u32[]{:S(2)}, u32[]{:S(2)}) %collective-permute-start.1) | collective-permute-done | bytes 16416 | tf_op jit(solution)/shard_map/ppermute | solution.py:218
  12.2 0.0 copy-done.3
  12.2 8.3 %all-gather = bf16[2560,128]{1,0:T(8,128)(2,1)} all-gather(bf16[640,128]{1,0:T(8,128)(2,1)S(1)} %pad_maximum_fusion), channel_id=2, replica_groups=mesh['rows'=8,'modes'=4] {'modes'}, dimensions={0}, use_global_device_ids=true | all-gather | bytes 819200 | tf_op jit(solution)/shard_map/all_gather | solution.py:219
  20.5 3.3 %image.1 = (bf16[512,512]{1,0:T(8,128)(2,1)}, f32[320,128]{1,0:T(8,128)}) custom-call(s32[7]{0:T(128)} %dynamic-slice_bitcast_fusion.refs_0_, f32[4]{0:T(128)} %refs_1_.1, s32[4]{0:T(128)} %refs_2_.1, bf16[4,640,128]{2,1,0:T(8,128)(2,1)} %bitcast.6, f32[512,1]{1,0:T(8,128)} %copy.10.refs_4_, f32[512,1]{1,0:T(8,128)} %copy.11.refs_5_), custom_call_target="tpu_custom_call" | custom-call | tf_op jit(solution)/shard_map/image/pallas_call | solution.py:233
  23.8 2.4 %collective-permute-start.2 = (f32[320,128]{1,0:T(8,128)}, f32[320,128]{1,0:T(8,128)S(1)}, u32[]{:S(2)}, u32[]{:S(2)}) collective-permute-start(f32[320,128]{1,0:T(8,128)} %get-tuple-element.10), channel_id=1, source_target_pairs={{0,4},{4,0},{8,12},{12,8},{16,20},{20,16},{24,28},{28,24},{1,5},{5... | collective-permute-start | bytes 491528 | tf_op jit(solution)/shard_map/ppermute | solution.py:188
  26.2 4.9 %collective-permute-done.2 = f32[320,128]{1,0:T(8,128)S(1)} collective-permute-done((f32[320,128]{1,0:T(8,128)}, f32[320,128]{1,0:T(8,128)S(1)}, u32[]{:S(2)}, u32[]{:S(2)}) %collective-permute-start.2) | collective-permute-done | bytes 163872 | tf_op jit(solution)/shard_map/ppermute | solution.py:188
  31.1 0.9 %add.21 = f32[320,128]{1,0:T(8,128)S(1)} add(f32[320,128]{1,0:T(8,128)} %get-tuple-element.10, f32[320,128]{1,0:T(8,128)S(1)} %collective-permute-done.2) | non-fusion elementwise | flops 40960 | bytes 491520 | tf_op jit(solution)/shard_map/add | solution.py:188
  32.1 0.0 copy-start
  32.1 1.6 %collective-permute-start.3 = (f32[320,128]{1,0:T(8,128)S(1)}, f32[320,128]{1,0:T(8,128)S(1)}, u32[]{:S(2)}, u32[]{:S(2)}) collective-permute-start(f32[320,128]{1,0:T(8,128)S(1)} %add.21), channel_id=1, source_target_pairs={{0,8},{4,12},{8,0},{12,4},{16,24},{20,28},{24,16},{28,20},{1,9},{5... | collective-permute-start | bytes 491528 | tf_op jit(solution)/shard_map/ppermute | solution.py:188
  33.7 4.3 %collective-permute-done.3 = f32[320,128]{1,0:T(8,128)S(1)} collective-permute-done((f32[320,128]{1,0:T(8,128)S(1)}, f32[320,128]{1,0:T(8,128)S(1)}, u32[]{:S(2)}, u32[]{:S(2)}) %collective-permute-start.3) | collective-permute-done | bytes 163872 | tf_op jit(solution)/shard_map/ppermute | solution.py:188
  38.0 2.5 %collective-permute-start.4 = (f32[320,128]{1,0:T(8,128)S(1)}, f32[320,128]{1,0:T(8,128)S(1)}, u32[]{:S(2)}, u32[]{:S(2)}) collective-permute-start(f32[320,128]{1,0:T(8,128)S(1)} %add.22), channel_id=1, source_target_pairs={{0,16},{4,20},{8,24},{12,28},{16,0},{20,4},{24,8},{28,12},{1,17},{... | collective-permute-start | bytes 491528 | tf_op jit(solution)/shard_map/ppermute | solution.py:188
  40.5 7.0 %collective-permute-done.4 = f32[320,128]{1,0:T(8,128)S(1)} collective-permute-done((f32[320,128]{1,0:T(8,128)S(1)}, f32[320,128]{1,0:T(8,128)S(1)}, u32[]{:S(2)}, u32[]{:S(2)}) %collective-permute-start.4) | collective-permute-done | bytes 163872 | tf_op jit(solution)/shard_map/ppermute | solution.py:188
  47.5 0.0 copy-done
  47.6 0.0 copy-start.6
  47.6 3.2 %collective-permute-start.6 = (bf16[256,512]{1,0:T(8,128)(2,1)S(1)}, bf16[256,512]{1,0:T(8,128)(2,1)S(1)}, u32[]{:S(2)}, u32[]{:S(2)}) collective-permute-start(bf16[256,512]{1,0:T(8,128)(2,1)S(1)} %get-tuple-element.13), channel_id=1, source_target_pairs={{4,0},{8,4},{12,8},{16,12},{20,16},{24,20},{28,24},{0,28},{5,1},{9... | collective-permute-start | bytes 786440 | tf_op jit(solution)/shard_map/ppermute | solution.py:253
  50.8 0.0 collective-permute-start.5
  50.8 0.0 copy-done.6
  50.8 0.6 reshape.11.blocks_ref
  51.4 7.6 %all-gather.1.gram = f32[1280,128]{1,0:T(8,128)} all-gather(f32[320,128]{1,0:T(8,128)S(1)} %add.23), channel_id=3, replica_groups=mesh['rows'=8,'modes'=4] {'modes'}, dimensions={0}, use_global_device_ids=true | all-gather | bytes 819200 | tf_op jit(solution)/shard_map/all_gather | solution.py:254
  59.0 23.1 %factor.1.inverse = bf16[128,512]{1,0:T(8,128)(2,1)} custom-call(s32[1]{0:T(128)} %bitcast.4.which_ref, f32[1280,128]{1,0:T(8,128)} %all-gather.1.gram), custom_call_target="tpu_custom_call" | custom-call | tf_op jit(solution)/shard_map/factor/pallas_call | solution.py:256
  82.1 0.0 collective-permute-done.6.high
  82.1 0.0 copy-start.1
  82.1 0.0 collective-permute-done.5.low
  82.1 0.7 copy-done.1
  82.8 0.0 copy-start.2
  82.8 0.7 copy-done.2
  83.5 3.1 %project.1 = bf16[2,128,512]{2,1,0:T(8,128)(2,1)} custom-call(s32[8]{0:T(128)} %reshape.11.blocks_ref, s32[2]{0:T(128)} %counts_ref.1, bf16[256,512]{1,0:T(8,128)(2,1)} %copy-done.2, bf16[512,512]{1,0:T(8,128)(2,1)} %get-tuple-element.11.own, bf16[256,512]{1,0:T(8,128)(2,1)} %copy-done.1, bf16[128,512]{1,0:T(8,128)(2,1)} %factor.1.inverse, ...), custom_call_target="tpu_custom_call" | custom-call | tf_op jit(solution)/shard_map/project/pallas_call | solution.py:273
  (5 shorter events, 0.1 us)
Async XLA Ops:
  1.6 9.1 %collective-permute-start = (bf16[64,128]{1,0:T(8,128)(2,1)S(1)}, bf16[64,128]{1,0:T(8,128)(2,1)S(1)}, u32[]{:S(2)}, u32[]{:S(2)}) collective-permute-start(bf16[64,128]{1,0:T(8,128)(2,1)S(1)} %get-tuple-element.15), channel_id=1, source_target_pairs={{0,4},{4,8},{8,12},{12,16},{16,20},{20,24},{24,28},{1,5},{5,9},{9,... | collective-permute-start | bytes 49160 | tf_op jit(solution)/shard_map/ppermute | solution.py:217
  6.5 5.6 %collective-permute-start.1 = (bf16[64,128]{1,0:T(8,128)(2,1)S(1)}, bf16[64,128]{1,0:T(8,128)(2,1)S(1)}, u32[]{:S(2)}, u32[]{:S(2)}) collective-permute-start(bf16[64,128]{1,0:T(8,128)(2,1)S(1)} %get-tuple-element.16), channel_id=1, source_target_pairs={{4,0},{8,4},{12,8},{16,12},{20,16},{24,20},{28,24},{5,1},{9,5},{13... | collective-permute-start | bytes 49160 | tf_op jit(solution)/shard_map/ppermute | solution.py:218
  7.8 1.2 %copy-start.5 = (f32[512]{0:T(512)S(1)}, f32[512]{0:T(512)}, u32[]{:S(2)}) copy-start(f32[512]{0:T(512)} %param.10) | copy-start | bytes 6148
  9.0 0.9 copy-start.4
  9.9 2.3 %copy-start.3 = (bf16[512,128]{1,0:T(8,128)(2,1)S(1)}, bf16[512,128]{1,0:T(8,128)(2,1)}, u32[]{:S(2)}) copy-start(bf16[512,128]{1,0:T(8,128)(2,1)} %param.9) | copy-start | bytes 393220
  23.8 7.3 %collective-permute-start.2 = (f32[320,128]{1,0:T(8,128)}, f32[320,128]{1,0:T(8,128)S(1)}, u32[]{:S(2)}, u32[]{:S(2)}) collective-permute-start(f32[320,128]{1,0:T(8,128)} %get-tuple-element.10), channel_id=1, source_target_pairs={{0,4},{4,0},{8,12},{12,8},{16,20},{20,16},{24,28},{28,24},{1,5},{5... | collective-permute-start | bytes 491528 | tf_op jit(solution)/shard_map/ppermute | solution.py:188
  32.1 15.5 %copy-start = (bf16[512,512]{1,0:T(8,128)(2,1)S(1)}, bf16[512,512]{1,0:T(8,128)(2,1)}, u32[]{:S(2)}) copy-start(bf16[512,512]{1,0:T(8,128)(2,1)} %get-tuple-element.11.own) | copy-start | bytes 1572868
  32.1 5.9 %collective-permute-start.3 = (f32[320,128]{1,0:T(8,128)S(1)}, f32[320,128]{1,0:T(8,128)S(1)}, u32[]{:S(2)}, u32[]{:S(2)}) collective-permute-start(f32[320,128]{1,0:T(8,128)S(1)} %add.21), channel_id=1, source_target_pairs={{0,8},{4,12},{8,0},{12,4},{16,24},{20,28},{24,16},{28,20},{1,9},{5... | collective-permute-start | bytes 491528 | tf_op jit(solution)/shard_map/ppermute | solution.py:188
  38.0 9.5 %collective-permute-start.4 = (f32[320,128]{1,0:T(8,128)S(1)}, f32[320,128]{1,0:T(8,128)S(1)}, u32[]{:S(2)}, u32[]{:S(2)}) collective-permute-start(f32[320,128]{1,0:T(8,128)S(1)} %add.22), channel_id=1, source_target_pairs={{0,16},{4,20},{8,24},{12,28},{16,0},{20,4},{24,8},{28,12},{1,17},{... | collective-permute-start | bytes 491528 | tf_op jit(solution)/shard_map/ppermute | solution.py:188
  47.6 3.2 %copy-start.6 = (s32[2,4]{1,0:T(2,128)S(1)}, s32[2,4]{1,0:T(2,128)}, u32[]{:S(2)}) copy-start(s32[2,4]{1,0:T(2,128)} %param.14) | copy-start | bytes 100
  47.6 34.5 %collective-permute-start.6 = (bf16[256,512]{1,0:T(8,128)(2,1)S(1)}, bf16[256,512]{1,0:T(8,128)(2,1)S(1)}, u32[]{:S(2)}, u32[]{:S(2)}) collective-permute-start(bf16[256,512]{1,0:T(8,128)(2,1)S(1)} %get-tuple-element.13), channel_id=1, source_target_pairs={{4,0},{8,4},{12,8},{16,12},{20,16},{24,20},{28,24},{0,28},{5,1},{9... | collective-permute-start | bytes 786440 | tf_op jit(solution)/shard_map/ppermute | solution.py:253
  50.8 31.3 %collective-permute-start.5 = (bf16[256,512]{1,0:T(8,128)(2,1)S(1)}, bf16[256,512]{1,0:T(8,128)(2,1)S(1)}, u32[]{:S(2)}, u32[]{:S(2)}) collective-permute-start(bf16[256,512]{1,0:T(8,128)(2,1)S(1)} %get-tuple-element.14), channel_id=1, source_target_pairs={{0,4},{4,8},{8,12},{12,16},{16,20},{20,24},{24,28},{28,0},{1,5},{5... | collective-permute-start | bytes 786440 | tf_op jit(solution)/shard_map/ppermute | solution.py:252
  82.1 0.7 copy-start.1
  82.8 0.7 copy-start.2

commit v2 on v1

--- a/solution.py
+++ b/solution.py
@@ -13,10 +13,15 @@
 f32 = jnp.float32
 bf16 = jnp.bfloat16
 VMEM = pl.BlockSpec(memory_space=pltpu.VMEM)
+
+
+def near(x):
+    return pltpu.with_memory_space_constraint(x, pltpu.VMEM)
+
 SMEM = pl.BlockSpec(memory_space=pltpu.SMEM)
 
 
-def halves(x):
+def bf16_parts(x):
     top = x.astype(bf16)
     rest = x - top.astype(f32)
     middle = rest.astype(bf16)
@@ -33,9 +38,10 @@
     )
 
 
-def image_kernel(scale, where_ref, coef_ref, offset_ref, gathered, diag_ref, gain_ref, image, share, scaled, blocks):
+def image_kernel(scale, where_ref, coef_ref, offset_ref, gathered, diag_ref, gain_ref, first, second, share, scaled, blocks):
     modes = gathered.shape[0]
     rows = diag_ref.shape[0]
+    half = first.shape[0]
     size = BLOCK
     wide = size + 2 * BAND
     row = lax.broadcasted_iota(jnp.int32, (size, wide), 0)
@@ -44,7 +50,7 @@
     band = jnp.zeros((size, wide), f32)
     for j in range(NOFF):
         band = band + jnp.where(distance == offset_ref[j], coef_ref[j], 0.0)
-    parts = halves(band)
+    parts = bf16_parts(band)
     for m in range(modes):
         lanes = slice(m * size, (m + 1) * size)
         scaled[0:BAND, lanes] = gathered[m, 0:BAND, :]
@@ -58,19 +64,21 @@
         for m in range(modes):
             lanes = slice(m * size, (m + 1) * size)
             slab = gathered[m, BAND + i * size : BAND + (i + 1) * size, :].astype(f32)
-            image[here, lanes] = (
+            image, at = (first, i * size) if i * size < half else (second, i * size - half)
+            image[at : at + size, lanes] = (
                 diag_ref[here, :] * slab + gain_ref[here, :] * neighbour[:, lanes]
             ).astype(bf16)
     for s in range(blocks.shape[0] // size):
         i, j = where_ref[2 * s], where_ref[2 * s + 1]
-        image_i = image[:, pl.ds(pl.multiple_of(i * size, size), size)]
-        image_j = image[:, pl.ds(pl.multiple_of(j * size, size), size)]
-        slab_i = gathered[i, BAND : BAND + rows, :]
-        slab_j = gathered[j, BAND : BAND + rows, :]
-        over_rows = ((0,), (0,))
-        blocks[s * size : (s + 1) * size, :] = (
-            dot(image_i, slab_j, over_rows) + dot(slab_i, image_j, over_rows)
-        ) * scale
+        total = jnp.zeros((size, size), f32)
+        for image, at in ((first, BAND), (second, BAND + half)):
+            image_i = image[:, pl.ds(pl.multiple_of(i * size, size), size)]
+            image_j = image[:, pl.ds(pl.multiple_of(j * size, size), size)]
+            slab_i = gathered[i, at : at + half, :]
+            slab_j = gathered[j, at : at + half, :]
+            over_rows = ((0,), (0,))
+            total = total + dot(image_i, slab_j, over_rows) + dot(slab_i, image_j, over_rows)
+        blocks[s * size : (s + 1) * size, :] = total * scale
     start = where_ref[2 * (blocks.shape[0] // size)]
     share[...] = blocks[pl.ds(pl.multiple_of(start, 8), share.shape[0]), :]
 
@@ -83,20 +91,22 @@
     return jnp.broadcast_to(x[t : t + 1, :], (8, BLOCK))
 
 
-def inverse_factor(square):
+def inverse_factor(square, depth=3):
     panels = BLOCK // 8
     sub = lax.broadcasted_iota(jnp.int32, (8, BLOCK), 0)
     lane = lax.broadcasted_iota(jnp.int32, (8, BLOCK), 1)
     left = [square[8 * p : 8 * p + 8, :] for p in range(panels)]
     right = [(lane == sub + 8 * p).astype(f32) for p in range(panels)]
+    own = [lanes_of(left[0], t) for t in range(8)]
     result = []
     for p in range(panels):
-        has_next = p + 1 < panels
+        below = range(p + 1, min(panels, p + 1 + depth))
+        columns = 16 if p + 1 < panels else 8
         a, b = left[p], right[p]
-        own = [lanes_of(a, 8 * p + t) for t in range(8)]
-        if has_next:
-            c, d = left[p + 1], right[p + 1]
-            below = [lanes_of(c, 8 * p + t) for t in range(8)]
+        own = own + [lanes_of(a, 8 * p + t) for t in range(8, columns)]
+        under = {
+            i: [lanes_of(left[i], 8 * p + t) for t in range(columns if i == p + 1 else 8)] for i in below
+        }
         pivots = jnp.ones((8, BLOCK), f32)
         inverses = jnp.ones((8, BLOCK), f32)
         for t in range(8):
@@ -104,34 +114,38 @@
             inverse = 1.0 / pivot
             pivots = jnp.where(sub == t, pivot, pivots)
             inverses = jnp.where(sub == t, inverse, inverses)
+            f = jnp.where(sub > t, own[t], 0.0) * inverse
+            g = {i: under[i][t] * inverse for i in below}
+            for u in range(t + 1, columns):
+                u_row = rows_of(own[u], t)
+                if t < 7:
+                    own[u] = own[u] - f * u_row
+                for i in below:
+                    if u < len(under[i]):
+                        under[i][u] = under[i][u] - g[i] * u_row
             a_row, b_row = rows_of(a, t), rows_of(b, t)
-            if has_next:
-                g = below[t] * inverse
             if t < 7:
-                f = jnp.where(sub > t, own[t] * inverse, 0.0)
-                for u in range(t + 1, 8):
-                    u_row = rows_of(own[u], t)
-                    own[u] = own[u] - f * u_row
-                    if has_next:
-                        below[u] = below[u] - g * u_row
                 a = a - f * a_row
                 b = b - f * b_row
-            if has_next:
-                c = c - g * a_row
-                d = d - g * b_row
+            for i in below:
+                left[i] = left[i] - g[i] * a_row
+                right[i] = right[i] - g[i] * b_row
         result.append(b * lax.rsqrt(pivots))
-        if has_next:
-            left[p + 1], right[p + 1] = c, d
-        if p + 2 < panels:
-            across = jnp.transpose(a * inverses)
-            a_rows = [rows_of(a, t) for t in range(8)]
-            b_rows = [rows_of(b, t) for t in range(8)]
-            for i in range(p + 2, panels):
-                factors = across[8 * i : 8 * i + 8, :]
-                for t in range(8):
-                    f = lanes_of(factors, t)
-                    left[i] = left[i] - f * a_rows[t]
-                    right[i] = right[i] - f * b_rows[t]
+        if p + 1 < panels:
+            own = under[p + 1][8:]
+        rest = p + 1 + depth
+        if rest < panels:
+            a0, a1, a2 = bf16_parts(a * inverses)
+            b0, b1, b2 = bf16_parts(jnp.concatenate([a, b], axis=1))
+            update = dot(
+                jnp.concatenate([a0, a0, a1, a0, a2, a1], axis=0)[:, 8 * rest :],
+                jnp.concatenate([b0, b1, b0, b2, b0, b1], axis=0),
+                ((0,), (0,)),
+            )
+            for i in range(rest, panels):
+                at = slice(8 * (i - rest), 8 * (i - rest) + 8)
+                left[i] = left[i] - update[at, :BLOCK]
+                right[i] = right[i] - update[at, BLOCK:]
     return jnp.concatenate(result, axis=0)
 
 
@@ -163,11 +177,11 @@
     inverse[...] = solved[pl.ds(mine, size), :].astype(bf16)
 
 
-def project_kernel(blocks_ref, counts_ref, low, own, high, inverse, shapes, out, basis, picked):
+def project_kernel(blocks_ref, counts_ref, low, first, second, high, inverse, shapes, out, basis, picked):
     size = BLOCK
     across = ((1,), (1,))
     at = 0
-    for part in (low, own, high):
+    for part in (low, first, second, high):
         for i in range(part.shape[0] // size):
             rows = part[i * size : (i + 1) * size, :]
             basis[at] = dot(rows, inverse[...], across).astype(bf16)
@@ -208,6 +222,7 @@
     per_dev = rows_dev // BLOCK
     rim_rows = per_dev // 2 * BLOCK
     total_rows = rows_dev * row_devices
+    assert rows_dev == 2 * rim_rows
     up = [(i, i + 1) for i in range(row_devices - 1)]
     down = [(i + 1, i) for i in range(row_devices - 1)]
 
@@ -230,32 +245,33 @@
     mode_index = lax.axis_index("modes")
     where = jnp.asarray(table, jnp.int32)[mode_index]
 
-    image, share = pl.pallas_call(
+    first, second, share = pl.pallas_call(
         lambda *refs: image_kernel(0.5 / total_rows, *refs),
         out_shape=(
-            jax.ShapeDtypeStruct((rows_dev, order), bf16),
-            jax.ShapeDtypeStruct((share_rows, BLOCK), f32),
+            pltpu.VMEM((rim_rows, order), bf16),
+            pltpu.VMEM((rim_rows, order), bf16),
+            pltpu.VMEM((share_rows, BLOCK), f32),
         ),
         in_specs=[SMEM, SMEM, SMEM, VMEM, VMEM, VMEM],
-        out_specs=(VMEM, VMEM),
+        out_specs=(VMEM, VMEM, VMEM),
         scratch_shapes=[
             pltpu.VMEM((rows_dev + 2 * BAND, order), bf16),
             pltpu.VMEM((taken * BLOCK, BLOCK), f32),
         ],
         name="image",
-    )(where, band_coef, band_offsets, gathered, mass_diag[:, None], mass_gain[:, None])
+    )(where, band_coef, band_offsets, near(gathered), near(mass_diag[:, None]), near(mass_gain[:, None]))
 
     share = sum_over_rows(share)
-    image, share = lax.optimization_barrier((image, share))
+    first, second, share = lax.optimization_barrier((first, second, share))
     around = [(i, (i + 1) % row_devices) for i in range(row_devices)]
     back = [(target, source) for source, target in around]
-    rim_low = lax.ppermute(image[rows_dev - rim_rows :, :], "rows", around)
-    rim_high = lax.ppermute(image[:rim_rows, :], "rows", back)
+    rim_low = lax.ppermute(second, "rows", around)
+    rim_high = lax.ppermute(first, "rows", back)
     gram = lax.all_gather(share, "modes", axis=0).reshape(len(lower) * BLOCK, BLOCK)
 
     inverse = pl.pallas_call(
         factor_kernel,
-        out_shape=jax.ShapeDtypeStruct((BLOCK, order), bf16),
+        out_shape=pltpu.VMEM((BLOCK, order), bf16),
         in_specs=[SMEM, VMEM],
         out_specs=VMEM,
         scratch_shapes=[
@@ -263,7 +279,7 @@
             pltpu.VMEM((order, order), f32),
         ],
         name="factor",
-    )(mode_index.reshape(1).astype(jnp.int32), gram)
+    )(mode_index.reshape(1).astype(jnp.int32), near(gram))
 
     total_blocks = per_dev * row_devices
     window_start = lax.axis_index("rows") * per_dev - per_dev // 2
@@ -273,14 +289,14 @@
     return pl.pallas_call(
         project_kernel,
         out_shape=jax.ShapeDtypeStruct((owned, mode_cols, width), bf16),
-        in_specs=[SMEM, SMEM, VMEM, VMEM, VMEM, VMEM, VMEM],
+        in_specs=[SMEM, SMEM, VMEM, VMEM, VMEM, VMEM, VMEM, VMEM],
         out_specs=VMEM,
         scratch_shapes=[
             pltpu.VMEM((window, BLOCK, BLOCK), bf16),
             pltpu.VMEM((BMAX * BLOCK, BLOCK), bf16),
         ],
         name="project",
-    )(local_blocks, boundary_counts, rim_low, image, rim_high, inverse, boundary_modes)
+    )(local_blocks, boundary_counts, near(rim_low), near(first), near(second), near(rim_high), near(inverse), near(boundary_modes))
 
 
 def solution(mesh):

time: 87 us -> 74.3 us (0.85)
  Pallas kernels: 29.5 us -> 18.5 us
  local copies, waits for them, and re-layouts: 5.76 us -> 3.53 us
  starting transfers between devices: 15.9 us -> 17.7 us
  other arithmetic: 1.81 us -> 0.89 us
  blocking collectives: 15.9 us -> 15 us
    pallas_call x1, Pallas kernels: 23.1 us -> 14.3 us  [local(): pl.pallas_call(factor_kernel, out_shape=pltpu.VMEM((BLOCK, order), bf16),...]
    ppermute x2, starting transfers between devices: 3.2 us -> 4.78 us  [the longest x1 3.46 us: local(): rim_high = lax.ppermute(first, 'rows', back)]
    pallas_call x1, Pallas kernels: 3.27 us -> 2.02 us  [local(): pl.pallas_call(lambda *refs: image_kernel(0.5 / total_rows, *refs), out_s...]
    pallas_call x1, Pallas kernels: 3.1 us -> 2.18 us  [local(): pl.pallas_call(project_kernel, out_shape=jax.ShapeDtypeStruct((owned, mod...]
    add x3, other arithmetic: 0.98 us -> 0.06 us  [sum_over_rows(): value + lax.ppermute(value, 'rows', [(i, i ^ step) for i in range(count)])]
  transfers between devices with their start and end apart: 7 -> 7, of which waited for: 4 -> 4; matrix products, arithmetic and copies ran while one was open for 4% -> 3% of each run, Pallas kernels for 27% -> 19%
where the time goes in v2:
time: 74.3 us; the launch traced here: 73.8 us
  Pallas kernels  18.5 us (25%)
  waiting for transfers between devices  18.1 us (24%)
  starting transfers between devices  17.7 us (24%)
  blocking collectives  15 us (20%)
  local copies, waits for them, and re-layouts  3.53 us (5%)
  other arithmetic  0.89 us (1%)
    ppermute x3, waiting for transfers between devices, sum_over_rows(): lax.ppermute(value, 'rows', [(i, i ^ step) for i in range(count)])  15.9 us
    pallas_call x1, Pallas kernels, local(): pl.pallas_call(factor_kernel, out_shape=pltpu.VMEM((BLOCK, order), bf16),...  14.3 us
    all_gather x1, blocking collectives, local(): lax.all_gather(jnp.concatenate([low, mode_slab, high], axis=0), 'modes',...  7.89 us
    all_gather x1, blocking collectives, local(): lax.all_gather(share, 'modes', axis=0).reshape(len(lower) * BLOCK, BLOCK)  7.09 us
    ppermute x3, starting transfers between devices, sum_over_rows(): lax.ppermute(value, 'rows', [(i, i ^ step) for i in range(count)])  6.73 us
    ppermute x1, starting transfers between devices, local(): lax.ppermute(scaled_edge(slice(rows_dev - BAND, rows_dev)), 'rows', up)  4.87 us
    ppermute x1, starting transfers between devices, local(): rim_high = lax.ppermute(first, 'rows', back)  3.46 us
    ppermute x1, waiting for transfers between devices, local(): high = lax.ppermute(scaled_edge(slice(0, BAND)), 'rows', down)  2.23 us
  transfers between devices with their start and end apart: 7, of which 4 were waited for; matrix products, arithmetic and copies ran while one was open for 3% of the time, Pallas kernels for 19%

profile of v2, /device:TPU:0, one launch (start us, length us, event | category | flops | bytes accessed | tf_op | source)
XLA Modules:
  0.0 73.8 jit_solution(2122942440432442292)
XLA Ops:
  0.0 0.8 %fusion.1 = (f32[64]{0:T(128)S(1)}, f32[64]{0:T(128)S(1)}) fusion(f32[512]{0:T(512)} %param.11), kind=kLoop, calls=%fused_computation.8 | loop fusion | bytes 1024 | tf_op jit(solution)/shard_map/slice | solution.py:230
  0.8 0.8 %multiply_convert_fusion.1 = (bf16[64,128]{1,0:T(8,128)(2,1)S(1)}, bf16[64,128]{1,0:T(8,128)(2,1)S(1)}) fusion(bf16[512,128]{1,0:T(8,128)(2,1)} %param.9, f32[64]{0:T(128)S(1)} %get-tuple-element.19, f32[64]{0:T(128)S(1)} %get-tuple-element.20), kind=kLoop, calls=%fused_computation.2 | loop fusion | flops 49152 | bytes 66048 | tf_op jit(solution)/shard_map/convert_element_type | solution.py:230
  1.6 4.9 %collective-permute-start = (bf16[64,128]{1,0:T(8,128)(2,1)S(1)}, bf16[64,128]{1,0:T(8,128)(2,1)S(1)}, u32[]{:S(2)}, u32[]{:S(2)}) collective-permute-start(bf16[64,128]{1,0:T(8,128)(2,1)S(1)} %get-tuple-element.17), channel_id=1, source_target_pairs={{0,4},{4,8},{8,12},{12,16},{16,20},{20,24},{24,28},{1,5},{5,9},{9,... | collective-permute-start | bytes 49160 | tf_op jit(solution)/shard_map/ppermute | solution.py:232
  6.5 1.3 %collective-permute-start.1 = (bf16[64,128]{1,0:T(8,128)(2,1)S(1)}, bf16[64,128]{1,0:T(8,128)(2,1)S(1)}, u32[]{:S(2)}, u32[]{:S(2)}) collective-permute-start(bf16[64,128]{1,0:T(8,128)(2,1)S(1)} %get-tuple-element.18), channel_id=1, source_target_pairs={{4,0},{8,4},{12,8},{16,12},{20,16},{24,20},{28,24},{5,1},{9,5},{13... | collective-permute-start | bytes 49160 | tf_op jit(solution)/shard_map/ppermute | solution.py:233
  7.8 0.0 copy-start.3
  7.8 1.2 %dynamic-slice_bitcast_fusion.refs_0_ = s32[7]{0:T(128)} fusion(s32[4,7]{1,0:T(4,128)} %constant.32.clone, s32[]{:T(128)S(6)} %select_n.11), kind=kLoop, calls=%fused_computation.7 | loop fusion | bytes 60 | tf_op jit(solution)/shard_map/squeeze | solution.py:246
  9.1 0.0 copy-done.3
  9.1 0.0 copy-start.2
  9.1 0.1 copy.10.refs_4_
  9.2 0.5 copy-done.2
  9.8 0.0 copy-start.1
  9.8 0.1 copy.11.refs_5_
  9.9 0.0 collective-permute-done
  9.9 2.2 %collective-permute-done.1 = bf16[64,128]{1,0:T(8,128)(2,1)S(1)} collective-permute-done((bf16[64,128]{1,0:T(8,128)(2,1)S(1)}, bf16[64,128]{1,0:T(8,128)(2,1)S(1)}, u32[]{:S(2)}, u32[]{:S(2)}) %collective-permute-start.1) | collective-permute-done | bytes 16416 | tf_op jit(solution)/shard_map/ppermute | solution.py:233
  12.2 0.0 copy-done.1
  12.2 7.9 %all-gather = bf16[2560,128]{1,0:T(8,128)(2,1)S(1)} all-gather(bf16[640,128]{1,0:T(8,128)(2,1)S(1)} %pad_maximum_fusion), channel_id=2, replica_groups=mesh['rows'=8,'modes'=4] {'modes'}, dimensions={0}, use_global_device_ids=true | all-gather | bytes 819200 | tf_op jit(solution)/shard_map/all_gather | solution.py:234
  20.1 2.0 %image.1 = (bf16[256,512]{1,0:T(8,128)(2,1)S(1)}, bf16[256,512]{1,0:T(8,128)(2,1)S(1)}, f32[320,128]{1,0:T(8,128)S(1)}) custom-call(s32[7]{0:T(128)} %dynamic-slice_bitcast_fusion.refs_0_, f32[4]{0:T(128)} %refs_1_.1, s32[4]{0:T(128)} %refs_2_.1, bf16[4,640,128]{2,1,0:T(8,128)(2,1)S(1)} %bitcast.6, f32[512,1]{1,0:T(8,128)S(1)} %copy.10.refs_4_, ...), custom_call_target="tpu_custom_call" | custom-call | tf_op jit(solution)/shard_map/image/pallas_call | solution.py:248
  22.1 2.5 %collective-permute-start.2 = (f32[320,128]{1,0:T(8,128)S(1)}, f32[320,128]{1,0:T(8,128)S(1)}, u32[]{:S(2)}, u32[]{:S(2)}) collective-permute-start(f32[320,128]{1,0:T(8,128)S(1)} %get-tuple-element.13), channel_id=1, source_target_pairs={{0,4},{4,0},{8,12},{12,8},{16,20},{20,16},{24,28},{28,24},{1,5},{5... | collective-permute-start | bytes 491528 | tf_op jit(solution)/shard_map/ppermute | solution.py:202
  24.6 4.7 %collective-permute-done.2 = f32[320,128]{1,0:T(8,128)S(1)} collective-permute-done((f32[320,128]{1,0:T(8,128)S(1)}, f32[320,128]{1,0:T(8,128)S(1)}, u32[]{:S(2)}, u32[]{:S(2)}) %collective-permute-start.2) | collective-permute-done | bytes 163872 | tf_op jit(solution)/shard_map/ppermute | solution.py:202
  29.3 1.6 %collective-permute-start.3 = (f32[320,128]{1,0:T(8,128)S(1)}, f32[320,128]{1,0:T(8,128)S(1)}, u32[]{:S(2)}, u32[]{:S(2)}) collective-permute-start(f32[320,128]{1,0:T(8,128)S(1)} %add.21), channel_id=1, source_target_pairs={{0,8},{4,12},{8,0},{12,4},{16,24},{20,28},{24,16},{28,20},{1,9},{5... | collective-permute-start | bytes 491528 | tf_op jit(solution)/shard_map/ppermute | solution.py:202
  31.0 4.3 %collective-permute-done.3 = f32[320,128]{1,0:T(8,128)S(1)} collective-permute-done((f32[320,128]{1,0:T(8,128)S(1)}, f32[320,128]{1,0:T(8,128)S(1)}, u32[]{:S(2)}, u32[]{:S(2)}) %collective-permute-start.3) | collective-permute-done | bytes 163872 | tf_op jit(solution)/shard_map/ppermute | solution.py:202
  35.3 0.0 copy-start.4
  35.3 2.6 %collective-permute-start.4 = (f32[320,128]{1,0:T(8,128)S(1)}, f32[320,128]{1,0:T(8,128)S(1)}, u32[]{:S(2)}, u32[]{:S(2)}) collective-permute-start(f32[320,128]{1,0:T(8,128)S(1)} %add.22), channel_id=1, source_target_pairs={{0,16},{4,20},{8,24},{12,28},{16,0},{20,4},{24,8},{28,12},{1,17},{... | collective-permute-start | bytes 491528 | tf_op jit(solution)/shard_map/ppermute | solution.py:202
  37.9 0.0 copy-start
  37.9 6.9 %collective-permute-done.4 = f32[320,128]{1,0:T(8,128)S(1)} collective-permute-done((f32[320,128]{1,0:T(8,128)S(1)}, f32[320,128]{1,0:T(8,128)S(1)}, u32[]{:S(2)}, u32[]{:S(2)}) %collective-permute-start.4) | collective-permute-done | bytes 163872 | tf_op jit(solution)/shard_map/ppermute | solution.py:202
  44.8 1.3 %collective-permute-start.5 = (bf16[256,512]{1,0:T(8,128)(2,1)S(1)}, bf16[256,512]{1,0:T(8,128)(2,1)S(1)}, u32[]{:S(2)}, u32[]{:S(2)}) collective-permute-start(bf16[256,512]{1,0:T(8,128)(2,1)S(1)} %get-tuple-element.14.second), channel_id=1, source_target_pairs={{0,4},{4,8},{8,12},{12,16},{16,20},{20,24},{24,28},{28,0},{1,5},{5... | collective-permute-start | bytes 786440 | tf_op jit(solution)/shard_map/ppermute | solution.py:268
  46.1 3.5 %collective-permute-start.6 = (bf16[256,512]{1,0:T(8,128)(2,1)S(1)}, bf16[256,512]{1,0:T(8,128)(2,1)S(1)}, u32[]{:S(2)}, u32[]{:S(2)}) collective-permute-start(bf16[256,512]{1,0:T(8,128)(2,1)S(1)} %get-tuple-element.15.first), channel_id=1, source_target_pairs={{4,0},{8,4},{12,8},{16,12},{20,16},{24,20},{28,24},{0,28},{5,1},{9... | collective-permute-start | bytes 786440 | tf_op jit(solution)/shard_map/ppermute | solution.py:269
  49.6 0.0 copy-done.4
  49.6 0.6 reshape.11.blocks_ref
  50.2 7.1 %all-gather.1.gram = f32[1280,128]{1,0:T(8,128)S(1)} all-gather(f32[320,128]{1,0:T(8,128)S(1)} %add.23), channel_id=3, replica_groups=mesh['rows'=8,'modes'=4] {'modes'}, dimensions={0}, use_global_device_ids=true | all-gather | bytes 819200 | tf_op jit(solution)/shard_map/all_gather | solution.py:270
  57.3 14.3 %factor.1.inverse = bf16[128,512]{1,0:T(8,128)(2,1)S(1)} custom-call(s32[1]{0:T(128)} %bitcast.4.which_ref, f32[1280,128]{1,0:T(8,128)S(1)} %all-gather.1.gram), custom_call_target="tpu_custom_call" | custom-call | tf_op jit(solution)/shard_map/factor/pallas_call | solution.py:272
  71.6 0.0 collective-permute-done.5.low
  71.6 0.0 collective-permute-done.6.high
  71.6 0.0 copy-done
  71.6 2.2 %project.1 = bf16[2,128,512]{2,1,0:T(8,128)(2,1)} custom-call(s32[8]{0:T(128)} %reshape.11.blocks_ref, s32[2]{0:T(128)} %counts_ref.1, bf16[256,512]{1,0:T(8,128)(2,1)S(1)} %collective-permute-done.5.low, bf16[256,512]{1,0:T(8,128)(2,1)S(1)} %get-tuple-element.15.first, bf16[256,512]{1,0:T(8,128)(2,1)S(1)} %get-tuple-element.14.second, ...), custom_call_target="tpu_custom_call" | custom-call | tf_op jit(solution)/shard_map/project/pallas_call | solution.py:289
  (5 shorter events, 0.1 us)
Async XLA Ops:
  1.6 8.3 %collective-permute-start = (bf16[64,128]{1,0:T(8,128)(2,1)S(1)}, bf16[64,128]{1,0:T(8,128)(2,1)S(1)}, u32[]{:S(2)}, u32[]{:S(2)}) collective-permute-start(bf16[64,128]{1,0:T(8,128)(2,1)S(1)} %get-tuple-element.17), channel_id=1, source_target_pairs={{0,4},{4,8},{8,12},{12,16},{16,20},{20,24},{24,28},{1,5},{5,9},{9,... | collective-permute-start | bytes 49160 | tf_op jit(solution)/shard_map/ppermute | solution.py:232
  6.5 5.6 %collective-permute-start.1 = (bf16[64,128]{1,0:T(8,128)(2,1)S(1)}, bf16[64,128]{1,0:T(8,128)(2,1)S(1)}, u32[]{:S(2)}, u32[]{:S(2)}) collective-permute-start(bf16[64,128]{1,0:T(8,128)(2,1)S(1)} %get-tuple-element.18), channel_id=1, source_target_pairs={{4,0},{8,4},{12,8},{16,12},{20,16},{24,20},{28,24},{5,1},{9,5},{13... | collective-permute-start | bytes 49160 | tf_op jit(solution)/shard_map/ppermute | solution.py:233
  7.8 1.3 %copy-start.3 = (f32[512]{0:T(512)S(1)}, f32[512]{0:T(512)}, u32[]{:S(2)}) copy-start(f32[512]{0:T(512)} %param.10) | copy-start | bytes 6148
  9.1 0.7 copy-start.2
  9.8 2.4 %copy-start.1 = (bf16[512,128]{1,0:T(8,128)(2,1)S(1)}, bf16[512,128]{1,0:T(8,128)(2,1)}, u32[]{:S(2)}) copy-start(bf16[512,128]{1,0:T(8,128)(2,1)} %param.9) | copy-start | bytes 393220
  22.1 7.2 %collective-permute-start.2 = (f32[320,128]{1,0:T(8,128)S(1)}, f32[320,128]{1,0:T(8,128)S(1)}, u32[]{:S(2)}, u32[]{:S(2)}) collective-permute-start(f32[320,128]{1,0:T(8,128)S(1)} %get-tuple-element.13), channel_id=1, source_target_pairs={{0,4},{4,0},{8,12},{12,8},{16,20},{20,16},{24,28},{28,24},{1,5},{5... | collective-permute-start | bytes 491528 | tf_op jit(solution)/shard_map/ppermute | solution.py:202
  29.3 5.9 %collective-permute-start.3 = (f32[320,128]{1,0:T(8,128)S(1)}, f32[320,128]{1,0:T(8,128)S(1)}, u32[]{:S(2)}, u32[]{:S(2)}) collective-permute-start(f32[320,128]{1,0:T(8,128)S(1)} %add.21), channel_id=1, source_target_pairs={{0,8},{4,12},{8,0},{12,4},{16,24},{20,28},{24,16},{28,20},{1,9},{5... | collective-permute-start | bytes 491528 | tf_op jit(solution)/shard_map/ppermute | solution.py:202
  35.3 14.3 %copy-start.4 = (s32[2,4]{1,0:T(2,128)S(1)}, s32[2,4]{1,0:T(2,128)}, u32[]{:S(2)}) copy-start(s32[2,4]{1,0:T(2,128)} %param.14) | copy-start | bytes 100
  35.3 9.5 %collective-permute-start.4 = (f32[320,128]{1,0:T(8,128)S(1)}, f32[320,128]{1,0:T(8,128)S(1)}, u32[]{:S(2)}, u32[]{:S(2)}) collective-permute-start(f32[320,128]{1,0:T(8,128)S(1)} %add.22), channel_id=1, source_target_pairs={{0,16},{4,20},{8,24},{12,28},{16,0},{20,4},{24,8},{28,12},{1,17},{... | collective-permute-start | bytes 491528 | tf_op jit(solution)/shard_map/ppermute | solution.py:202
  37.9 33.7 %copy-start = (bf16[2,512,512]{2,1,0:T(8,128)(2,1)S(1)}, bf16[2,512,512]{2,1,0:T(8,128)(2,1)}, u32[]{:S(2)}) copy-start(bf16[2,512,512]{2,1,0:T(8,128)(2,1)} %shapes.1) | copy-start | bytes 3145732
  44.8 26.8 %collective-permute-start.5 = (bf16[256,512]{1,0:T(8,128)(2,1)S(1)}, bf16[256,512]{1,0:T(8,128)(2,1)S(1)}, u32[]{:S(2)}, u32[]{:S(2)}) collective-permute-start(bf16[256,512]{1,0:T(8,128)(2,1)S(1)} %get-tuple-element.14.second), channel_id=1, source_target_pairs={{0,4},{4,8},{8,12},{12,16},{16,20},{20,24},{24,28},{28,0},{1,5},{5... | collective-permute-start | bytes 786440 | tf_op jit(solution)/shard_map/ppermute | solution.py:268
  46.1 25.5 %collective-permute-start.6 = (bf16[256,512]{1,0:T(8,128)(2,1)S(1)}, bf16[256,512]{1,0:T(8,128)(2,1)S(1)}, u32[]{:S(2)}, u32[]{:S(2)}) collective-permute-start(bf16[256,512]{1,0:T(8,128)(2,1)S(1)} %get-tuple-element.15.first), channel_id=1, source_target_pairs={{4,0},{8,4},{12,8},{16,12},{20,16},{24,20},{28,24},{0,28},{5,1},{9... | collective-permute-start | bytes 786440 | tf_op jit(solution)/shard_map/ppermute | solution.py:269

commit v3 on v2

v3 whole, which is shorter than its diff:
```python
import jax
import jax.numpy as jnp
from jax import lax
from jax.experimental import pallas as pl
from jax.experimental.pallas import tpu as pltpu
from jax.sharding import PartitionSpec as P

BLOCK = 128
BMAX = 4
NOFF = 4
BAND = 64
SHARES = (
    ((0, 0), (1, 1), (1, 0)),
    ((2, 2), (3, 3), (2, 0)),
    ((2, 1), (2, 1), (3, 0)),
    ((3, 1), (3, 1), (3, 2)),
)

f32 = jnp.float32
bf16 = jnp.bfloat16
VMEM = pl.BlockSpec(memory_space=pltpu.VMEM)


def near(x):
    return pltpu.with_memory_space_constraint(x, pltpu.VMEM)

SMEM = pl.BlockSpec(memory_space=pltpu.SMEM)


def bf16_parts(x):
    top = x.astype(bf16)
    rest = x - top.astype(f32)
    middle = rest.astype(bf16)
    return top, middle, (rest - middle.astype(f32)).astype(bf16)


def dot(a, b, dims=((1,), (0,))):
    return lax.dot_general(a, b, (dims, ((), ())), preferred_element_type=f32)


def dot_f32(a, b, dims=((1,), (0,))):
    return lax.dot_general(
        a, b, (dims, ((), ())), precision=lax.Precision.HIGHEST, preferred_element_type=f32
    )


def pack_kernel(slab, gain, diag, out):
    size = BLOCK
    out[0:size, :] = slab[0:size, :]
    rows = [*bf16_parts(gain[0:1, :]), *bf16_parts(diag[0:1, :])]
    rows.append(jnp.zeros((out.shape[0] - size - len(rows), size), bf16))
    out[size:, :] = jnp.concatenate(rows, axis=0)


def image_kernel(scale, which_ref, coef_ref, offset_ref, gathered, packed, gain_ref, diag_ref, first, second, share, scaled, gains, diags):
    modes = gathered.shape[0]
    size = BLOCK
    tiles = gain_ref.shape[0]
    rows = tiles * size
    split = first.shape[0]
    wide = size + 2 * BAND
    row = lax.broadcasted_iota(jnp.int32, (size, wide), 0)
    column = lax.broadcasted_iota(jnp.int32, (size, wide), 1)
    distance = jnp.abs(column - row - BAND)
    band = jnp.zeros((size, wide), f32)
    for j in range(NOFF):
        band = band + jnp.where(distance == offset_ref[j], coef_ref[j], 0.0)
    parts = bf16_parts(band)
    across_end = jnp.logical_and(which_ref[1] != 0, (row < size - BAND) != (column < size))
    last_parts = bf16_parts(jnp.where(across_end, 0.0, band))
    tail = packed[size:, :].astype(f32)
    next_gain = tail[0:1, :] + tail[1:2, :] + tail[2:3, :]
    next_diag = tail[3:4, :] + tail[4:5, :] + tail[5:6, :]
    for ref, own, extra in ((gains, gain_ref, next_gain), (diags, diag_ref, next_diag)):
        filler = jnp.zeros((8 - (tiles + 1) % 8, size), f32)
        turned = jnp.transpose(jnp.concatenate([own[...], extra, filler], axis=0))
        for i in range(tiles + 1):
            ref[i * size : (i + 1) * size, :] = jnp.broadcast_to(turned[:, i : i + 1], (size, size))
    for m in range(modes):
        lanes = slice(m * size, (m + 1) * size)
        scaled[:, lanes] = (gains[...] * gathered[m].astype(f32)).astype(bf16)
    for i in range(tiles):
        rows_in = scaled[i * size : i * size + wide, :]
        p = last_parts if i == tiles - 1 else parts
        neighbour = dot(p[0], rows_in) + dot(p[1], rows_in) + dot(p[2], rows_in)
        here = slice(BAND + i * size, BAND + (i + 1) * size)
        gain, diag = gains[here, :], diags[here, :]
        for m in range(modes):
            lanes = slice(m * size, (m + 1) * size)
            value = (diag * gathered[m, here, :].astype(f32) + gain * neighbour[:, lanes]).astype(bf16)
            for image, low, high in ((first, 0, split), (second, split, rows)):
                a, b = max(low, i * size), min(high, (i + 1) * size)
                if a < b:
                    image[a - low : b - low, lanes] = value[a - i * size : b - i * size, :]

    def block(s):
        i, j = which_ref[2 + 2 * s], which_ref[3 + 2 * s]
        total = jnp.zeros((size, size), f32)
        for image, at in ((first, BAND), (second, BAND + split)):
            image_i = image[:, pl.ds(pl.multiple_of(i * size, size), size)]
            image_j = image[:, pl.ds(pl.multiple_of(j * size, size), size)]
            slab_i = gathered[i, at : at + image.shape[0], :]
            slab_j = gathered[j, at : at + image.shape[0], :]
            over_rows = ((0,), (0,))
            total = total + dot(image_i, slab_j, over_rows) + dot(slab_i, image_j, over_rows)
        return total * scale

    row = lax.broadcasted_iota(jnp.int32, (size, size), 0)
    column = lax.broadcasted_iota(jnp.int32, (size, size), 1)
    upper = block(1)
    share[0:size, :] = jnp.where(row >= column, block(0), upper)
    share[size : 2 * size, :] = block(2)
    diagonal = jnp.sum(jnp.where(row == column, upper, 0.0), axis=0, keepdims=True)
    share[2 * size :, :] = jnp.broadcast_to(diagonal, (8, size))


def lanes_of(x, t):
    return jnp.broadcast_to(x[:, t : t + 1], (8, BLOCK))


def rows_of(x, t):
    return jnp.broadcast_to(x[t : t + 1, :], (8, BLOCK))


def inverse_factor(square, depth=3):
    panels = BLOCK // 8
    sub = lax.broadcasted_iota(jnp.int32, (8, BLOCK), 0)
    lane = lax.broadcasted_iota(jnp.int32, (8, BLOCK), 1)
    rows = [square[8 * p : 8 * p + 8, :] for p in range(panels)]
    own = [lanes_of(rows[0], t) for t in range(8)]
    result = []
    for p in range(panels):
        below = range(p + 1, min(panels, p + 1 + depth))
        under = {i: [lanes_of(rows[i], 8 * p + t) for t in range(8)] for i in below}
        ahead = [lanes_of(rows[p + 1], 8 * p + 8 + t) for t in range(8)] if p + 1 < panels else []
        inside = jnp.logical_and(lane >= 8 * p, lane < 8 * p + 8)
        a = jnp.where(inside, (lane == sub + 8 * p).astype(f32), rows[p])
        for i in below:
            rows[i] = jnp.where(inside, 0.0, rows[i])
        pivots = jnp.ones((8, BLOCK), f32)
        inverses = jnp.ones((8, BLOCK), f32)
        for t in range(8):
            pivot = rows_of(own[t], t)
            inverse = 1.0 / pivot
            pivots = jnp.where(sub == t, pivot, pivots)
            inverses = jnp.where(sub == t, inverse, inverses)
            f = jnp.where(sub > t, own[t], 0.0) * inverse
            g = {i: under[i][t] * inverse for i in below}
            for u in range(t + 1, 8):
                u_row = rows_of(own[u], t)
                own[u] = own[u] - f * u_row
                for i in below:
                    under[i][u] = under[i][u] - g[i] * u_row
            for u in range(len(ahead)):
                ahead[u] = ahead[u] - g[p + 1] * rows_of(under[p + 1][t], u)
            a_row = rows_of(a, t)
            if t < 7:
                a = a - f * a_row
            for i in below:
                rows[i] = rows[i] - g[i] * a_row
        result.append(jnp.where(lane < 8 * p + 8, a * lax.rsqrt(pivots), 0.0))
        own = ahead
        rest = p + 1 + depth
        if rest < panels:
            a0, a1, a2 = bf16_parts(a * inverses)
            b0, b1, b2 = bf16_parts(a)
            update = dot(
                jnp.concatenate([a0, a0, a1, a0, a2, a1], axis=0)[:, 8 * rest :],
                jnp.concatenate([b0, b1, b0, b2, b0, b1], axis=0),
                ((0,), (0,)),
            )
            for i in range(rest, panels):
                at = slice(8 * (i - rest), 8 * (i - rest) + 8)
                rows[i] = jnp.where(inside, 0.0, rows[i]) - update[at, :]
    return jnp.concatenate(result, axis=0)


def factor_kernel(which_ref, share, beside, across, opposite, inverse, gram, schur, solved):
    for distance, part in enumerate((share, beside, across, opposite)):
        gram[which_ref[0] ^ distance] = part[...]
    count = inverse.shape[1] // BLOCK
    size = BLOCK
    place = lambda i, j: slice((i * (i + 1) // 2 + j) * size, (i * (i + 1) // 2 + j + 1) * size)
    across = ((1,), (1,))
    row = lax.broadcasted_iota(jnp.int32, (size, size), 0)
    column = lax.broadcasted_iota(jnp.int32, (size, size), 1)
    for m, (one, two, three) in enumerate(SHARES):
        square = gram[m, 0:size, :]
        if one == two:
            schur[place(*one), :] = square
        else:
            turned = jnp.transpose(square)
            schur[place(*one), :] = jnp.where(row >= column, square, turned)
            diagonal = jnp.broadcast_to(gram[m, 2 * size : 2 * size + 1, :], (size, size))
            schur[place(*two), :] = jnp.where(
                row < column, square, jnp.where(row == column, diagonal, turned)
            )
        schur[place(*three), :] = gram[m, size : 2 * size, :]
    solved[...] = jnp.zeros(solved.shape, f32)
    for k in range(count):
        w = inverse_factor(schur[place(k, k), :])
        here = slice(k * size, (k + 1) * size)
        if k:
            solved[here, : k * size] = -dot_f32(w, solved[here, : k * size])
        solved[here, here] = w
        lower = [None] * count
        for i in range(k + 1, count):
            lower[i] = dot_f32(schur[place(i, k), :], w, across)
        for i in range(k + 1, count):
            for j in range(k + 1, i + 1):
                schur[place(i, j), :] = schur[place(i, j), :] - dot_f32(lower[i], lower[j], across)
        for i in range(k + 1, count):
            there = slice(i * size, (i + 1) * size)
            done = (k + 1) * size
            solved[there, :done] = solved[there, :done] + dot_f32(lower[i], solved[here, :done])
    mine = pl.multiple_of(which_ref[0] * size, size)
    inverse[...] = solved[pl.ds(mine, size), :].astype(bf16)


def project_kernel(blocks_ref, counts_ref, low, first, second, high, inverse, shapes, out, basis, picked):
    size = BLOCK
    across = ((1,), (1,))
    at = 0
    for part in (low, first, second, high):
        basis[at : at + part.shape[0], :] = dot(part[...], inverse[...], across).astype(bf16)
        at += part.shape[0]
    for c in range(out.shape[0]):
        for s in range(BMAX):
            start = pl.multiple_of(blocks_ref[BMAX * c + s] * size, size)
            rows = basis[pl.ds(start, size), :]
            picked[s * size : (s + 1) * size, :] = jnp.where(s < counts_ref[c], rows, jnp.zeros_like(rows))
        out[c] = dot(picked[...], shapes[c], ((0,), (0,))).astype(bf16)


def exchange(value, axis, step):
    return lax.ppermute(value, axis, [(i, i ^ step) for i in range(lax.axis_size(axis))])


def sum_over_rows(value):
    step = 1
    while step < lax.axis_size("rows"):
        value = value + exchange(value, "rows", step)
        step *= 2
    return value


def local(
    mode_slab,
    mass_diag,
    mass_gain,
    band_coef,
    band_offsets,
    boundary_blocks,
    boundary_counts,
    boundary_modes,
):
    rows_dev, mode_cols = mode_slab.shape
    modes = lax.axis_size("modes")
    row_devices = lax.axis_size("rows")
    order = mode_cols * modes
    count = order // BLOCK
    per_dev = rows_dev // BLOCK
    rim_rows = per_dev // 2 * BLOCK
    total_rows = rows_dev * row_devices
    assert modes == len(SHARES) and order == modes * BLOCK and mode_cols == BLOCK
    assert rows_dev == 2 * rim_rows and row_devices & (row_devices - 1) == 0
    around = [(i, (i + 1) % row_devices) for i in range(row_devices)]
    back = [(target, source) for source, target in around]
    gain_rows = near(mass_gain.reshape(per_dev, BLOCK))
    diag_rows = near(mass_diag.reshape(per_dev, BLOCK))

    packed = pl.pallas_call(
        pack_kernel,
        out_shape=pltpu.VMEM((BLOCK + 16, mode_cols), bf16),
        in_specs=[VMEM, VMEM, VMEM],
        out_specs=VMEM,
        name="pack",
    )(mode_slab, mass_gain.reshape(per_dev, BLOCK), mass_diag.reshape(per_dev, BLOCK))
    packed = lax.ppermute(packed, "rows", back)
    gathered = lax.all_gather(jnp.concatenate([mode_slab, packed[:BLOCK, :]], axis=0), "modes", axis=0)

    mode_index = lax.axis_index("modes")
    is_last = lax.axis_index("rows") == row_devices - 1
    blocks = jnp.asarray(SHARES, jnp.int32).reshape(modes, -1)[mode_index]
    which = jnp.concatenate([jnp.stack([mode_index, is_last.astype(jnp.int32)]).astype(jnp.int32), blocks])
    extended = rows_dev + BLOCK
    first, second, share = pl.pallas_call(
        lambda *refs: image_kernel(0.5 / total_rows, *refs),
        out_shape=(
            pltpu.VMEM((rim_rows - BAND, order), bf16),
            pltpu.VMEM((rim_rows + BAND, order), bf16),
            pltpu.VMEM((2 * BLOCK + 8, BLOCK), f32),
        ),
        in_specs=[SMEM, SMEM, SMEM, VMEM, VMEM, VMEM, VMEM],
        out_specs=(VMEM, VMEM, VMEM),
        scratch_shapes=[
            pltpu.VMEM((extended, order), bf16),
            pltpu.VMEM((extended, BLOCK), f32),
            pltpu.VMEM((extended, BLOCK), f32),
        ],
        name="image",
    )(which, band_coef, band_offsets, near(gathered), near(packed), gain_rows, diag_rows)

    share = sum_over_rows(share)
    share, one, two = lax.optimization_barrier((share, first, second))
    across = exchange(share, "modes", 2)
    beside = exchange(share, "modes", 1)
    rim_low = lax.ppermute(two, "rows", around)
    rim_high = lax.ppermute(one, "rows", back)
    opposite = exchange(across, "modes", 1)

    inverse = pl.pallas_call(
        factor_kernel,
        out_shape=pltpu.VMEM((BLOCK, order), bf16),
        in_specs=[SMEM, VMEM, VMEM, VMEM, VMEM],
        out_specs=VMEM,
        scratch_shapes=[
            pltpu.VMEM((modes, 2 * BLOCK + 8, BLOCK), f32),
            pltpu.VMEM((count * (count + 1) // 2 * BLOCK, BLOCK), f32),
            pltpu.VMEM((order, order), f32),
        ],
        name="factor",
    )(which, near(share), near(beside), near(across), near(opposite))

    total_blocks = per_dev * row_devices
    window_start = lax.axis_index("rows") * per_dev - per_dev // 2
    local_blocks = jnp.mod(boundary_blocks - window_start, total_blocks).reshape(-1)
    owned, _, width = boundary_modes.shape
    window = per_dev + 2 * (per_dev // 2)
    return pl.pallas_call(
        project_kernel,
        out_shape=jax.ShapeDtypeStruct((owned, mode_cols, width), bf16),
        in_specs=[SMEM, SMEM, VMEM, VMEM, VMEM, VMEM, VMEM, VMEM],
        out_specs=VMEM,
        scratch_shapes=[
            pltpu.VMEM((window * BLOCK, BLOCK), bf16),
            pltpu.VMEM((BMAX * BLOCK, BLOCK), bf16),
        ],
        name="project",
    )(local_blocks, boundary_counts, near(rim_low), near(first), near(second), near(rim_high), near(inverse), near(boundary_modes))


def solution(mesh):
    in_specs = (
        P("rows", "modes"),
        P("rows"),
        P("rows"),
        P(),
        P(),
        P("rows", None),
        P("rows"),
        P("rows", None, None),
    )
    out_specs = P("rows", "modes", None)
    return jax.shard_map(local, mesh=mesh, in_specs=in_specs, out_specs=out_specs, check_vma=False)
```

time: 74.3 us -> 62.3 us (0.84)
  blocking collectives: 15 us -> 7.89 us
  starting transfers between devices: 17.7 us -> 14.9 us
  local copies, waits for them, and re-layouts: 3.53 us -> 1.37 us
  Pallas kernels: 18.5 us -> 19.8 us
    all_gather x2 -> x1, blocking collectives: 15 us -> 7.89 us  [local(): lax.all_gather(jnp.concatenate([mode_slab, packed[:BLOCK, :]], axis=0), '...]
    ppermute x7 -> x9, starting transfers between devices: 17.7 us -> 14.9 us  [the longest x1 6.06 us: local(): packed = lax.ppermute(packed, 'rows', back)]
    pallas_call x0 -> x1, Pallas kernels: none -> 0.99 us  [local(): pl.pallas_call(pack_kernel, out_shape=pltpu.VMEM((BLOCK + 16, mode_cols),...]
    slice x1, local copies, waits for them, and re-layouts: 0.83 us -> 0.01 us  [local(): packed[:BLOCK, :]]
    convert_element_type x1 -> x0, other arithmetic: 0.81 us -> none  [scaled_edge(): return (mass_gain[rows, None] * mode_slab[rows, :].astype(f32)).astype(bf16)]
    ppermute x7 -> x9, waiting for transfers between devices: 18.1 us -> 17.4 us  [the longest x6 17 us: exchange(): lax.ppermute(value, axis, [(i, i ^ step) for i in range(lax.axis_size(axi...]
  transfers between devices with their start and end apart: 7 -> 9, of which waited for: 4 -> 5; matrix products, arithmetic and copies ran while one was open for 3% -> 3% of each run, Pallas kernels for 19% -> 23%
where the time goes in v3:
time: 62.3 us; the launch traced here: 62 us
  Pallas kernels  19.8 us (32%)
  waiting for transfers between devices  17.4 us (28%)
  starting transfers between devices  14.9 us (24%)
  blocking collectives  7.89 us (13%)
  local copies, waits for them, and re-layouts  1.37 us (2%)
  other arithmetic  0.7 us (1%)
    ppermute x6, waiting for transfers between devices, exchange(): lax.ppermute(value, axis, [(i, i ^ step) for i in range(lax.axis_size(axi...  17 us
    pallas_call x1, Pallas kernels, local(): pl.pallas_call(factor_kernel, out_shape=pltpu.VMEM((BLOCK, order), bf16),...  14.5 us
    all_gather x1, blocking collectives, local(): lax.all_gather(jnp.concatenate([mode_slab, packed[:BLOCK, :]], axis=0), '...  7.89 us
    ppermute x1, starting transfers between devices, local(): packed = lax.ppermute(packed, 'rows', back)  6.06 us
    ppermute x6, starting transfers between devices, exchange(): lax.ppermute(value, axis, [(i, i ^ step) for i in range(lax.axis_size(axi...  4.1 us
    ppermute x1, starting transfers between devices, local(): rim_high = lax.ppermute(one, 'rows', back)  3.47 us
    pallas_call x1, Pallas kernels, local(): pl.pallas_call(project_kernel, out_shape=jax.ShapeDtypeStruct((owned, mod...  2.17 us
    pallas_call x1, Pallas kernels, local(): pl.pallas_call(lambda *refs: image_kernel(0.5 / total_rows, *refs), out_s...  2.06 us
  transfers between devices with their start and end apart: 9, of which 5 were waited for; matrix products, arithmetic and copies ran while one was open for 3% of the time, Pallas kernels for 23%

profile of v3, /device:TPU:0, one launch (start us, length us, event | category | flops | bytes accessed | tf_op | source)
XLA Modules:
  0.0 62.0 jit_solution(14323618396341594939)
XLA Ops:
  0.0 0.0 copy-start.3
  0.0 1.0 %pack.1 = bf16[144,128]{1,0:T(8,128)(2,1)S(1)} custom-call(bf16[512,128]{1,0:T(8,128)(2,1)} %slab.1, f32[4,128]{1,0:T(4,128)} %bitcast.8, f32[4,128]{1,0:T(4,128)} %bitcast.10), custom_call_target="tpu_custom_call" | custom-call | tf_op jit(solution)/shard_map/pack/pallas_call | solution.py:272
  1.0 6.1 %collective-permute-start = (bf16[144,128]{1,0:T(8,128)(2,1)S(1)}, bf16[144,128]{1,0:T(8,128)(2,1)S(1)}, u32[]{:S(2)}, u32[]{:S(2)}) collective-permute-start(bf16[144,128]{1,0:T(8,128)(2,1)S(1)} %pack.1), channel_id=1, source_target_pairs={{4,0},{8,4},{12,8},{16,12},{20,16},{24,20},{28,24},{0,28},{5,1},{9... | collective-permute-start | bytes 110600 | tf_op jit(solution)/shard_map/ppermute | solution.py:279
  7.1 0.7 %dynamic-slice_bitcast_fusion = s32[6]{0:T(128)S(1)} fusion(s32[4,6]{1,0:T(4,128)} %constant.38, s32[]{:T(128)S(6)} %select_n.11), kind=kLoop, calls=%fused_computation.6 | loop fusion | bytes 52 | tf_op jit(solution)/shard_map/squeeze | solution.py:284
  7.7 0.6 %pad_add_fusion.refs_0_.which_ref = s32[8]{0:T(128)} fusion(s32[6]{0:T(128)S(1)} %dynamic-slice_bitcast_fusion, s32[1]{0:T(128)} %bitcast.1, s32[1]{0:T(128)} %bitcast), kind=kLoop, calls=%fused_computation.5 | loop fusion | flops 16 | bytes 64 | tf_op jit(solution)/shard_map/concatenate | solution.py:285
  8.4 0.3 collective-permute-done.refs_4_
  8.7 0.0 copy-done.3
  8.7 0.0 copy-start.1
  8.7 0.0 copy-start.2
  8.7 7.9 %all-gather = bf16[2560,128]{1,0:T(8,128)(2,1)S(1)} all-gather(bf16[640,128]{1,0:T(8,128)(2,1)S(1)} %pad_maximum_fusion), channel_id=2, replica_groups=mesh['rows'=8,'modes'=4] {'modes'}, dimensions={0}, use_global_device_ids=true | all-gather | bytes 819200 | tf_op jit(solution)/shard_map/all_gather | solution.py:280
  16.6 0.0 copy-done.1
  16.6 0.0 copy-done.2
  16.6 2.1 %image.1 = (bf16[192,512]{1,0:T(8,128)(2,1)S(1)}, bf16[320,512]{1,0:T(8,128)(2,1)S(1)}, f32[264,128]{1,0:T(8,128)S(1)}) custom-call(s32[8]{0:T(128)} %pad_add_fusion.refs_0_.which_ref, f32[4]{0:T(128)} %refs_1_.1, s32[4]{0:T(128)} %refs_2_.1, bf16[4,640,128]{2,1,0:T(8,128)(2,1)S(1)} %bitcast.7, bf16[144,128]{1,0:T(8,128)(2,1)S(1)} %collective-permute-done.refs_4_, ...), custom_call_target="tpu_custom_call" | custom-call | tf_op jit(solution)/shard_map/image/pallas_call | solution.py:287
  18.7 0.0 copy-start
  18.7 0.2 collective-permute-start.1
  18.9 5.7 %collective-permute-done.1 = f32[264,128]{1,0:T(8,128)S(1)} collective-permute-done((f32[264,128]{1,0:T(8,128)S(1)}, f32[264,128]{1,0:T(8,128)S(1)}, u32[]{:S(2)}, u32[]{:S(2)}) %collective-permute-start.1) | collective-permute-done | bytes 135200 | tf_op jit(solution)/shard_map/ppermute | solution.py:236
  24.6 0.1 collective-permute-start.2
  24.7 5.0 %collective-permute-done.2 = f32[264,128]{1,0:T(8,128)S(1)} collective-permute-done((f32[264,128]{1,0:T(8,128)S(1)}, f32[264,128]{1,0:T(8,128)S(1)}, u32[]{:S(2)}, u32[]{:S(2)}) %collective-permute-start.2) | collective-permute-done | bytes 135200 | tf_op jit(solution)/shard_map/ppermute | solution.py:236
  29.8 2.9 %collective-permute-start.3 = (f32[264,128]{1,0:T(8,128)S(1)}, f32[264,128]{1,0:T(8,128)S(1)}, u32[]{:S(2)}, u32[]{:S(2)}) collective-permute-start(f32[264,128]{1,0:T(8,128)S(1)} %add.22), channel_id=1, source_target_pairs={{0,16},{4,20},{8,24},{12,28},{16,0},{20,4},{24,8},{28,12},{1,17},{... | collective-permute-start | bytes 405512 | tf_op jit(solution)/shard_map/ppermute | solution.py:236
  32.7 5.9 %collective-permute-done.3 = f32[264,128]{1,0:T(8,128)S(1)} collective-permute-done((f32[264,128]{1,0:T(8,128)S(1)}, f32[264,128]{1,0:T(8,128)S(1)}, u32[]{:S(2)}, u32[]{:S(2)}) %collective-permute-start.3) | collective-permute-done | bytes 135200 | tf_op jit(solution)/shard_map/ppermute | solution.py:236
  38.6 0.6 collective-permute-start.7
  39.2 1.3 %collective-permute-start.4 = (bf16[320,512]{1,0:T(8,128)(2,1)S(1)}, bf16[320,512]{1,0:T(8,128)(2,1)S(1)}, u32[]{:S(2)}, u32[]{:S(2)}) collective-permute-start(bf16[320,512]{1,0:T(8,128)(2,1)S(1)} %get-tuple-element.14.second), channel_id=1, source_target_pairs={{0,4},{4,8},{8,12},{12,16},{16,20},{20,24},{24,28},{28,0},{1,5},{5... | collective-permute-start | bytes 983048 | tf_op jit(solution)/shard_map/ppermute | solution.py:308
  40.5 0.0 copy-start.4
  40.5 0.0 collective-permute-start.6
  40.5 3.5 %collective-permute-start.5 = (bf16[192,512]{1,0:T(8,128)(2,1)S(1)}, bf16[192,512]{1,0:T(8,128)(2,1)S(1)}, u32[]{:S(2)}, u32[]{:S(2)}) collective-permute-start(bf16[192,512]{1,0:T(8,128)(2,1)S(1)} %get-tuple-element.15.first), channel_id=1, source_target_pairs={{4,0},{8,4},{12,8},{16,12},{20,16},{24,20},{28,24},{0,28},{5,1},{9... | collective-permute-start | bytes 589832 | tf_op jit(solution)/shard_map/ppermute | solution.py:309
  43.9 0.0 collective-permute-done.7.across
  43.9 0.2 collective-permute-start.8
  44.2 0.0 copy-done.4
  44.2 0.7 %reshape.14.blocks_ref = s32[8]{0:T(128)} reshape(s32[2,4]{1,0:T(2,128)S(1)} %and_select_fusion) | data formatting | bytes 64 | tf_op jit(solution)/shard_map/reshape | solution.py:327
  44.8 0.0 collective-permute-done.6.beside
  44.8 0.5 collective-permute-done.8.opposite
  45.3 14.5 %factor.1.inverse = bf16[128,512]{1,0:T(8,128)(2,1)S(1)} custom-call(s32[8]{0:T(128)} %pad_add_fusion.refs_0_.which_ref, f32[264,128]{1,0:T(8,128)S(1)} %add.23.share, f32[264,128]{1,0:T(8,128)S(1)} %collective-permute-done.6.beside, f32[264,128]{1,0:T(8,128)S(1)} %collective-permute-done.7.across, f32[264,128]{1,0:T(8,128)S(1)} %collective-permute-done.8.opposite), custom_call_target="tpu_custom_call" | custom-call | tf_op jit(solution)/shard_map/factor/pallas_call | solution.py:312
  59.8 0.0 collective-permute-done.5.high
  59.9 0.0 collective-permute-done.4.low
  59.9 0.0 copy-done
  59.9 2.2 %project.1 = bf16[2,128,512]{2,1,0:T(8,128)(2,1)} custom-call(s32[8]{0:T(128)} %reshape.14.blocks_ref, s32[2]{0:T(128)} %counts_ref.1, bf16[320,512]{1,0:T(8,128)(2,1)S(1)} %collective-permute-done.4.low, bf16[192,512]{1,0:T(8,128)(2,1)S(1)} %get-tuple-element.15.first, bf16[320,512]{1,0:T(8,128)(2,1)S(1)} %get-tuple-element.14.second, ...), custom_call_target="tpu_custom_call" | custom-call | tf_op jit(solution)/shard_map/project/pallas_call | solution.py:330
  (6 shorter events, 0.1 us)
Async XLA Ops:
  0.0 8.7 %copy-start.3 = (bf16[512,128]{1,0:T(8,128)(2,1)S(1)}, bf16[512,128]{1,0:T(8,128)(2,1)}, u32[]{:S(2)}) copy-start(bf16[512,128]{1,0:T(8,128)(2,1)} %slab.1) | copy-start | bytes 393220
  1.0 7.7 %collective-permute-start = (bf16[144,128]{1,0:T(8,128)(2,1)S(1)}, bf16[144,128]{1,0:T(8,128)(2,1)S(1)}, u32[]{:S(2)}, u32[]{:S(2)}) collective-permute-start(bf16[144,128]{1,0:T(8,128)(2,1)S(1)} %pack.1), channel_id=1, source_target_pairs={{4,0},{8,4},{12,8},{16,12},{20,16},{24,20},{28,24},{0,28},{5,1},{9... | collective-permute-start | bytes 110600 | tf_op jit(solution)/shard_map/ppermute | solution.py:279
  8.7 7.9 %copy-start.1 = (f32[512]{0:T(512)S(1)}, f32[512]{0:T(512)}, u32[]{:S(2)}) copy-start(f32[512]{0:T(512)} %param.11) | copy-start | bytes 6148
  8.7 7.9 %copy-start.2 = (f32[512]{0:T(512)S(1)}, f32[512]{0:T(512)}, u32[]{:S(2)}) copy-start(f32[512]{0:T(512)} %param.10) | copy-start | bytes 6148
  18.7 41.2 %copy-start = (bf16[2,512,512]{2,1,0:T(8,128)(2,1)S(1)}, bf16[2,512,512]{2,1,0:T(8,128)(2,1)}, u32[]{:S(2)}) copy-start(bf16[2,512,512]{2,1,0:T(8,128)(2,1)} %shapes.1) | copy-start | bytes 3145732
  18.7 5.9 %collective-permute-start.1 = (f32[264,128]{1,0:T(8,128)S(1)}, f32[264,128]{1,0:T(8,128)S(1)}, u32[]{:S(2)}, u32[]{:S(2)}) collective-permute-start(f32[264,128]{1,0:T(8,128)S(1)} %get-tuple-element.11), channel_id=1, source_target_pairs={{0,4},{4,0},{8,12},{12,8},{16,20},{20,16},{24,28},{28,24},{1,5},{5... | collective-permute-start | bytes 405512 | tf_op jit(solution)/shard_map/ppermute | solution.py:236
  24.6 5.1 %collective-permute-start.2 = (f32[264,128]{1,0:T(8,128)S(1)}, f32[264,128]{1,0:T(8,128)S(1)}, u32[]{:S(2)}, u32[]{:S(2)}) collective-permute-start(f32[264,128]{1,0:T(8,128)S(1)} %add.21), channel_id=1, source_target_pairs={{0,8},{4,12},{8,0},{12,4},{16,24},{20,28},{24,16},{28,20},{1,9},{5... | collective-permute-start | bytes 405512 | tf_op jit(solution)/shard_map/ppermute | solution.py:236
  29.8 8.8 %collective-permute-start.3 = (f32[264,128]{1,0:T(8,128)S(1)}, f32[264,128]{1,0:T(8,128)S(1)}, u32[]{:S(2)}, u32[]{:S(2)}) collective-permute-start(f32[264,128]{1,0:T(8,128)S(1)} %add.22), channel_id=1, source_target_pairs={{0,16},{4,20},{8,24},{12,28},{16,0},{20,4},{24,8},{28,12},{1,17},{... | collective-permute-start | bytes 405512 | tf_op jit(solution)/shard_map/ppermute | solution.py:236
  38.6 5.3 %collective-permute-start.7 = (f32[264,128]{1,0:T(8,128)S(1)}, f32[264,128]{1,0:T(8,128)S(1)}, u32[]{:S(2)}, u32[]{:S(2)}) collective-permute-start(f32[264,128]{1,0:T(8,128)S(1)} %add.23.share), channel_id=1, source_target_pairs={{0,2},{1,3},{2,0},{3,1},{4,6},{5,7},{6,4},{7,5},{8,10},{9,11},{10,... | collective-permute-start | bytes 405512 | tf_op jit(solution)/shard_map/ppermute | solution.py:236
  39.2 20.7 %collective-permute-start.4 = (bf16[320,512]{1,0:T(8,128)(2,1)S(1)}, bf16[320,512]{1,0:T(8,128)(2,1)S(1)}, u32[]{:S(2)}, u32[]{:S(2)}) collective-permute-start(bf16[320,512]{1,0:T(8,128)(2,1)S(1)} %get-tuple-element.14.second), channel_id=1, source_target_pairs={{0,4},{4,8},{8,12},{12,16},{16,20},{20,24},{24,28},{28,0},{1,5},{5... | collective-permute-start | bytes 983048 | tf_op jit(solution)/shard_map/ppermute | solution.py:308
  40.5 3.7 %copy-start.4 = (s32[2,4]{1,0:T(2,128)S(1)}, s32[2,4]{1,0:T(2,128)}, u32[]{:S(2)}) copy-start(s32[2,4]{1,0:T(2,128)} %param.14) | copy-start | bytes 100
  40.5 4.4 %collective-permute-start.6 = (f32[264,128]{1,0:T(8,128)S(1)}, f32[264,128]{1,0:T(8,128)S(1)}, u32[]{:S(2)}, u32[]{:S(2)}) collective-permute-start(f32[264,128]{1,0:T(8,128)S(1)} %add.23.share), channel_id=1, source_target_pairs={{0,1},{1,0},{2,3},{3,2},{4,5},{5,4},{6,7},{7,6},{8,9},{9,8},{10,11... | collective-permute-start | bytes 405512 | tf_op jit(solution)/shard_map/ppermute | solution.py:236
  40.5 19.4 %collective-permute-start.5 = (bf16[192,512]{1,0:T(8,128)(2,1)S(1)}, bf16[192,512]{1,0:T(8,128)(2,1)S(1)}, u32[]{:S(2)}, u32[]{:S(2)}) collective-permute-start(bf16[192,512]{1,0:T(8,128)(2,1)S(1)} %get-tuple-element.15.first), channel_id=1, source_target_pairs={{4,0},{8,4},{12,8},{16,12},{20,16},{24,20},{28,24},{0,28},{5,1},{9... | collective-permute-start | bytes 589832 | tf_op jit(solution)/shard_map/ppermute | solution.py:309
  43.9 1.4 %collective-permute-start.8 = (f32[264,128]{1,0:T(8,128)S(1)}, f32[264,128]{1,0:T(8,128)S(1)}, u32[]{:S(2)}, u32[]{:S(2)}) collective-permute-start(f32[264,128]{1,0:T(8,128)S(1)} %collective-permute-done.7.across), channel_id=1, source_target_pairs={{0,1},{1,0},{2,3},{3,2},{4,5},{5,4},{6,7},{7,6},{8,9},{9,8},{10,11... | collective-permute-start | bytes 405512 | tf_op jit(solution)/shard_map/ppermute | solution.py:236

commit v4 on v3

--- a/solution.py
+++ b/solution.py
@@ -39,8 +39,12 @@
 
 
 def dot_f32(a, b, dims=((1,), (0,))):
-    return lax.dot_general(
-        a, b, (dims, ((), ())), precision=lax.Precision.HIGHEST, preferred_element_type=f32
+    a0, a1, a2 = bf16_parts(a)
+    b0, b1, b2 = bf16_parts(b)
+    return dot(
+        jnp.concatenate([a0, a0, a1, a0, a2, a1], axis=dims[0][0]),
+        jnp.concatenate([b0, b1, b0, b2, b0, b1], axis=dims[1][0]),
+        dims,
     )
 
 
@@ -52,11 +56,17 @@
     out[size:, :] = jnp.concatenate(rows, axis=0)
 
 
-def image_kernel(scale, which_ref, coef_ref, offset_ref, gathered, packed, gain_ref, diag_ref, first, second, share, scaled, gains, diags):
+def image_kernel(scale, which_ref, coef_ref, offset_ref, *refs):
+    slabs, edges = refs[:4], refs[4:8]
+    gain_ref, diag_ref, first, second, share, gathered, scaled, gains, diags = refs[8:]
     modes = gathered.shape[0]
     size = BLOCK
     tiles = gain_ref.shape[0]
     rows = tiles * size
+    for distance in range(modes):
+        m = which_ref[0] ^ distance
+        gathered[m, 0:rows, :] = slabs[distance][...]
+        gathered[m, rows:, :] = edges[distance][0:size, :]
     split = first.shape[0]
     wide = size + 2 * BAND
     row = lax.broadcasted_iota(jnp.int32, (size, wide), 0)
@@ -68,7 +78,7 @@
     parts = bf16_parts(band)
     across_end = jnp.logical_and(which_ref[1] != 0, (row < size - BAND) != (column < size))
     last_parts = bf16_parts(jnp.where(across_end, 0.0, band))
-    tail = packed[size:, :].astype(f32)
+    tail = edges[0][size:, :].astype(f32)
     next_gain = tail[0:1, :] + tail[1:2, :] + tail[2:3, :]
     next_diag = tail[3:4, :] + tail[4:5, :] + tail[5:6, :]
     for ref, own, extra in ((gains, gain_ref, next_gain), (diags, diag_ref, next_diag)):
@@ -236,6 +246,12 @@
     return lax.ppermute(value, axis, [(i, i ^ step) for i in range(lax.axis_size(axis))])
 
 
+def from_modes(value):
+    across = exchange(value, "modes", 2)
+    beside = exchange(value, "modes", 1)
+    return value, beside, across, exchange(across, "modes", 1)
+
+
 def sum_over_rows(value):
     step = 1
     while step < lax.axis_size("rows"):
@@ -276,8 +292,9 @@
         out_specs=VMEM,
         name="pack",
     )(mode_slab, mass_gain.reshape(per_dev, BLOCK), mass_diag.reshape(per_dev, BLOCK))
-    packed = lax.ppermute(packed, "rows", back)
-    gathered = lax.all_gather(jnp.concatenate([mode_slab, packed[:BLOCK, :]], axis=0), "modes", axis=0)
+    edge = lax.ppermute(packed, "rows", back)
+    slabs = from_modes(mode_slab)
+    edges = from_modes(edge)
 
     mode_index = lax.axis_index("modes")
     is_last = lax.axis_index("rows") == row_devices - 1
@@ -291,15 +308,16 @@
             pltpu.VMEM((rim_rows + BAND, order), bf16),
             pltpu.VMEM((2 * BLOCK + 8, BLOCK), f32),
         ),
-        in_specs=[SMEM, SMEM, SMEM, VMEM, VMEM, VMEM, VMEM],
+        in_specs=[SMEM, SMEM, SMEM] + [VMEM] * 10,
         out_specs=(VMEM, VMEM, VMEM),
         scratch_shapes=[
+            pltpu.VMEM((modes, extended, BLOCK), bf16),
             pltpu.VMEM((extended, order), bf16),
             pltpu.VMEM((extended, BLOCK), f32),
             pltpu.VMEM((extended, BLOCK), f32),
         ],
         name="image",
-    )(which, band_coef, band_offsets, near(gathered), near(packed), gain_rows, diag_rows)
+    )(which, band_coef, band_offsets, *map(near, slabs), *map(near, edges), gain_rows, diag_rows)
 
     share = sum_over_rows(share)
     share, one, two = lax.optimization_barrier((share, first, second))

time: 62.3 us -> 59.5 us (0.955)
  blocking collectives: 7.89 us -> 0 us
  waiting for transfers between devices: 17.4 us -> 21.2 us
  starting transfers between devices: 14.9 us -> 17.4 us
  Pallas kernels: 19.8 us -> 18.8 us
    all_gather x1 -> x0, blocking collectives: 7.89 us -> none  [local(): lax.all_gather(jnp.concatenate([mode_slab, packed[:BLOCK, :]], axis=0), '...]
    ppermute x6 -> x12, starting transfers between devices: 4.1 us -> 8.03 us  [exchange(): lax.ppermute(value, axis, [(i, i ^ step) for i in range(lax.axis_size(axi...]
    ppermute x6 -> x12, waiting for transfers between devices: 17 us -> 19.5 us  [exchange(): lax.ppermute(value, axis, [(i, i ^ step) for i in range(lax.axis_size(axi...]
    ppermute x1, starting transfers between devices: 6.06 us -> 4.61 us  [local(): edge = lax.ppermute(packed, 'rows', back)]
    ppermute x1, waiting for transfers between devices: 0.33 us -> 1.63 us  [local(): edge = lax.ppermute(packed, 'rows', back)]
    pallas_call x1, Pallas kernels: 14.5 us -> 13.6 us  [local(): pl.pallas_call(factor_kernel, out_shape=pltpu.VMEM((BLOCK, order), bf16),...]
  transfers between devices with their start and end apart: 9 -> 15, of which waited for: 5 -> 7; matrix products, arithmetic and copies ran while one was open for 3% -> 3% of each run, Pallas kernels for 23% -> 24%
where the time goes in v4:
time: 59.5 us; the launch traced here: 59.3 us
  waiting for transfers between devices  21.2 us (36%)
  Pallas kernels  18.8 us (32%)
  starting transfers between devices  17.4 us (29%)
  local copies, waits for them, and re-layouts  1.32 us (2%)
  other arithmetic  0.65 us (1%)
    ppermute x12, waiting for transfers between devices, exchange(): lax.ppermute(value, axis, [(i, i ^ step) for i in range(lax.axis_size(axi...  19.5 us
    pallas_call x1, Pallas kernels, local(): pl.pallas_call(factor_kernel, out_shape=pltpu.VMEM((BLOCK, order), bf16),...  13.6 us
    ppermute x12, starting transfers between devices, exchange(): lax.ppermute(value, axis, [(i, i ^ step) for i in range(lax.axis_size(axi...  8.03 us
    ppermute x1, starting transfers between devices, local(): edge = lax.ppermute(packed, 'rows', back)  4.61 us
    ppermute x1, starting transfers between devices, local(): rim_high = lax.ppermute(one, 'rows', back)  3.66 us
    pallas_call x1, Pallas kernels, local(): pl.pallas_call(project_kernel, out_shape=jax.ShapeDtypeStruct((owned, mod...  2.18 us
    pallas_call x1, Pallas kernels, local(): pl.pallas_call(lambda *refs: image_kernel(0.5 / total_rows, *refs), out_s...  2.06 us
    ppermute x1, waiting for transfers between devices, local(): edge = lax.ppermute(packed, 'rows', back)  1.63 us
  transfers between devices with their start and end apart: 15, of which 7 were waited for; matrix products, arithmetic and copies ran while one was open for 3% of the time, Pallas kernels for 24%

profile of v4, /device:TPU:0, one launch (start us, length us, event | category | flops | bytes accessed | tf_op | source)
XLA Modules:
  0.0 59.3 jit_solution(16084552728082593146)
XLA Ops:
  0.0 0.0 copy-start.1
  0.0 2.9 %collective-permute-start.1 = (bf16[512,128]{1,0:T(8,128)(2,1)}, bf16[512,128]{1,0:T(8,128)(2,1)S(1)}, u32[]{:S(2)}, u32[]{:S(2)}) collective-permute-start(bf16[512,128]{1,0:T(8,128)(2,1)} %refs_3_.1), channel_id=1, source_target_pairs={{0,2},{1,3},{2,0},{3,1},{4,6},{5,7},{6,4},{7,5},{8,10},{9,11},{10,... | collective-permute-start | bytes 393224 | tf_op jit(solution)/shard_map/ppermute | solution.py:246
  2.9 1.0 %pack.1 = bf16[144,128]{1,0:T(8,128)(2,1)S(1)} custom-call(bf16[512,128]{1,0:T(8,128)(2,1)} %refs_3_.1, f32[4,128]{1,0:T(4,128)} %bitcast.6, f32[4,128]{1,0:T(4,128)} %bitcast.8), custom_call_target="tpu_custom_call" | custom-call | tf_op jit(solution)/shard_map/pack/pallas_call | solution.py:288
  3.9 4.6 %collective-permute-start.3 = (bf16[144,128]{1,0:T(8,128)(2,1)S(1)}, bf16[144,128]{1,0:T(8,128)(2,1)S(1)}, u32[]{:S(2)}, u32[]{:S(2)}) collective-permute-start(bf16[144,128]{1,0:T(8,128)(2,1)S(1)} %pack.1), channel_id=1, source_target_pairs={{4,0},{8,4},{12,8},{16,12},{20,16},{24,20},{28,24},{0,28},{5,1},{9... | collective-permute-start | bytes 110600 | tf_op jit(solution)/shard_map/ppermute | solution.py:295
  8.5 0.0 copy-done.1
  8.5 0.0 collective-permute-start
  8.5 1.6 %collective-permute-done.3.refs_7_ = bf16[144,128]{1,0:T(8,128)(2,1)S(1)} collective-permute-done((bf16[144,128]{1,0:T(8,128)(2,1)S(1)}, bf16[144,128]{1,0:T(8,128)(2,1)S(1)}, u32[]{:S(2)}, u32[]{:S(2)}) %collective-permute-start.3) | collective-permute-done | bytes 36896 | tf_op jit(solution)/shard_map/ppermute | solution.py:295
  10.1 0.5 collective-permute-start.5
  10.7 0.0 collective-permute-done.1.refs_5_
  10.7 0.0 collective-permute-start.2
  10.7 0.7 %dynamic-slice_bitcast_fusion = s32[6]{0:T(128)S(1)} fusion(s32[4,6]{1,0:T(4,128)} %constant.38, s32[]{:T(128)S(6)} %select_n.11), kind=kLoop, calls=%fused_computation.5 | loop fusion | bytes 52 | tf_op jit(solution)/shard_map/squeeze | solution.py:301
  11.4 0.5 collective-permute-start.4
  11.9 2.2 %collective-permute-done.5.refs_9_ = bf16[144,128]{1,0:T(8,128)(2,1)S(1)} collective-permute-done((bf16[144,128]{1,0:T(8,128)(2,1)S(1)}, bf16[144,128]{1,0:T(8,128)(2,1)S(1)}, u32[]{:S(2)}, u32[]{:S(2)}) %collective-permute-start.5) | collective-permute-done | bytes 36896 | tf_op jit(solution)/shard_map/ppermute | solution.py:246
  14.1 0.0 collective-permute-start.6
  14.1 0.0 copy-start.3
  14.1 0.0 copy-start.2
  14.1 0.6 pad_add_fusion.refs_0_.which_ref
  14.7 0.0 collective-permute-done.4.refs_8_
  14.7 0.6 %collective-permute-done.6.refs_10_ = bf16[144,128]{1,0:T(8,128)(2,1)S(1)} collective-permute-done((bf16[144,128]{1,0:T(8,128)(2,1)S(1)}, bf16[144,128]{1,0:T(8,128)(2,1)S(1)}, u32[]{:S(2)}, u32[]{:S(2)}) %collective-permute-start.6) | collective-permute-done | bytes 36896 | tf_op jit(solution)/shard_map/ppermute | solution.py:246
  15.3 0.0 collective-permute-done.refs_4_
  15.3 0.0 collective-permute-done.2.refs_6_
  15.3 0.0 copy-done.3
  15.3 0.0 copy-done.2
  15.3 2.1 %image.1 = (bf16[192,512]{1,0:T(8,128)(2,1)S(1)}, bf16[320,512]{1,0:T(8,128)(2,1)S(1)}, f32[264,128]{1,0:T(8,128)S(1)}) custom-call(s32[8]{0:T(128)} %pad_add_fusion.refs_0_.which_ref, f32[4]{0:T(128)} %refs_1_.1, s32[4]{0:T(128)} %refs_2_.1, bf16[512,128]{1,0:T(8,128)(2,1)S(1)} %copy-done.1, bf16[512,128]{1,0:T(8,128)(2,1)S(1)} %collective-permute-done.refs_4_, ...), custom_call_target="tpu_custom_call" | custom-call | tf_op jit(solution)/shard_map/image/pallas_call | solution.py:304
  17.4 0.0 copy-start
  17.4 0.3 collective-permute-start.7
  17.7 5.5 %collective-permute-done.7 = f32[264,128]{1,0:T(8,128)S(1)} collective-permute-done((f32[264,128]{1,0:T(8,128)S(1)}, f32[264,128]{1,0:T(8,128)S(1)}, u32[]{:S(2)}, u32[]{:S(2)}) %collective-permute-start.7) | collective-permute-done | bytes 135200 | tf_op jit(solution)/shard_map/ppermute | solution.py:246
  23.2 0.1 collective-permute-start.8
  23.2 5.0 %collective-permute-done.8 = f32[264,128]{1,0:T(8,128)S(1)} collective-permute-done((f32[264,128]{1,0:T(8,128)S(1)}, f32[264,128]{1,0:T(8,128)S(1)}, u32[]{:S(2)}, u32[]{:S(2)}) %collective-permute-start.8) | collective-permute-done | bytes 135200 | tf_op jit(solution)/shard_map/ppermute | solution.py:246
  28.3 2.8 %collective-permute-start.9 = (f32[264,128]{1,0:T(8,128)S(1)}, f32[264,128]{1,0:T(8,128)S(1)}, u32[]{:S(2)}, u32[]{:S(2)}) collective-permute-start(f32[264,128]{1,0:T(8,128)S(1)} %add.22), channel_id=1, source_target_pairs={{0,16},{4,20},{8,24},{12,28},{16,0},{20,4},{24,8},{28,12},{1,17},{... | collective-permute-start | bytes 405512 | tf_op jit(solution)/shard_map/ppermute | solution.py:246
  31.1 5.7 %collective-permute-done.9 = f32[264,128]{1,0:T(8,128)S(1)} collective-permute-done((f32[264,128]{1,0:T(8,128)S(1)}, f32[264,128]{1,0:T(8,128)S(1)}, u32[]{:S(2)}, u32[]{:S(2)}) %collective-permute-start.9) | collective-permute-done | bytes 135200 | tf_op jit(solution)/shard_map/ppermute | solution.py:246
  36.8 0.6 %collective-permute-start.13 = (f32[264,128]{1,0:T(8,128)S(1)}, f32[264,128]{1,0:T(8,128)S(1)}, u32[]{:S(2)}, u32[]{:S(2)}) collective-permute-start(f32[264,128]{1,0:T(8,128)S(1)} %add.23.share), channel_id=1, source_target_pairs={{0,2},{1,3},{2,0},{3,1},{4,6},{5,7},{6,4},{7,5},{8,10},{9,11},{10,... | collective-permute-start | bytes 405512 | tf_op jit(solution)/shard_map/ppermute | solution.py:246
  37.5 1.1 %collective-permute-start.10 = (bf16[320,512]{1,0:T(8,128)(2,1)S(1)}, bf16[320,512]{1,0:T(8,128)(2,1)S(1)}, u32[]{:S(2)}, u32[]{:S(2)}) collective-permute-start(bf16[320,512]{1,0:T(8,128)(2,1)S(1)} %get-tuple-element.14.second), channel_id=1, source_target_pairs={{0,4},{4,8},{8,12},{12,16},{16,20},{20,24},{24,28},{28,0},{1,5},{5... | collective-permute-start | bytes 983048 | tf_op jit(solution)/shard_map/ppermute | solution.py:326
  38.5 0.0 copy-start.4
  38.5 0.0 collective-permute-start.12
  38.5 3.7 %collective-permute-start.11 = (bf16[192,512]{1,0:T(8,128)(2,1)S(1)}, bf16[192,512]{1,0:T(8,128)(2,1)S(1)}, u32[]{:S(2)}, u32[]{:S(2)}) collective-permute-start(bf16[192,512]{1,0:T(8,128)(2,1)S(1)} %get-tuple-element.15.first), channel_id=1, source_target_pairs={{4,0},{8,4},{12,8},{16,12},{20,16},{24,20},{28,24},{0,28},{5,1},{9... | collective-permute-start | bytes 589832 | tf_op jit(solution)/shard_map/ppermute | solution.py:327
  42.2 0.0 collective-permute-done.13.across
  42.2 0.2 collective-permute-start.14
  42.4 0.0 copy-done.4
  42.4 0.6 %reshape.14.blocks_ref = s32[8]{0:T(128)} reshape(s32[2,4]{1,0:T(2,128)S(1)} %and_select_fusion) | data formatting | bytes 64 | tf_op jit(solution)/shard_map/reshape | solution.py:345
  43.0 0.0 collective-permute-done.12.beside
  43.0 0.5 collective-permute-done.14.opposite
  43.5 13.6 %factor.1.inverse = bf16[128,512]{1,0:T(8,128)(2,1)S(1)} custom-call(s32[8]{0:T(128)} %pad_add_fusion.refs_0_.which_ref, f32[264,128]{1,0:T(8,128)S(1)} %add.23.share, f32[264,128]{1,0:T(8,128)S(1)} %collective-permute-done.12.beside, f32[264,128]{1,0:T(8,128)S(1)} %collective-permute-done.13.across, f32[264,128]{1,0:T(8,128)S(1)} %collective-permute-done.14.opposite), custom_call_target="tpu_custom_call" | custom-call | tf_op jit(solution)/shard_map/factor/pallas_call | solution.py:330
  57.1 0.0 collective-permute-done.11.high
  57.1 0.0 collective-permute-done.10.low
  57.1 0.0 copy-done
  57.1 2.2 %project.1 = bf16[2,128,512]{2,1,0:T(8,128)(2,1)} custom-call(s32[8]{0:T(128)} %reshape.14.blocks_ref, s32[2]{0:T(128)} %counts_ref.1, bf16[320,512]{1,0:T(8,128)(2,1)S(1)} %collective-permute-done.10.low, bf16[192,512]{1,0:T(8,128)(2,1)S(1)} %get-tuple-element.15.first, bf16[320,512]{1,0:T(8,128)(2,1)S(1)} %get-tuple-element.14.second, ...), custom_call_target="tpu_custom_call" | custom-call | tf_op jit(solution)/shard_map/project/pallas_call | solution.py:348
  (4 shorter events, 0.1 us)
Async XLA Ops:
  0.0 8.5 %copy-start.1 = (bf16[512,128]{1,0:T(8,128)(2,1)S(1)}, bf16[512,128]{1,0:T(8,128)(2,1)}, u32[]{:S(2)}) copy-start(bf16[512,128]{1,0:T(8,128)(2,1)} %refs_3_.1) | copy-start | bytes 393220
  0.0 10.7 %collective-permute-start.1 = (bf16[512,128]{1,0:T(8,128)(2,1)}, bf16[512,128]{1,0:T(8,128)(2,1)S(1)}, u32[]{:S(2)}, u32[]{:S(2)}) collective-permute-start(bf16[512,128]{1,0:T(8,128)(2,1)} %refs_3_.1), channel_id=1, source_target_pairs={{0,2},{1,3},{2,0},{3,1},{4,6},{5,7},{6,4},{7,5},{8,10},{9,11},{10,... | collective-permute-start | bytes 393224 | tf_op jit(solution)/shard_map/ppermute | solution.py:246
  3.9 6.2 %collective-permute-start.3 = (bf16[144,128]{1,0:T(8,128)(2,1)S(1)}, bf16[144,128]{1,0:T(8,128)(2,1)S(1)}, u32[]{:S(2)}, u32[]{:S(2)}) collective-permute-start(bf16[144,128]{1,0:T(8,128)(2,1)S(1)} %pack.1), channel_id=1, source_target_pairs={{4,0},{8,4},{12,8},{16,12},{20,16},{24,20},{28,24},{0,28},{5,1},{9... | collective-permute-start | bytes 110600 | tf_op jit(solution)/shard_map/ppermute | solution.py:295
  8.5 6.8 %collective-permute-start = (bf16[512,128]{1,0:T(8,128)(2,1)S(1)}, bf16[512,128]{1,0:T(8,128)(2,1)S(1)}, u32[]{:S(2)}, u32[]{:S(2)}) collective-permute-start(bf16[512,128]{1,0:T(8,128)(2,1)S(1)} %copy-done.1), channel_id=1, source_target_pairs={{0,1},{1,0},{2,3},{3,2},{4,5},{5,4},{6,7},{7,6},{8,9},{9,8},{10,11... | collective-permute-start | bytes 393224 | tf_op jit(solution)/shard_map/ppermute | solution.py:246
  10.1 4.0 %collective-permute-start.5 = (bf16[144,128]{1,0:T(8,128)(2,1)S(1)}, bf16[144,128]{1,0:T(8,128)(2,1)S(1)}, u32[]{:S(2)}, u32[]{:S(2)}) collective-permute-start(bf16[144,128]{1,0:T(8,128)(2,1)S(1)} %collective-permute-done.3.refs_7_), channel_id=1, source_target_pairs={{0,2},{1,3},{2,0},{3,1},{4,6},{5,7},{6,4},{7,5},{8,10},{9,11},{10,... | collective-permute-start | bytes 110600 | tf_op jit(solution)/shard_map/ppermute | solution.py:246
  10.7 4.6 %collective-permute-start.2 = (bf16[512,128]{1,0:T(8,128)(2,1)S(1)}, bf16[512,128]{1,0:T(8,128)(2,1)S(1)}, u32[]{:S(2)}, u32[]{:S(2)}) collective-permute-start(bf16[512,128]{1,0:T(8,128)(2,1)S(1)} %collective-permute-done.1.refs_5_), channel_id=1, source_target_pairs={{0,1},{1,0},{2,3},{3,2},{4,5},{5,4},{6,7},{7,6},{8,9},{9,8},{10,11... | collective-permute-start | bytes 393224 | tf_op jit(solution)/shard_map/ppermute | solution.py:246
  11.4 3.3 %collective-permute-start.4 = (bf16[144,128]{1,0:T(8,128)(2,1)S(1)}, bf16[144,128]{1,0:T(8,128)(2,1)S(1)}, u32[]{:S(2)}, u32[]{:S(2)}) collective-permute-start(bf16[144,128]{1,0:T(8,128)(2,1)S(1)} %collective-permute-done.3.refs_7_), channel_id=1, source_target_pairs={{0,1},{1,0},{2,3},{3,2},{4,5},{5,4},{6,7},{7,6},{8,9},{9,8},{10,11... | collective-permute-start | bytes 110600 | tf_op jit(solution)/shard_map/ppermute | solution.py:246
  14.1 1.2 %collective-permute-start.6 = (bf16[144,128]{1,0:T(8,128)(2,1)S(1)}, bf16[144,128]{1,0:T(8,128)(2,1)S(1)}, u32[]{:S(2)}, u32[]{:S(2)}) collective-permute-start(bf16[144,128]{1,0:T(8,128)(2,1)S(1)} %collective-permute-done.5.refs_9_), channel_id=1, source_target_pairs={{0,1},{1,0},{2,3},{3,2},{4,5},{5,4},{6,7},{7,6},{8,9},{9,8},{10,11... | collective-permute-start | bytes 110600 | tf_op jit(solution)/shard_map/ppermute | solution.py:246
  14.1 1.2 %copy-start.3 = (f32[512]{0:T(512)S(1)}, f32[512]{0:T(512)}, u32[]{:S(2)}) copy-start(f32[512]{0:T(512)} %param.10) | copy-start | bytes 6148
  14.1 1.2 %copy-start.2 = (f32[512]{0:T(512)S(1)}, f32[512]{0:T(512)}, u32[]{:S(2)}) copy-start(f32[512]{0:T(512)} %param.11) | copy-start | bytes 6148
  17.4 39.7 %copy-start = (bf16[2,512,512]{2,1,0:T(8,128)(2,1)S(1)}, bf16[2,512,512]{2,1,0:T(8,128)(2,1)}, u32[]{:S(2)}) copy-start(bf16[2,512,512]{2,1,0:T(8,128)(2,1)} %shapes.1) | copy-start | bytes 3145732
  17.4 5.7 %collective-permute-start.7 = (f32[264,128]{1,0:T(8,128)S(1)}, f32[264,128]{1,0:T(8,128)S(1)}, u32[]{:S(2)}, u32[]{:S(2)}) collective-permute-start(f32[264,128]{1,0:T(8,128)S(1)} %get-tuple-element.11), channel_id=1, source_target_pairs={{0,4},{4,0},{8,12},{12,8},{16,20},{20,16},{24,28},{28,24},{1,5},{5... | collective-permute-start | bytes 405512 | tf_op jit(solution)/shard_map/ppermute | solution.py:246
  23.2 5.1 %collective-permute-start.8 = (f32[264,128]{1,0:T(8,128)S(1)}, f32[264,128]{1,0:T(8,128)S(1)}, u32[]{:S(2)}, u32[]{:S(2)}) collective-permute-start(f32[264,128]{1,0:T(8,128)S(1)} %add.21), channel_id=1, source_target_pairs={{0,8},{4,12},{8,0},{12,4},{16,24},{20,28},{24,16},{28,20},{1,9},{5... | collective-permute-start | bytes 405512 | tf_op jit(solution)/shard_map/ppermute | solution.py:246
  28.3 8.5 %collective-permute-start.9 = (f32[264,128]{1,0:T(8,128)S(1)}, f32[264,128]{1,0:T(8,128)S(1)}, u32[]{:S(2)}, u32[]{:S(2)}) collective-permute-start(f32[264,128]{1,0:T(8,128)S(1)} %add.22), channel_id=1, source_target_pairs={{0,16},{4,20},{8,24},{12,28},{16,0},{20,4},{24,8},{28,12},{1,17},{... | collective-permute-start | bytes 405512 | tf_op jit(solution)/shard_map/ppermute | solution.py:246
  36.8 5.4 %collective-permute-start.13 = (f32[264,128]{1,0:T(8,128)S(1)}, f32[264,128]{1,0:T(8,128)S(1)}, u32[]{:S(2)}, u32[]{:S(2)}) collective-permute-start(f32[264,128]{1,0:T(8,128)S(1)} %add.23.share), channel_id=1, source_target_pairs={{0,2},{1,3},{2,0},{3,1},{4,6},{5,7},{6,4},{7,5},{8,10},{9,11},{10,... | collective-permute-start | bytes 405512 | tf_op jit(solution)/shard_map/ppermute | solution.py:246
  37.5 19.7 %collective-permute-start.10 = (bf16[320,512]{1,0:T(8,128)(2,1)S(1)}, bf16[320,512]{1,0:T(8,128)(2,1)S(1)}, u32[]{:S(2)}, u32[]{:S(2)}) collective-permute-start(bf16[320,512]{1,0:T(8,128)(2,1)S(1)} %get-tuple-element.14.second), channel_id=1, source_target_pairs={{0,4},{4,8},{8,12},{12,16},{16,20},{20,24},{24,28},{28,0},{1,5},{5... | collective-permute-start | bytes 983048 | tf_op jit(solution)/shard_map/ppermute | solution.py:326
  38.5 3.9 %copy-start.4 = (s32[2,4]{1,0:T(2,128)S(1)}, s32[2,4]{1,0:T(2,128)}, u32[]{:S(2)}) copy-start(s32[2,4]{1,0:T(2,128)} %param.14) | copy-start | bytes 100
  38.5 4.5 %collective-permute-start.12 = (f32[264,128]{1,0:T(8,128)S(1)}, f32[264,128]{1,0:T(8,128)S(1)}, u32[]{:S(2)}, u32[]{:S(2)}) collective-permute-start(f32[264,128]{1,0:T(8,128)S(1)} %add.23.share), channel_id=1, source_target_pairs={{0,1},{1,0},{2,3},{3,2},{4,5},{5,4},{6,7},{7,6},{8,9},{9,8},{10,11... | collective-permute-start | bytes 405512 | tf_op jit(solution)/shard_map/ppermute | solution.py:246
  38.5 18.6 %collective-permute-start.11 = (bf16[192,512]{1,0:T(8,128)(2,1)S(1)}, bf16[192,512]{1,0:T(8,128)(2,1)S(1)}, u32[]{:S(2)}, u32[]{:S(2)}) collective-permute-start(bf16[192,512]{1,0:T(8,128)(2,1)S(1)} %get-tuple-element.15.first), channel_id=1, source_target_pairs={{4,0},{8,4},{12,8},{16,12},{20,16},{24,20},{28,24},{0,28},{5,1},{9... | collective-permute-start | bytes 589832 | tf_op jit(solution)/shard_map/ppermute | solution.py:327
  42.2 1.4 %collective-permute-start.14 = (f32[264,128]{1,0:T(8,128)S(1)}, f32[264,128]{1,0:T(8,128)S(1)}, u32[]{:S(2)}, u32[]{:S(2)}) collective-permute-start(f32[264,128]{1,0:T(8,128)S(1)} %collective-permute-done.13.across), channel_id=1, source_target_pairs={{0,1},{1,0},{2,3},{3,2},{4,5},{5,4},{6,7},{7,6},{8,9},{9,8},{10,11... | collective-permute-start | bytes 405512 | tf_op jit(solution)/shard_map/ppermute | solution.py:246

commit v5 on v4

--- a/solution.py
+++ b/solution.py
@@ -294,7 +294,7 @@
     )(mode_slab, mass_gain.reshape(per_dev, BLOCK), mass_diag.reshape(per_dev, BLOCK))
     edge = lax.ppermute(packed, "rows", back)
     slabs = from_modes(mode_slab)
-    edges = from_modes(edge)
+    edges = [edge] + [exchange(edge, "modes", d) for d in (1, 2, 3)]
 
     mode_index = lax.axis_index("modes")
     is_last = lax.axis_index("rows") == row_devices - 1

time: 59.5 us -> 58.8 us (0.988)
  waiting for transfers between devices: 21.2 us -> 19 us
  starting transfers between devices: 17.4 us -> 18.8 us
    ppermute x12, starting transfers between devices: 8.03 us -> 9.47 us  [exchange(): lax.ppermute(value, axis, [(i, i ^ step) for i in range(lax.axis_size(axi...]
    ppermute x12, waiting for transfers between devices: 19.5 us -> 18.2 us  [exchange(): lax.ppermute(value, axis, [(i, i ^ step) for i in range(lax.axis_size(axi...]
    ppermute x1, waiting for transfers between devices: 1.63 us -> 0.73 us  [local(): edge = lax.ppermute(packed, 'rows', back)]
  transfers between devices with their start and end apart: 15 -> 15, of which waited for: 7 -> 7; matrix products, arithmetic and copies ran while one was open for 3% -> 3% of each run, Pallas kernels for 24% -> 25%
where the time goes in v5:
time: 58.8 us; the launch traced here: 58.6 us
  waiting for transfers between devices  19 us (32%)
  starting transfers between devices  18.8 us (32%)
  Pallas kernels  18.7 us (32%)
  local copies, waits for them, and re-layouts  1.31 us (2%)
  other arithmetic  0.65 us (1%)
    ppermute x12, waiting for transfers between devices, exchange(): lax.ppermute(value, axis, [(i, i ^ step) for i in range(lax.axis_size(axi...  18.2 us
    pallas_call x1, Pallas kernels, local(): pl.pallas_call(factor_kernel, out_shape=pltpu.VMEM((BLOCK, order), bf16),...  13.6 us
    ppermute x12, starting transfers between devices, exchange(): lax.ppermute(value, axis, [(i, i ^ step) for i in range(lax.axis_size(axi...  9.47 us
    ppermute x1, starting transfers between devices, local(): edge = lax.ppermute(packed, 'rows', back)  4.61 us
    ppermute x1, starting transfers between devices, local(): rim_high = lax.ppermute(one, 'rows', back)  3.94 us
    pallas_call x1, Pallas kernels, local(): pl.pallas_call(project_kernel, out_shape=jax.ShapeDtypeStruct((owned, mod...  2.17 us
    pallas_call x1, Pallas kernels, local(): pl.pallas_call(lambda *refs: image_kernel(0.5 / total_rows, *refs), out_s...  2.06 us
  transfers between devices with their start and end apart: 15, of which 7 were waited for; matrix products, arithmetic and copies ran while one was open for 3% of the time, Pallas kernels for 25%

profile of v5, /device:TPU:0, one launch (start us, length us, event | category | flops | bytes accessed | tf_op | source)
XLA Modules:
  0.0 58.6 jit_solution(11109901634575477815)
XLA Ops:
  0.0 0.0 copy-start.1
  0.0 2.9 %collective-permute-start.1 = (bf16[512,128]{1,0:T(8,128)(2,1)}, bf16[512,128]{1,0:T(8,128)(2,1)S(1)}, u32[]{:S(2)}, u32[]{:S(2)}) collective-permute-start(bf16[512,128]{1,0:T(8,128)(2,1)} %refs_3_.1), channel_id=1, source_target_pairs={{0,2},{1,3},{2,0},{3,1},{4,6},{5,7},{6,4},{7,5},{8,10},{9,11},{10,... | collective-permute-start | bytes 393224 | tf_op jit(solution)/shard_map/ppermute | solution.py:246
  2.9 0.0 collective-permute-start
  2.9 1.0 %pack.1 = bf16[144,128]{1,0:T(8,128)(2,1)S(1)} custom-call(bf16[512,128]{1,0:T(8,128)(2,1)} %refs_3_.1, f32[4,128]{1,0:T(4,128)} %bitcast.6, f32[4,128]{1,0:T(4,128)} %bitcast.8), custom_call_target="tpu_custom_call" | custom-call | tf_op jit(solution)/shard_map/pack/pallas_call | solution.py:288
  3.9 4.6 %collective-permute-start.3 = (bf16[144,128]{1,0:T(8,128)(2,1)S(1)}, bf16[144,128]{1,0:T(8,128)(2,1)S(1)}, u32[]{:S(2)}, u32[]{:S(2)}) collective-permute-start(bf16[144,128]{1,0:T(8,128)(2,1)S(1)} %pack.1), channel_id=1, source_target_pairs={{4,0},{8,4},{12,8},{16,12},{20,16},{24,20},{28,24},{0,28},{5,1},{9... | collective-permute-start | bytes 110600 | tf_op jit(solution)/shard_map/ppermute | solution.py:295
  8.5 0.0 collective-permute-done.1.refs_5_
  8.5 0.2 collective-permute-start.2
  8.7 0.7 %dynamic-slice_bitcast_fusion = s32[6]{0:T(128)S(1)} fusion(s32[4,6]{1,0:T(4,128)} %constant.38, s32[]{:T(128)S(6)} %select_n.11), kind=kLoop, calls=%fused_computation.5 | loop fusion | bytes 52 | tf_op jit(solution)/shard_map/squeeze | solution.py:301
  9.4 0.7 %collective-permute-done.3.refs_7_ = bf16[144,128]{1,0:T(8,128)(2,1)S(1)} collective-permute-done((bf16[144,128]{1,0:T(8,128)(2,1)S(1)}, bf16[144,128]{1,0:T(8,128)(2,1)S(1)}, u32[]{:S(2)}, u32[]{:S(2)}) %collective-permute-start.3) | collective-permute-done | bytes 36896 | tf_op jit(solution)/shard_map/ppermute | solution.py:295
  10.1 0.0 collective-permute-start.6
  10.1 1.3 %collective-permute-start.5 = (bf16[144,128]{1,0:T(8,128)(2,1)S(1)}, bf16[144,128]{1,0:T(8,128)(2,1)S(1)}, u32[]{:S(2)}, u32[]{:S(2)}) collective-permute-start(bf16[144,128]{1,0:T(8,128)(2,1)S(1)} %collective-permute-done.3.refs_7_), channel_id=1, source_target_pairs={{0,2},{1,3},{2,0},{3,1},{4,6},{5,7},{6,4},{7,5},{8,10},{9,11},{10,... | collective-permute-start | bytes 110600 | tf_op jit(solution)/shard_map/ppermute | solution.py:246
  11.4 0.6 %collective-permute-start.4 = (bf16[144,128]{1,0:T(8,128)(2,1)S(1)}, bf16[144,128]{1,0:T(8,128)(2,1)S(1)}, u32[]{:S(2)}, u32[]{:S(2)}) collective-permute-start(bf16[144,128]{1,0:T(8,128)(2,1)S(1)} %collective-permute-done.3.refs_7_), channel_id=1, source_target_pairs={{0,1},{1,0},{2,3},{3,2},{4,5},{5,4},{6,7},{7,6},{8,9},{9,8},{10,11... | collective-permute-start | bytes 110600 | tf_op jit(solution)/shard_map/ppermute | solution.py:246
  12.0 0.0 copy-start.3
  12.0 0.0 copy-start.2
  12.0 0.6 %pad_add_fusion.refs_0_.which_ref = s32[8]{0:T(128)} fusion(s32[6]{0:T(128)S(1)} %dynamic-slice_bitcast_fusion, s32[1]{0:T(128)} %bitcast.1, s32[1]{0:T(128)} %bitcast), kind=kLoop, calls=%fused_computation.4 | loop fusion | flops 16 | bytes 64 | tf_op jit(solution)/shard_map/concatenate | solution.py:302
  12.6 1.1 %collective-permute-done.6.refs_10_ = bf16[144,128]{1,0:T(8,128)(2,1)S(1)} collective-permute-done((bf16[144,128]{1,0:T(8,128)(2,1)S(1)}, bf16[144,128]{1,0:T(8,128)(2,1)S(1)}, u32[]{:S(2)}, u32[]{:S(2)}) %collective-permute-start.6) | collective-permute-done | bytes 36896 | tf_op jit(solution)/shard_map/ppermute | solution.py:246
  13.7 0.7 %collective-permute-done.5.refs_9_ = bf16[144,128]{1,0:T(8,128)(2,1)S(1)} collective-permute-done((bf16[144,128]{1,0:T(8,128)(2,1)S(1)}, bf16[144,128]{1,0:T(8,128)(2,1)S(1)}, u32[]{:S(2)}, u32[]{:S(2)}) %collective-permute-start.5) | collective-permute-done | bytes 36896 | tf_op jit(solution)/shard_map/ppermute | solution.py:246
  14.5 0.0 collective-permute-done.4.refs_8_
  14.5 0.0 collective-permute-done.refs_4_
  14.5 0.0 collective-permute-done.2.refs_6_
  14.5 0.0 copy-done.1
  14.5 0.0 copy-done.3
  14.5 0.0 copy-done.2
  14.5 2.1 %image.1 = (bf16[192,512]{1,0:T(8,128)(2,1)S(1)}, bf16[320,512]{1,0:T(8,128)(2,1)S(1)}, f32[264,128]{1,0:T(8,128)S(1)}) custom-call(s32[8]{0:T(128)} %pad_add_fusion.refs_0_.which_ref, f32[4]{0:T(128)} %refs_1_.1, s32[4]{0:T(128)} %refs_2_.1, bf16[512,128]{1,0:T(8,128)(2,1)S(1)} %copy-done.1, bf16[512,128]{1,0:T(8,128)(2,1)S(1)} %collective-permute-done.refs_4_, ...), custom_call_target="tpu_custom_call" | custom-call | tf_op jit(solution)/shard_map/image/pallas_call | solution.py:304
  16.6 0.0 copy-start
  16.6 0.3 collective-permute-start.7
  16.9 5.4 %collective-permute-done.7 = f32[264,128]{1,0:T(8,128)S(1)} collective-permute-done((f32[264,128]{1,0:T(8,128)S(1)}, f32[264,128]{1,0:T(8,128)S(1)}, u32[]{:S(2)}, u32[]{:S(2)}) %collective-permute-start.7) | collective-permute-done | bytes 135200 | tf_op jit(solution)/shard_map/ppermute | solution.py:246
  22.3 0.1 collective-permute-start.8
  22.4 5.0 %collective-permute-done.8 = f32[264,128]{1,0:T(8,128)S(1)} collective-permute-done((f32[264,128]{1,0:T(8,128)S(1)}, f32[264,128]{1,0:T(8,128)S(1)}, u32[]{:S(2)}, u32[]{:S(2)}) %collective-permute-start.8) | collective-permute-done | bytes 135200 | tf_op jit(solution)/shard_map/ppermute | solution.py:246
  27.4 2.3 %collective-permute-start.9 = (f32[264,128]{1,0:T(8,128)S(1)}, f32[264,128]{1,0:T(8,128)S(1)}, u32[]{:S(2)}, u32[]{:S(2)}) collective-permute-start(f32[264,128]{1,0:T(8,128)S(1)} %add.22), channel_id=1, source_target_pairs={{0,16},{4,20},{8,24},{12,28},{16,0},{20,4},{24,8},{28,12},{1,17},{... | collective-permute-start | bytes 405512 | tf_op jit(solution)/shard_map/ppermute | solution.py:246
  29.7 5.5 %collective-permute-done.9 = f32[264,128]{1,0:T(8,128)S(1)} collective-permute-done((f32[264,128]{1,0:T(8,128)S(1)}, f32[264,128]{1,0:T(8,128)S(1)}, u32[]{:S(2)}, u32[]{:S(2)}) %collective-permute-start.9) | collective-permute-done | bytes 135200 | tf_op jit(solution)/shard_map/ppermute | solution.py:246
  35.2 1.6 %collective-permute-start.13 = (f32[264,128]{1,0:T(8,128)S(1)}, f32[264,128]{1,0:T(8,128)S(1)}, u32[]{:S(2)}, u32[]{:S(2)}) collective-permute-start(f32[264,128]{1,0:T(8,128)S(1)} %add.23.share), channel_id=1, source_target_pairs={{0,2},{1,3},{2,0},{3,1},{4,6},{5,7},{6,4},{7,5},{8,10},{9,11},{10,... | collective-permute-start | bytes 405512 | tf_op jit(solution)/shard_map/ppermute | solution.py:246
  36.7 0.8 %collective-permute-start.10 = (bf16[320,512]{1,0:T(8,128)(2,1)S(1)}, bf16[320,512]{1,0:T(8,128)(2,1)S(1)}, u32[]{:S(2)}, u32[]{:S(2)}) collective-permute-start(bf16[320,512]{1,0:T(8,128)(2,1)S(1)} %get-tuple-element.14.second), channel_id=1, source_target_pairs={{0,4},{4,8},{8,12},{12,16},{16,20},{20,24},{24,28},{28,0},{1,5},{5... | collective-permute-start | bytes 983048 | tf_op jit(solution)/shard_map/ppermute | solution.py:326
  37.5 0.0 copy-start.4
  37.5 0.0 collective-permute-start.12
  37.5 3.9 %collective-permute-start.11 = (bf16[192,512]{1,0:T(8,128)(2,1)S(1)}, bf16[192,512]{1,0:T(8,128)(2,1)S(1)}, u32[]{:S(2)}, u32[]{:S(2)}) collective-permute-start(bf16[192,512]{1,0:T(8,128)(2,1)S(1)} %get-tuple-element.15.first), channel_id=1, source_target_pairs={{4,0},{8,4},{12,8},{16,12},{20,16},{24,20},{28,24},{0,28},{5,1},{9... | collective-permute-start | bytes 589832 | tf_op jit(solution)/shard_map/ppermute | solution.py:327
  41.5 0.0 collective-permute-done.13.across
  41.5 0.2 collective-permute-start.14
  41.7 0.0 copy-done.4
  41.7 0.6 %reshape.14.blocks_ref = s32[8]{0:T(128)} reshape(s32[2,4]{1,0:T(2,128)S(1)} %and_select_fusion) | data formatting | bytes 64 | tf_op jit(solution)/shard_map/reshape | solution.py:345
  42.3 0.0 collective-permute-done.12.beside
  42.3 0.5 collective-permute-done.14.opposite
  42.8 13.6 %factor.1.inverse = bf16[128,512]{1,0:T(8,128)(2,1)S(1)} custom-call(s32[8]{0:T(128)} %pad_add_fusion.refs_0_.which_ref, f32[264,128]{1,0:T(8,128)S(1)} %add.23.share, f32[264,128]{1,0:T(8,128)S(1)} %collective-permute-done.12.beside, f32[264,128]{1,0:T(8,128)S(1)} %collective-permute-done.13.across, f32[264,128]{1,0:T(8,128)S(1)} %collective-permute-done.14.opposite), custom_call_target="tpu_custom_call" | custom-call | tf_op jit(solution)/shard_map/factor/pallas_call | solution.py:330
  56.4 0.0 collective-permute-done.11.high
  56.4 0.0 collective-permute-done.10.low
  56.4 0.0 copy-done
  56.4 2.2 %project.1 = bf16[2,128,512]{2,1,0:T(8,128)(2,1)} custom-call(s32[8]{0:T(128)} %reshape.14.blocks_ref, s32[2]{0:T(128)} %counts_ref.1, bf16[320,512]{1,0:T(8,128)(2,1)S(1)} %collective-permute-done.10.low, bf16[192,512]{1,0:T(8,128)(2,1)S(1)} %get-tuple-element.15.first, bf16[320,512]{1,0:T(8,128)(2,1)S(1)} %get-tuple-element.14.second, ...), custom_call_target="tpu_custom_call" | custom-call | tf_op jit(solution)/shard_map/project/pallas_call | solution.py:348
  (4 shorter events, 0.1 us)
Async XLA Ops:
  0.0 14.5 %copy-start.1 = (bf16[512,128]{1,0:T(8,128)(2,1)S(1)}, bf16[512,128]{1,0:T(8,128)(2,1)}, u32[]{:S(2)}) copy-start(bf16[512,128]{1,0:T(8,128)(2,1)} %refs_3_.1) | copy-start | bytes 393220
  0.0 8.5 %collective-permute-start.1 = (bf16[512,128]{1,0:T(8,128)(2,1)}, bf16[512,128]{1,0:T(8,128)(2,1)S(1)}, u32[]{:S(2)}, u32[]{:S(2)}) collective-permute-start(bf16[512,128]{1,0:T(8,128)(2,1)} %refs_3_.1), channel_id=1, source_target_pairs={{0,2},{1,3},{2,0},{3,1},{4,6},{5,7},{6,4},{7,5},{8,10},{9,11},{10,... | collective-permute-start | bytes 393224 | tf_op jit(solution)/shard_map/ppermute | solution.py:246
  2.9 11.5 %collective-permute-start = (bf16[512,128]{1,0:T(8,128)(2,1)}, bf16[512,128]{1,0:T(8,128)(2,1)S(1)}, u32[]{:S(2)}, u32[]{:S(2)}) collective-permute-start(bf16[512,128]{1,0:T(8,128)(2,1)} %refs_3_.1), channel_id=1, source_target_pairs={{0,1},{1,0},{2,3},{3,2},{4,5},{5,4},{6,7},{7,6},{8,9},{9,8},{10,11... | collective-permute-start | bytes 393224 | tf_op jit(solution)/shard_map/ppermute | solution.py:246
  3.9 6.2 %collective-permute-start.3 = (bf16[144,128]{1,0:T(8,128)(2,1)S(1)}, bf16[144,128]{1,0:T(8,128)(2,1)S(1)}, u32[]{:S(2)}, u32[]{:S(2)}) collective-permute-start(bf16[144,128]{1,0:T(8,128)(2,1)S(1)} %pack.1), channel_id=1, source_target_pairs={{4,0},{8,4},{12,8},{16,12},{20,16},{24,20},{28,24},{0,28},{5,1},{9... | collective-permute-start | bytes 110600 | tf_op jit(solution)/shard_map/ppermute | solution.py:295
  8.5 6.0 %collective-permute-start.2 = (bf16[512,128]{1,0:T(8,128)(2,1)S(1)}, bf16[512,128]{1,0:T(8,128)(2,1)S(1)}, u32[]{:S(2)}, u32[]{:S(2)}) collective-permute-start(bf16[512,128]{1,0:T(8,128)(2,1)S(1)} %collective-permute-done.1.refs_5_), channel_id=1, source_target_pairs={{0,1},{1,0},{2,3},{3,2},{4,5},{5,4},{6,7},{7,6},{8,9},{9,8},{10,11... | collective-permute-start | bytes 393224 | tf_op jit(solution)/shard_map/ppermute | solution.py:246
  10.1 3.6 %collective-permute-start.6 = (bf16[144,128]{1,0:T(8,128)(2,1)S(1)}, bf16[144,128]{1,0:T(8,128)(2,1)S(1)}, u32[]{:S(2)}, u32[]{:S(2)}) collective-permute-start(bf16[144,128]{1,0:T(8,128)(2,1)S(1)} %collective-permute-done.3.refs_7_), channel_id=1, source_target_pairs={{0,3},{1,2},{2,1},{3,0},{4,7},{5,6},{6,5},{7,4},{8,11},{9,10},{10,... | collective-permute-start | bytes 110600 | tf_op jit(solution)/shard_map/ppermute | solution.py:246
  10.1 4.3 %collective-permute-start.5 = (bf16[144,128]{1,0:T(8,128)(2,1)S(1)}, bf16[144,128]{1,0:T(8,128)(2,1)S(1)}, u32[]{:S(2)}, u32[]{:S(2)}) collective-permute-start(bf16[144,128]{1,0:T(8,128)(2,1)S(1)} %collective-permute-done.3.refs_7_), channel_id=1, source_target_pairs={{0,2},{1,3},{2,0},{3,1},{4,6},{5,7},{6,4},{7,5},{8,10},{9,11},{10,... | collective-permute-start | bytes 110600 | tf_op jit(solution)/shard_map/ppermute | solution.py:246
  11.4 3.1 %collective-permute-start.4 = (bf16[144,128]{1,0:T(8,128)(2,1)S(1)}, bf16[144,128]{1,0:T(8,128)(2,1)S(1)}, u32[]{:S(2)}, u32[]{:S(2)}) collective-permute-start(bf16[144,128]{1,0:T(8,128)(2,1)S(1)} %collective-permute-done.3.refs_7_), channel_id=1, source_target_pairs={{0,1},{1,0},{2,3},{3,2},{4,5},{5,4},{6,7},{7,6},{8,9},{9,8},{10,11... | collective-permute-start | bytes 110600 | tf_op jit(solution)/shard_map/ppermute | solution.py:246
  12.0 2.5 %copy-start.3 = (f32[512]{0:T(512)S(1)}, f32[512]{0:T(512)}, u32[]{:S(2)}) copy-start(f32[512]{0:T(512)} %param.10) | copy-start | bytes 6148
  12.0 2.5 %copy-start.2 = (f32[512]{0:T(512)S(1)}, f32[512]{0:T(512)}, u32[]{:S(2)}) copy-start(f32[512]{0:T(512)} %param.11) | copy-start | bytes 6148
  16.6 39.8 %copy-start = (bf16[2,512,512]{2,1,0:T(8,128)(2,1)S(1)}, bf16[2,512,512]{2,1,0:T(8,128)(2,1)}, u32[]{:S(2)}) copy-start(bf16[2,512,512]{2,1,0:T(8,128)(2,1)} %shapes.1) | copy-start | bytes 3145732
  16.6 5.7 %collective-permute-start.7 = (f32[264,128]{1,0:T(8,128)S(1)}, f32[264,128]{1,0:T(8,128)S(1)}, u32[]{:S(2)}, u32[]{:S(2)}) collective-permute-start(f32[264,128]{1,0:T(8,128)S(1)} %get-tuple-element.11), channel_id=1, source_target_pairs={{0,4},{4,0},{8,12},{12,8},{16,20},{20,16},{24,28},{28,24},{1,5},{5... | collective-permute-start | bytes 405512 | tf_op jit(solution)/shard_map/ppermute | solution.py:246
  22.3 5.1 %collective-permute-start.8 = (f32[264,128]{1,0:T(8,128)S(1)}, f32[264,128]{1,0:T(8,128)S(1)}, u32[]{:S(2)}, u32[]{:S(2)}) collective-permute-start(f32[264,128]{1,0:T(8,128)S(1)} %add.21), channel_id=1, source_target_pairs={{0,8},{4,12},{8,0},{12,4},{16,24},{20,28},{24,16},{28,20},{1,9},{5... | collective-permute-start | bytes 405512 | tf_op jit(solution)/shard_map/ppermute | solution.py:246
  27.4 7.8 %collective-permute-start.9 = (f32[264,128]{1,0:T(8,128)S(1)}, f32[264,128]{1,0:T(8,128)S(1)}, u32[]{:S(2)}, u32[]{:S(2)}) collective-permute-start(f32[264,128]{1,0:T(8,128)S(1)} %add.22), channel_id=1, source_target_pairs={{0,16},{4,20},{8,24},{12,28},{16,0},{20,4},{24,8},{28,12},{1,17},{... | collective-permute-start | bytes 405512 | tf_op jit(solution)/shard_map/ppermute | solution.py:246
  35.2 6.3 %collective-permute-start.13 = (f32[264,128]{1,0:T(8,128)S(1)}, f32[264,128]{1,0:T(8,128)S(1)}, u32[]{:S(2)}, u32[]{:S(2)}) collective-permute-start(f32[264,128]{1,0:T(8,128)S(1)} %add.23.share), channel_id=1, source_target_pairs={{0,2},{1,3},{2,0},{3,1},{4,6},{5,7},{6,4},{7,5},{8,10},{9,11},{10,... | collective-permute-start | bytes 405512 | tf_op jit(solution)/shard_map/ppermute | solution.py:246
  36.7 19.7 %collective-permute-start.10 = (bf16[320,512]{1,0:T(8,128)(2,1)S(1)}, bf16[320,512]{1,0:T(8,128)(2,1)S(1)}, u32[]{:S(2)}, u32[]{:S(2)}) collective-permute-start(bf16[320,512]{1,0:T(8,128)(2,1)S(1)} %get-tuple-element.14.second), channel_id=1, source_target_pairs={{0,4},{4,8},{8,12},{12,16},{16,20},{20,24},{24,28},{28,0},{1,5},{5... | collective-permute-start | bytes 983048 | tf_op jit(solution)/shard_map/ppermute | solution.py:326
  37.5 4.2 %copy-start.4 = (s32[2,4]{1,0:T(2,128)S(1)}, s32[2,4]{1,0:T(2,128)}, u32[]{:S(2)}) copy-start(s32[2,4]{1,0:T(2,128)} %param.14) | copy-start | bytes 100
  37.5 4.8 %collective-permute-start.12 = (f32[264,128]{1,0:T(8,128)S(1)}, f32[264,128]{1,0:T(8,128)S(1)}, u32[]{:S(2)}, u32[]{:S(2)}) collective-permute-start(f32[264,128]{1,0:T(8,128)S(1)} %add.23.share), channel_id=1, source_target_pairs={{0,1},{1,0},{2,3},{3,2},{4,5},{5,4},{6,7},{7,6},{8,9},{9,8},{10,11... | collective-permute-start | bytes 405512 | tf_op jit(solution)/shard_map/ppermute | solution.py:246
  37.5 18.9 %collective-permute-start.11 = (bf16[192,512]{1,0:T(8,128)(2,1)S(1)}, bf16[192,512]{1,0:T(8,128)(2,1)S(1)}, u32[]{:S(2)}, u32[]{:S(2)}) collective-permute-start(bf16[192,512]{1,0:T(8,128)(2,1)S(1)} %get-tuple-element.15.first), channel_id=1, source_target_pairs={{4,0},{8,4},{12,8},{16,12},{20,16},{24,20},{28,24},{0,28},{5,1},{9... | collective-permute-start | bytes 589832 | tf_op jit(solution)/shard_map/ppermute | solution.py:327
  41.5 1.4 %collective-permute-start.14 = (f32[264,128]{1,0:T(8,128)S(1)}, f32[264,128]{1,0:T(8,128)S(1)}, u32[]{:S(2)}, u32[]{:S(2)}) collective-permute-start(f32[264,128]{1,0:T(8,128)S(1)} %collective-permute-done.13.across), channel_id=1, source_target_pairs={{0,1},{1,0},{2,3},{3,2},{4,5},{5,4},{6,7},{7,6},{8,9},{9,8},{10,11... | collective-permute-start | bytes 405512 | tf_op jit(solution)/shard_map/ppermute | solution.py:246

commit v6 on v5

--- a/solution.py
+++ b/solution.py
@@ -132,7 +132,7 @@
     return jnp.broadcast_to(x[t : t + 1, :], (8, BLOCK))
 
 
-def inverse_factor(square, depth=3):
+def inverse_factor(square, beside, depth=3):
     panels = BLOCK // 8
     sub = lax.broadcasted_iota(jnp.int32, (8, BLOCK), 0)
     lane = lax.broadcasted_iota(jnp.int32, (8, BLOCK), 1)
@@ -170,6 +170,8 @@
                 rows[i] = rows[i] - g[i] * a_row
         result.append(jnp.where(lane < 8 * p + 8, a * lax.rsqrt(pivots), 0.0))
         own = ahead
+        for _ in range(-(-len(beside) // (panels - p))):
+            beside.pop(0)()
         rest = p + 1 + depth
         if rest < panels:
             a0, a1, a2 = bf16_parts(a * inverses)
@@ -194,35 +196,77 @@
     across = ((1,), (1,))
     row = lax.broadcasted_iota(jnp.int32, (size, size), 0)
     column = lax.broadcasted_iota(jnp.int32, (size, size), 1)
+    blocks = {}
     for m, (one, two, three) in enumerate(SHARES):
+        blocks[three] = (m, size)
+        if one == two:
+            blocks[one] = (m, 0)
+
+    def diagonal(m, second):
         square = gram[m, 0:size, :]
-        if one == two:
-            schur[place(*one), :] = square
-        else:
-            turned = jnp.transpose(square)
-            schur[place(*one), :] = jnp.where(row >= column, square, turned)
-            diagonal = jnp.broadcast_to(gram[m, 2 * size : 2 * size + 1, :], (size, size))
-            schur[place(*two), :] = jnp.where(
-                row < column, square, jnp.where(row == column, diagonal, turned)
+        turned = jnp.transpose(square)
+        if not second:
+            return jnp.where(row >= column, square, turned)
+        middle = jnp.broadcast_to(gram[m, 2 * size : 2 * size + 1, :], (size, size))
+        return jnp.where(row < column, square, jnp.where(row == column, middle, turned))
+
+    def symmetric(k):
+        for m, (one, two, _) in enumerate(SHARES):
+            if one != two and (k, k) in (one, two):
+                return diagonal(m, (k, k) == two)
+
+    def original(i, j):
+        if i == j:
+            return symmetric(i)
+        m, at = blocks[i, j]
+        return gram[m, at : at + size, :]
+
+    lower = {}
+
+    def lower_block(i, k, w):
+        lower[i, k] = dot_f32(current(i, k), w, across)
+
+    def current(i, j):
+        return schur[place(i, j), :] if j else original(i, j)
+
+    def update(i, j, k):
+        value = schur[place(i, j), :] if k else original(i, j)
+        schur[place(i, j), :] = value - dot_f32(lower[i, k], lower[j, k], across)
+
+    def solve(i, k):
+        there, done = slice(i * size, (i + 1) * size), (k + 1) * size
+        product = dot_f32(lower[i, k], solved[k * size : done, :done])
+        if k:
+            product = product + jnp.concatenate(
+                [solved[there, : k * size], jnp.zeros((size, size), f32)], axis=1
             )
-        schur[place(*three), :] = gram[m, size : 2 * size, :]
-    solved[...] = jnp.zeros(solved.shape, f32)
+        solved[there, :done] = product
+
+    beside = []
     for k in range(count):
-        w = inverse_factor(schur[place(k, k), :])
+        w = inverse_factor(current(k, k), beside)
         here = slice(k * size, (k + 1) * size)
-        if k:
-            solved[here, : k * size] = -dot_f32(w, solved[here, : k * size])
-        solved[here, here] = w
-        lower = [None] * count
+        if k + 1 < count:
+            lower_block(k + 1, k, w)
+            update(k + 1, k + 1, k)
+
+        def finish(k=k, w=w, here=here):
+            if k:
+                solved[here, : k * size] = -dot_f32(w, solved[here, : k * size])
+            solved[here, here] = w
+            if k + 1 < count:
+                solved[here, (k + 1) * size :] = jnp.zeros((size, (count - 1 - k) * size), f32)
+
+        beside = [finish] if k + 1 < count else []
+        for i in range(k + 2, count):
+            beside.append(lambda i=i, k=k, w=w: lower_block(i, k, w))
         for i in range(k + 1, count):
-            lower[i] = dot_f32(schur[place(i, k), :], w, across)
-        for i in range(k + 1, count):
+            beside.append(lambda i=i, k=k: solve(i, k))
+        for i in range(k + 2, count):
             for j in range(k + 1, i + 1):
-                schur[place(i, j), :] = schur[place(i, j), :] - dot_f32(lower[i], lower[j], across)
-        for i in range(k + 1, count):
-            there = slice(i * size, (i + 1) * size)
-            done = (k + 1) * size
-            solved[there, :done] = solved[there, :done] + dot_f32(lower[i], solved[here, :done])
+                beside.append(lambda i=i, j=j, k=k: update(i, j, k))
+        if k + 1 == count:
+            finish()
     mine = pl.multiple_of(which_ref[0] * size, size)
     inverse[...] = solved[pl.ds(mine, size), :].astype(bf16)
 
@@ -253,10 +297,10 @@
 
 
 def sum_over_rows(value):
-    step = 1
-    while step < lax.axis_size("rows"):
+    step = lax.axis_size("rows") // 2
+    while step:
         value = value + exchange(value, "rows", step)
-        step *= 2
+        step //= 2
     return value
 
 

time: 58.8 us -> 58.5 us (level)
  starting transfers between devices: 18.8 us -> 18 us
    ppermute x12, starting transfers between devices: 9.47 us -> 8.71 us  [exchange(): lax.ppermute(value, axis, [(i, i ^ step) for i in range(lax.axis_size(axi...]
where the time goes in v6:
time: 58.5 us; the launch traced here: 58.3 us
  waiting for transfers between devices  19.5 us (33%)
  Pallas kernels  18.7 us (32%)
  starting transfers between devices  18 us (31%)
  local copies, waits for them, and re-layouts  1.31 us (2%)
  other arithmetic  0.65 us (1%)
    ppermute x12, waiting for transfers between devices, exchange(): lax.ppermute(value, axis, [(i, i ^ step) for i in range(lax.axis_size(axi...  18.8 us
    pallas_call x1, Pallas kernels, local(): pl.pallas_call(factor_kernel, out_shape=pltpu.VMEM((BLOCK, order), bf16),...  13.5 us
    ppermute x12, starting transfers between devices, exchange(): lax.ppermute(value, axis, [(i, i ^ step) for i in range(lax.axis_size(axi...  8.71 us
    ppermute x1, starting transfers between devices, local(): edge = lax.ppermute(packed, 'rows', back)  4.61 us
    ppermute x1, starting transfers between devices, local(): rim_high = lax.ppermute(one, 'rows', back)  3.92 us
    pallas_call x1, Pallas kernels, local(): pl.pallas_call(project_kernel, out_shape=jax.ShapeDtypeStruct((owned, mod...  2.18 us
    pallas_call x1, Pallas kernels, local(): pl.pallas_call(lambda *refs: image_kernel(0.5 / total_rows, *refs), out_s...  2.06 us
  transfers between devices with their start and end apart: 15, of which 7 were waited for; matrix products, arithmetic and copies ran while one was open for 3% of the time, Pallas kernels for 25%

profile of v6, /device:TPU:0, one launch (start us, length us, event | category | flops | bytes accessed | tf_op | source)
XLA Modules:
  0.0 58.3 jit_solution(7634829532480282295)
XLA Ops:
  0.0 0.0 copy-start.1
  0.0 2.9 %collective-permute-start.1 = (bf16[512,128]{1,0:T(8,128)(2,1)}, bf16[512,128]{1,0:T(8,128)(2,1)S(1)}, u32[]{:S(2)}, u32[]{:S(2)}) collective-permute-start(bf16[512,128]{1,0:T(8,128)(2,1)} %refs_3_.1), channel_id=1, source_target_pairs={{0,2},{1,3},{2,0},{3,1},{4,6},{5,7},{6,4},{7,5},{8,10},{9,11},{10,... | collective-permute-start | bytes 393224 | tf_op jit(solution)/shard_map/ppermute | solution.py:290
  2.9 0.0 collective-permute-start
  2.9 1.0 %pack.1 = bf16[144,128]{1,0:T(8,128)(2,1)S(1)} custom-call(bf16[512,128]{1,0:T(8,128)(2,1)} %refs_3_.1, f32[4,128]{1,0:T(4,128)} %bitcast.6, f32[4,128]{1,0:T(4,128)} %bitcast.8), custom_call_target="tpu_custom_call" | custom-call | tf_op jit(solution)/shard_map/pack/pallas_call | solution.py:332
  3.9 4.6 %collective-permute-start.3 = (bf16[144,128]{1,0:T(8,128)(2,1)S(1)}, bf16[144,128]{1,0:T(8,128)(2,1)S(1)}, u32[]{:S(2)}, u32[]{:S(2)}) collective-permute-start(bf16[144,128]{1,0:T(8,128)(2,1)S(1)} %pack.1), channel_id=1, source_target_pairs={{4,0},{8,4},{12,8},{16,12},{20,16},{24,20},{28,24},{0,28},{5,1},{9... | collective-permute-start | bytes 110600 | tf_op jit(solution)/shard_map/ppermute | solution.py:339
  8.5 0.0 collective-permute-done.1.refs_5_
  8.5 0.2 collective-permute-start.2
  8.7 0.7 %dynamic-slice_bitcast_fusion = s32[6]{0:T(128)S(1)} fusion(s32[4,6]{1,0:T(4,128)} %constant.38, s32[]{:T(128)S(6)} %select_n.11), kind=kLoop, calls=%fused_computation.5 | loop fusion | bytes 52 | tf_op jit(solution)/shard_map/squeeze | solution.py:345
  9.4 0.7 %collective-permute-done.3.refs_7_ = bf16[144,128]{1,0:T(8,128)(2,1)S(1)} collective-permute-done((bf16[144,128]{1,0:T(8,128)(2,1)S(1)}, bf16[144,128]{1,0:T(8,128)(2,1)S(1)}, u32[]{:S(2)}, u32[]{:S(2)}) %collective-permute-start.3) | collective-permute-done | bytes 36896 | tf_op jit(solution)/shard_map/ppermute | solution.py:339
  10.1 0.0 collective-permute-start.6
  10.1 1.3 %collective-permute-start.5 = (bf16[144,128]{1,0:T(8,128)(2,1)S(1)}, bf16[144,128]{1,0:T(8,128)(2,1)S(1)}, u32[]{:S(2)}, u32[]{:S(2)}) collective-permute-start(bf16[144,128]{1,0:T(8,128)(2,1)S(1)} %collective-permute-done.3.refs_7_), channel_id=1, source_target_pairs={{0,2},{1,3},{2,0},{3,1},{4,6},{5,7},{6,4},{7,5},{8,10},{9,11},{10,... | collective-permute-start | bytes 110600 | tf_op jit(solution)/shard_map/ppermute | solution.py:290
  11.4 0.6 %collective-permute-start.4 = (bf16[144,128]{1,0:T(8,128)(2,1)S(1)}, bf16[144,128]{1,0:T(8,128)(2,1)S(1)}, u32[]{:S(2)}, u32[]{:S(2)}) collective-permute-start(bf16[144,128]{1,0:T(8,128)(2,1)S(1)} %collective-permute-done.3.refs_7_), channel_id=1, source_target_pairs={{0,1},{1,0},{2,3},{3,2},{4,5},{5,4},{6,7},{7,6},{8,9},{9,8},{10,11... | collective-permute-start | bytes 110600 | tf_op jit(solution)/shard_map/ppermute | solution.py:290
  12.0 0.0 copy-start.3
  12.0 0.0 copy-start.2
  12.0 0.6 %pad_add_fusion.refs_0_.which_ref = s32[8]{0:T(128)} fusion(s32[6]{0:T(128)S(1)} %dynamic-slice_bitcast_fusion, s32[1]{0:T(128)} %bitcast.1, s32[1]{0:T(128)} %bitcast), kind=kLoop, calls=%fused_computation.4 | loop fusion | flops 16 | bytes 64 | tf_op jit(solution)/shard_map/concatenate | solution.py:346
  12.6 1.1 %collective-permute-done.6.refs_10_ = bf16[144,128]{1,0:T(8,128)(2,1)S(1)} collective-permute-done((bf16[144,128]{1,0:T(8,128)(2,1)S(1)}, bf16[144,128]{1,0:T(8,128)(2,1)S(1)}, u32[]{:S(2)}, u32[]{:S(2)}) %collective-permute-start.6) | collective-permute-done | bytes 36896 | tf_op jit(solution)/shard_map/ppermute | solution.py:290
  13.7 0.7 %collective-permute-done.5.refs_9_ = bf16[144,128]{1,0:T(8,128)(2,1)S(1)} collective-permute-done((bf16[144,128]{1,0:T(8,128)(2,1)S(1)}, bf16[144,128]{1,0:T(8,128)(2,1)S(1)}, u32[]{:S(2)}, u32[]{:S(2)}) %collective-permute-start.5) | collective-permute-done | bytes 36896 | tf_op jit(solution)/shard_map/ppermute | solution.py:290
  14.5 0.0 collective-permute-done.4.refs_8_
  14.5 0.0 collective-permute-done.refs_4_
  14.5 0.0 collective-permute-done.2.refs_6_
  14.5 0.0 copy-done.1
  14.5 0.0 copy-done.3
  14.5 0.0 copy-done.2
  14.5 2.1 %image.1 = (bf16[192,512]{1,0:T(8,128)(2,1)S(1)}, bf16[320,512]{1,0:T(8,128)(2,1)S(1)}, f32[264,128]{1,0:T(8,128)S(1)}) custom-call(s32[8]{0:T(128)} %pad_add_fusion.refs_0_.which_ref, f32[4]{0:T(128)} %refs_1_.1, s32[4]{0:T(128)} %refs_2_.1, bf16[512,128]{1,0:T(8,128)(2,1)S(1)} %copy-done.1, bf16[512,128]{1,0:T(8,128)(2,1)S(1)} %collective-permute-done.refs_4_, ...), custom_call_target="tpu_custom_call" | custom-call | tf_op jit(solution)/shard_map/image/pallas_call | solution.py:348
  16.6 0.0 copy-start
  16.6 1.3 %collective-permute-start.7 = (f32[264,128]{1,0:T(8,128)S(1)}, f32[264,128]{1,0:T(8,128)S(1)}, u32[]{:S(2)}, u32[]{:S(2)}) collective-permute-start(f32[264,128]{1,0:T(8,128)S(1)} %get-tuple-element.11), channel_id=1, source_target_pairs={{0,16},{4,20},{8,24},{12,28},{16,0},{20,4},{24,8},{28,12},{1,17},{... | collective-permute-start | bytes 405512 | tf_op jit(solution)/shard_map/ppermute | solution.py:290
  17.9 6.7 %collective-permute-done.7 = f32[264,128]{1,0:T(8,128)S(1)} collective-permute-done((f32[264,128]{1,0:T(8,128)S(1)}, f32[264,128]{1,0:T(8,128)S(1)}, u32[]{:S(2)}, u32[]{:S(2)}) %collective-permute-start.7) | collective-permute-done | bytes 135200 | tf_op jit(solution)/shard_map/ppermute | solution.py:290
  24.6 0.1 collective-permute-start.8
  24.7 5.0 %collective-permute-done.8 = f32[264,128]{1,0:T(8,128)S(1)} collective-permute-done((f32[264,128]{1,0:T(8,128)S(1)}, f32[264,128]{1,0:T(8,128)S(1)}, u32[]{:S(2)}, u32[]{:S(2)}) %collective-permute-start.8) | collective-permute-done | bytes 135200 | tf_op jit(solution)/shard_map/ppermute | solution.py:290
  29.7 0.4 collective-permute-start.9
  30.1 4.7 %collective-permute-done.9 = f32[264,128]{1,0:T(8,128)S(1)} collective-permute-done((f32[264,128]{1,0:T(8,128)S(1)}, f32[264,128]{1,0:T(8,128)S(1)}, u32[]{:S(2)}, u32[]{:S(2)}) %collective-permute-start.9) | collective-permute-done | bytes 135200 | tf_op jit(solution)/shard_map/ppermute | solution.py:290
  34.8 1.7 %collective-permute-start.13 = (f32[264,128]{1,0:T(8,128)S(1)}, f32[264,128]{1,0:T(8,128)S(1)}, u32[]{:S(2)}, u32[]{:S(2)}) collective-permute-start(f32[264,128]{1,0:T(8,128)S(1)} %add.23.share), channel_id=1, source_target_pairs={{0,2},{1,3},{2,0},{3,1},{4,6},{5,7},{6,4},{7,5},{8,10},{9,11},{10,... | collective-permute-start | bytes 405512 | tf_op jit(solution)/shard_map/ppermute | solution.py:290
  36.5 0.8 %collective-permute-start.10 = (bf16[320,512]{1,0:T(8,128)(2,1)S(1)}, bf16[320,512]{1,0:T(8,128)(2,1)S(1)}, u32[]{:S(2)}, u32[]{:S(2)}) collective-permute-start(bf16[320,512]{1,0:T(8,128)(2,1)S(1)} %get-tuple-element.14.second), channel_id=1, source_target_pairs={{0,4},{4,8},{8,12},{12,16},{16,20},{20,24},{24,28},{28,0},{1,5},{5... | collective-permute-start | bytes 983048 | tf_op jit(solution)/shard_map/ppermute | solution.py:370
  37.3 0.0 copy-start.4
  37.3 0.0 collective-permute-start.12
  37.3 3.9 %collective-permute-start.11 = (bf16[192,512]{1,0:T(8,128)(2,1)S(1)}, bf16[192,512]{1,0:T(8,128)(2,1)S(1)}, u32[]{:S(2)}, u32[]{:S(2)}) collective-permute-start(bf16[192,512]{1,0:T(8,128)(2,1)S(1)} %get-tuple-element.15.first), channel_id=1, source_target_pairs={{4,0},{8,4},{12,8},{16,12},{20,16},{24,20},{28,24},{0,28},{5,1},{9... | collective-permute-start | bytes 589832 | tf_op jit(solution)/shard_map/ppermute | solution.py:371
  41.3 0.0 collective-permute-done.13.across
  41.3 0.2 collective-permute-start.14
  41.5 0.0 copy-done.4
  41.5 0.6 %reshape.14.blocks_ref = s32[8]{0:T(128)} reshape(s32[2,4]{1,0:T(2,128)S(1)} %and_select_fusion) | data formatting | bytes 64 | tf_op jit(solution)/shard_map/reshape | solution.py:389
  42.1 0.0 collective-permute-done.12.beside
  42.1 0.5 collective-permute-done.14.opposite
  42.6 13.5 %factor.1.inverse = bf16[128,512]{1,0:T(8,128)(2,1)S(1)} custom-call(s32[8]{0:T(128)} %pad_add_fusion.refs_0_.which_ref, f32[264,128]{1,0:T(8,128)S(1)} %add.23.share, f32[264,128]{1,0:T(8,128)S(1)} %collective-permute-done.12.beside, f32[264,128]{1,0:T(8,128)S(1)} %collective-permute-done.13.across, f32[264,128]{1,0:T(8,128)S(1)} %collective-permute-done.14.opposite), custom_call_target="tpu_custom_call" | custom-call | tf_op jit(solution)/shard_map/factor/pallas_call | solution.py:374
  56.1 0.0 collective-permute-done.11.high
  56.1 0.0 collective-permute-done.10.low
  56.1 0.0 copy-done
  56.2 2.2 %project.1 = bf16[2,128,512]{2,1,0:T(8,128)(2,1)} custom-call(s32[8]{0:T(128)} %reshape.14.blocks_ref, s32[2]{0:T(128)} %counts_ref.1, bf16[320,512]{1,0:T(8,128)(2,1)S(1)} %collective-permute-done.10.low, bf16[192,512]{1,0:T(8,128)(2,1)S(1)} %get-tuple-element.15.first, bf16[320,512]{1,0:T(8,128)(2,1)S(1)} %get-tuple-element.14.second, ...), custom_call_target="tpu_custom_call" | custom-call | tf_op jit(solution)/shard_map/project/pallas_call | solution.py:392
  (4 shorter events, 0.1 us)
Async XLA Ops:
  0.0 14.5 %copy-start.1 = (bf16[512,128]{1,0:T(8,128)(2,1)S(1)}, bf16[512,128]{1,0:T(8,128)(2,1)}, u32[]{:S(2)}) copy-start(bf16[512,128]{1,0:T(8,128)(2,1)} %refs_3_.1) | copy-start | bytes 393220
  0.0 8.5 %collective-permute-start.1 = (bf16[512,128]{1,0:T(8,128)(2,1)}, bf16[512,128]{1,0:T(8,128)(2,1)S(1)}, u32[]{:S(2)}, u32[]{:S(2)}) collective-permute-start(bf16[512,128]{1,0:T(8,128)(2,1)} %refs_3_.1), channel_id=1, source_target_pairs={{0,2},{1,3},{2,0},{3,1},{4,6},{5,7},{6,4},{7,5},{8,10},{9,11},{10,... | collective-permute-start | bytes 393224 | tf_op jit(solution)/shard_map/ppermute | solution.py:290
  2.9 11.5 %collective-permute-start = (bf16[512,128]{1,0:T(8,128)(2,1)}, bf16[512,128]{1,0:T(8,128)(2,1)S(1)}, u32[]{:S(2)}, u32[]{:S(2)}) collective-permute-start(bf16[512,128]{1,0:T(8,128)(2,1)} %refs_3_.1), channel_id=1, source_target_pairs={{0,1},{1,0},{2,3},{3,2},{4,5},{5,4},{6,7},{7,6},{8,9},{9,8},{10,11... | collective-permute-start | bytes 393224 | tf_op jit(solution)/shard_map/ppermute | solution.py:290
  3.9 6.2 %collective-permute-start.3 = (bf16[144,128]{1,0:T(8,128)(2,1)S(1)}, bf16[144,128]{1,0:T(8,128)(2,1)S(1)}, u32[]{:S(2)}, u32[]{:S(2)}) collective-permute-start(bf16[144,128]{1,0:T(8,128)(2,1)S(1)} %pack.1), channel_id=1, source_target_pairs={{4,0},{8,4},{12,8},{16,12},{20,16},{24,20},{28,24},{0,28},{5,1},{9... | collective-permute-start | bytes 110600 | tf_op jit(solution)/shard_map/ppermute | solution.py:339
  8.5 6.0 %collective-permute-start.2 = (bf16[512,128]{1,0:T(8,128)(2,1)S(1)}, bf16[512,128]{1,0:T(8,128)(2,1)S(1)}, u32[]{:S(2)}, u32[]{:S(2)}) collective-permute-start(bf16[512,128]{1,0:T(8,128)(2,1)S(1)} %collective-permute-done.1.refs_5_), channel_id=1, source_target_pairs={{0,1},{1,0},{2,3},{3,2},{4,5},{5,4},{6,7},{7,6},{8,9},{9,8},{10,11... | collective-permute-start | bytes 393224 | tf_op jit(solution)/shard_map/ppermute | solution.py:290
  10.1 3.6 %collective-permute-start.6 = (bf16[144,128]{1,0:T(8,128)(2,1)S(1)}, bf16[144,128]{1,0:T(8,128)(2,1)S(1)}, u32[]{:S(2)}, u32[]{:S(2)}) collective-permute-start(bf16[144,128]{1,0:T(8,128)(2,1)S(1)} %collective-permute-done.3.refs_7_), channel_id=1, source_target_pairs={{0,3},{1,2},{2,1},{3,0},{4,7},{5,6},{6,5},{7,4},{8,11},{9,10},{10,... | collective-permute-start | bytes 110600 | tf_op jit(solution)/shard_map/ppermute | solution.py:290
  10.1 4.3 %collective-permute-start.5 = (bf16[144,128]{1,0:T(8,128)(2,1)S(1)}, bf16[144,128]{1,0:T(8,128)(2,1)S(1)}, u32[]{:S(2)}, u32[]{:S(2)}) collective-permute-start(bf16[144,128]{1,0:T(8,128)(2,1)S(1)} %collective-permute-done.3.refs_7_), channel_id=1, source_target_pairs={{0,2},{1,3},{2,0},{3,1},{4,6},{5,7},{6,4},{7,5},{8,10},{9,11},{10,... | collective-permute-start | bytes 110600 | tf_op jit(solution)/shard_map/ppermute | solution.py:290
  11.4 3.1 %collective-permute-start.4 = (bf16[144,128]{1,0:T(8,128)(2,1)S(1)}, bf16[144,128]{1,0:T(8,128)(2,1)S(1)}, u32[]{:S(2)}, u32[]{:S(2)}) collective-permute-start(bf16[144,128]{1,0:T(8,128)(2,1)S(1)} %collective-permute-done.3.refs_7_), channel_id=1, source_target_pairs={{0,1},{1,0},{2,3},{3,2},{4,5},{5,4},{6,7},{7,6},{8,9},{9,8},{10,11... | collective-permute-start | bytes 110600 | tf_op jit(solution)/shard_map/ppermute | solution.py:290
  12.0 2.5 %copy-start.3 = (f32[512]{0:T(512)S(1)}, f32[512]{0:T(512)}, u32[]{:S(2)}) copy-start(f32[512]{0:T(512)} %param.10) | copy-start | bytes 6148
  12.0 2.5 %copy-start.2 = (f32[512]{0:T(512)S(1)}, f32[512]{0:T(512)}, u32[]{:S(2)}) copy-start(f32[512]{0:T(512)} %param.11) | copy-start | bytes 6148
  16.6 39.6 %copy-start = (bf16[2,512,512]{2,1,0:T(8,128)(2,1)S(1)}, bf16[2,512,512]{2,1,0:T(8,128)(2,1)}, u32[]{:S(2)}) copy-start(bf16[2,512,512]{2,1,0:T(8,128)(2,1)} %shapes.1) | copy-start | bytes 3145732
  16.6 8.0 %collective-permute-start.7 = (f32[264,128]{1,0:T(8,128)S(1)}, f32[264,128]{1,0:T(8,128)S(1)}, u32[]{:S(2)}, u32[]{:S(2)}) collective-permute-start(f32[264,128]{1,0:T(8,128)S(1)} %get-tuple-element.11), channel_id=1, source_target_pairs={{0,16},{4,20},{8,24},{12,28},{16,0},{20,4},{24,8},{28,12},{1,17},{... | collective-permute-start | bytes 405512 | tf_op jit(solution)/shard_map/ppermute | solution.py:290
  24.6 5.1 %collective-permute-start.8 = (f32[264,128]{1,0:T(8,128)S(1)}, f32[264,128]{1,0:T(8,128)S(1)}, u32[]{:S(2)}, u32[]{:S(2)}) collective-permute-start(f32[264,128]{1,0:T(8,128)S(1)} %add.21), channel_id=1, source_target_pairs={{0,8},{4,12},{8,0},{12,4},{16,24},{20,28},{24,16},{28,20},{1,9},{5... | collective-permute-start | bytes 405512 | tf_op jit(solution)/shard_map/ppermute | solution.py:290
  29.7 5.1 %collective-permute-start.9 = (f32[264,128]{1,0:T(8,128)S(1)}, f32[264,128]{1,0:T(8,128)S(1)}, u32[]{:S(2)}, u32[]{:S(2)}) collective-permute-start(f32[264,128]{1,0:T(8,128)S(1)} %add.22), channel_id=1, source_target_pairs={{0,4},{4,0},{8,12},{12,8},{16,20},{20,16},{24,28},{28,24},{1,5},{5... | collective-permute-start | bytes 405512 | tf_op jit(solution)/shard_map/ppermute | solution.py:290
  34.8 6.4 %collective-permute-start.13 = (f32[264,128]{1,0:T(8,128)S(1)}, f32[264,128]{1,0:T(8,128)S(1)}, u32[]{:S(2)}, u32[]{:S(2)}) collective-permute-start(f32[264,128]{1,0:T(8,128)S(1)} %add.23.share), channel_id=1, source_target_pairs={{0,2},{1,3},{2,0},{3,1},{4,6},{5,7},{6,4},{7,5},{8,10},{9,11},{10,... | collective-permute-start | bytes 405512 | tf_op jit(solution)/shard_map/ppermute | solution.py:290
  36.5 19.6 %collective-permute-start.10 = (bf16[320,512]{1,0:T(8,128)(2,1)S(1)}, bf16[320,512]{1,0:T(8,128)(2,1)S(1)}, u32[]{:S(2)}, u32[]{:S(2)}) collective-permute-start(bf16[320,512]{1,0:T(8,128)(2,1)S(1)} %get-tuple-element.14.second), channel_id=1, source_target_pairs={{0,4},{4,8},{8,12},{12,16},{16,20},{20,24},{24,28},{28,0},{1,5},{5... | collective-permute-start | bytes 983048 | tf_op jit(solution)/shard_map/ppermute | solution.py:370
  37.3 4.2 %copy-start.4 = (s32[2,4]{1,0:T(2,128)S(1)}, s32[2,4]{1,0:T(2,128)}, u32[]{:S(2)}) copy-start(s32[2,4]{1,0:T(2,128)} %param.14) | copy-start | bytes 100
  37.3 4.8 %collective-permute-start.12 = (f32[264,128]{1,0:T(8,128)S(1)}, f32[264,128]{1,0:T(8,128)S(1)}, u32[]{:S(2)}, u32[]{:S(2)}) collective-permute-start(f32[264,128]{1,0:T(8,128)S(1)} %add.23.share), channel_id=1, source_target_pairs={{0,1},{1,0},{2,3},{3,2},{4,5},{5,4},{6,7},{7,6},{8,9},{9,8},{10,11... | collective-permute-start | bytes 405512 | tf_op jit(solution)/shard_map/ppermute | solution.py:290
  37.3 18.8 %collective-permute-start.11 = (bf16[192,512]{1,0:T(8,128)(2,1)S(1)}, bf16[192,512]{1,0:T(8,128)(2,1)S(1)}, u32[]{:S(2)}, u32[]{:S(2)}) collective-permute-start(bf16[192,512]{1,0:T(8,128)(2,1)S(1)} %get-tuple-element.15.first), channel_id=1, source_target_pairs={{4,0},{8,4},{12,8},{16,12},{20,16},{24,20},{28,24},{0,28},{5,1},{9... | collective-permute-start | bytes 589832 | tf_op jit(solution)/shard_map/ppermute | solution.py:371
  41.3 1.4 %collective-permute-start.14 = (f32[264,128]{1,0:T(8,128)S(1)}, f32[264,128]{1,0:T(8,128)S(1)}, u32[]{:S(2)}, u32[]{:S(2)}) collective-permute-start(f32[264,128]{1,0:T(8,128)S(1)} %collective-permute-done.13.across), channel_id=1, source_target_pairs={{0,1},{1,0},{2,3},{3,2},{4,5},{5,4},{6,7},{7,6},{8,9},{9,8},{10,11... | collective-permute-start | bytes 405512 | tf_op jit(solution)/shard_map/ppermute | solution.py:290

commit v7 on v6

--- a/solution.py
+++ b/solution.py
@@ -140,35 +140,49 @@
     own = [lanes_of(rows[0], t) for t in range(8)]
     result = []
     for p in range(panels):
-        below = range(p + 1, min(panels, p + 1 + depth))
-        under = {i: [lanes_of(rows[i], 8 * p + t) for t in range(8)] for i in below}
-        ahead = [lanes_of(rows[p + 1], 8 * p + 8 + t) for t in range(8)] if p + 1 < panels else []
+        has_next = p + 1 < panels
         inside = jnp.logical_and(lane >= 8 * p, lane < 8 * p + 8)
         a = jnp.where(inside, (lane == sub + 8 * p).astype(f32), rows[p])
-        for i in below:
-            rows[i] = jnp.where(inside, 0.0, rows[i])
+        ahead = []
+        if has_next:
+            under = [lanes_of(rows[p + 1], 8 * p + t) for t in range(8)]
+            ahead = [lanes_of(rows[p + 1], 8 * p + 8 + t) for t in range(8)]
+            c = jnp.where(inside, 0.0, rows[p + 1])
         pivots = jnp.ones((8, BLOCK), f32)
         inverses = jnp.ones((8, BLOCK), f32)
+        steps = []
         for t in range(8):
             pivot = rows_of(own[t], t)
             inverse = 1.0 / pivot
             pivots = jnp.where(sub == t, pivot, pivots)
             inverses = jnp.where(sub == t, inverse, inverses)
             f = jnp.where(sub > t, own[t], 0.0) * inverse
-            g = {i: under[i][t] * inverse for i in below}
+            a_row = rows_of(a, t)
+            u_rows = {u: rows_of(own[u], t) for u in range(t + 1, 8)}
+            steps.append((inverse, u_rows, a_row))
             for u in range(t + 1, 8):
-                u_row = rows_of(own[u], t)
-                own[u] = own[u] - f * u_row
-                for i in below:
-                    under[i][u] = under[i][u] - g[i] * u_row
-            for u in range(len(ahead)):
-                ahead[u] = ahead[u] - g[p + 1] * rows_of(under[p + 1][t], u)
-            a_row = rows_of(a, t)
+                own[u] = own[u] - f * u_rows[u]
             if t < 7:
                 a = a - f * a_row
-            for i in below:
-                rows[i] = rows[i] - g[i] * a_row
+            if has_next:
+                g = under[t] * inverse
+                for u in range(t + 1, 8):
+                    under[u] = under[u] - g * u_rows[u]
+                for u in range(8):
+                    ahead[u] = ahead[u] - g * rows_of(under[t], u)
+                c = c - g * a_row
         result.append(jnp.where(lane < 8 * p + 8, a * lax.rsqrt(pivots), 0.0))
+        for i in range(p + 2, min(panels, p + 1 + depth)):
+            below = [lanes_of(rows[i], 8 * p + t) for t in range(8)]
+            d = jnp.where(inside, 0.0, rows[i])
+            for t, (inverse, u_rows, a_row) in enumerate(steps):
+                g = below[t] * inverse
+                for u in range(t + 1, 8):
+                    below[u] = below[u] - g * u_rows[u]
+                d = d - g * a_row
+            rows[i] = d
+        if has_next:
+            rows[p + 1] = c
         own = ahead
         for _ in range(-(-len(beside) // (panels - p))):
             beside.pop(0)()

time: 58.5 us -> 58.6 us (level)
  no operation moved by 1% of the time
where the time goes in v7:
time: 58.6 us; the launch traced here: 58.4 us
  waiting for transfers between devices  19.5 us (33%)
  Pallas kernels  18.7 us (32%)
  starting transfers between devices  18 us (31%)
  local copies, waits for them, and re-layouts  1.31 us (2%)
  other arithmetic  0.65 us (1%)
    ppermute x12, waiting for transfers between devices, exchange(): lax.ppermute(value, axis, [(i, i ^ step) for i in range(lax.axis_size(axi...  18.8 us
    pallas_call x1, Pallas kernels, local(): pl.pallas_call(factor_kernel, out_shape=pltpu.VMEM((BLOCK, order), bf16),...  13.5 us
    ppermute x12, starting transfers between devices, exchange(): lax.ppermute(value, axis, [(i, i ^ step) for i in range(lax.axis_size(axi...  8.71 us
    ppermute x1, starting transfers between devices, local(): edge = lax.ppermute(packed, 'rows', back)  4.61 us
    ppermute x1, starting transfers between devices, local(): rim_high = lax.ppermute(one, 'rows', back)  3.92 us
    pallas_call x1, Pallas kernels, local(): pl.pallas_call(project_kernel, out_shape=jax.ShapeDtypeStruct((owned, mod...  2.17 us
    pallas_call x1, Pallas kernels, local(): pl.pallas_call(lambda *refs: image_kernel(0.5 / total_rows, *refs), out_s...  2.06 us
  transfers between devices with their start and end apart: 15, of which 7 were waited for; matrix products, arithmetic and copies ran while one was open for 3% of the time, Pallas kernels for 25%

profile of v7, /device:TPU:0, one launch (start us, length us, event | category | flops | bytes accessed | tf_op | source)
XLA Modules:
  0.0 58.4 jit_solution(3662036297662370443)
XLA Ops:
  0.0 0.0 copy-start.1
  0.0 2.9 %collective-permute-start.1 = (bf16[512,128]{1,0:T(8,128)(2,1)}, bf16[512,128]{1,0:T(8,128)(2,1)S(1)}, u32[]{:S(2)}, u32[]{:S(2)}) collective-permute-start(bf16[512,128]{1,0:T(8,128)(2,1)} %refs_3_.1), channel_id=1, source_target_pairs={{0,2},{1,3},{2,0},{3,1},{4,6},{5,7},{6,4},{7,5},{8,10},{9,11},{10,... | collective-permute-start | bytes 393224 | tf_op jit(solution)/shard_map/ppermute | solution.py:304
  2.9 0.0 collective-permute-start
  2.9 1.0 %pack.1 = bf16[144,128]{1,0:T(8,128)(2,1)S(1)} custom-call(bf16[512,128]{1,0:T(8,128)(2,1)} %refs_3_.1, f32[4,128]{1,0:T(4,128)} %bitcast.6, f32[4,128]{1,0:T(4,128)} %bitcast.8), custom_call_target="tpu_custom_call" | custom-call | tf_op jit(solution)/shard_map/pack/pallas_call | solution.py:346
  3.9 4.6 %collective-permute-start.3 = (bf16[144,128]{1,0:T(8,128)(2,1)S(1)}, bf16[144,128]{1,0:T(8,128)(2,1)S(1)}, u32[]{:S(2)}, u32[]{:S(2)}) collective-permute-start(bf16[144,128]{1,0:T(8,128)(2,1)S(1)} %pack.1), channel_id=1, source_target_pairs={{4,0},{8,4},{12,8},{16,12},{20,16},{24,20},{28,24},{0,28},{5,1},{9... | collective-permute-start | bytes 110600 | tf_op jit(solution)/shard_map/ppermute | solution.py:353
  8.5 0.0 collective-permute-done.1.refs_5_
  8.5 0.2 collective-permute-start.2
  8.7 0.7 %dynamic-slice_bitcast_fusion = s32[6]{0:T(128)S(1)} fusion(s32[4,6]{1,0:T(4,128)} %constant.38, s32[]{:T(128)S(6)} %select_n.11), kind=kLoop, calls=%fused_computation.5 | loop fusion | bytes 52 | tf_op jit(solution)/shard_map/squeeze | solution.py:359
  9.4 0.7 %collective-permute-done.3.refs_7_ = bf16[144,128]{1,0:T(8,128)(2,1)S(1)} collective-permute-done((bf16[144,128]{1,0:T(8,128)(2,1)S(1)}, bf16[144,128]{1,0:T(8,128)(2,1)S(1)}, u32[]{:S(2)}, u32[]{:S(2)}) %collective-permute-start.3) | collective-permute-done | bytes 36896 | tf_op jit(solution)/shard_map/ppermute | solution.py:353
  10.1 0.0 collective-permute-start.6
  10.1 1.3 %collective-permute-start.5 = (bf16[144,128]{1,0:T(8,128)(2,1)S(1)}, bf16[144,128]{1,0:T(8,128)(2,1)S(1)}, u32[]{:S(2)}, u32[]{:S(2)}) collective-permute-start(bf16[144,128]{1,0:T(8,128)(2,1)S(1)} %collective-permute-done.3.refs_7_), channel_id=1, source_target_pairs={{0,2},{1,3},{2,0},{3,1},{4,6},{5,7},{6,4},{7,5},{8,10},{9,11},{10,... | collective-permute-start | bytes 110600 | tf_op jit(solution)/shard_map/ppermute | solution.py:304
  11.4 0.6 %collective-permute-start.4 = (bf16[144,128]{1,0:T(8,128)(2,1)S(1)}, bf16[144,128]{1,0:T(8,128)(2,1)S(1)}, u32[]{:S(2)}, u32[]{:S(2)}) collective-permute-start(bf16[144,128]{1,0:T(8,128)(2,1)S(1)} %collective-permute-done.3.refs_7_), channel_id=1, source_target_pairs={{0,1},{1,0},{2,3},{3,2},{4,5},{5,4},{6,7},{7,6},{8,9},{9,8},{10,11... | collective-permute-start | bytes 110600 | tf_op jit(solution)/shard_map/ppermute | solution.py:304
  12.0 0.0 copy-start.3
  12.0 0.0 copy-start.2
  12.0 0.6 %pad_add_fusion.refs_0_.which_ref = s32[8]{0:T(128)} fusion(s32[6]{0:T(128)S(1)} %dynamic-slice_bitcast_fusion, s32[1]{0:T(128)} %bitcast.1, s32[1]{0:T(128)} %bitcast), kind=kLoop, calls=%fused_computation.4 | loop fusion | flops 16 | bytes 64 | tf_op jit(solution)/shard_map/concatenate | solution.py:360
  12.6 1.1 %collective-permute-done.6.refs_10_ = bf16[144,128]{1,0:T(8,128)(2,1)S(1)} collective-permute-done((bf16[144,128]{1,0:T(8,128)(2,1)S(1)}, bf16[144,128]{1,0:T(8,128)(2,1)S(1)}, u32[]{:S(2)}, u32[]{:S(2)}) %collective-permute-start.6) | collective-permute-done | bytes 36896 | tf_op jit(solution)/shard_map/ppermute | solution.py:304
  13.7 0.7 %collective-permute-done.5.refs_9_ = bf16[144,128]{1,0:T(8,128)(2,1)S(1)} collective-permute-done((bf16[144,128]{1,0:T(8,128)(2,1)S(1)}, bf16[144,128]{1,0:T(8,128)(2,1)S(1)}, u32[]{:S(2)}, u32[]{:S(2)}) %collective-permute-start.5) | collective-permute-done | bytes 36896 | tf_op jit(solution)/shard_map/ppermute | solution.py:304
  14.5 0.0 collective-permute-done.4.refs_8_
  14.5 0.0 collective-permute-done.refs_4_
  14.5 0.0 collective-permute-done.2.refs_6_
  14.5 0.0 copy-done.1
  14.5 0.0 copy-done.3
  14.5 0.0 copy-done.2
  14.5 2.1 %image.1 = (bf16[192,512]{1,0:T(8,128)(2,1)S(1)}, bf16[320,512]{1,0:T(8,128)(2,1)S(1)}, f32[264,128]{1,0:T(8,128)S(1)}) custom-call(s32[8]{0:T(128)} %pad_add_fusion.refs_0_.which_ref, f32[4]{0:T(128)} %refs_1_.1, s32[4]{0:T(128)} %refs_2_.1, bf16[512,128]{1,0:T(8,128)(2,1)S(1)} %copy-done.1, bf16[512,128]{1,0:T(8,128)(2,1)S(1)} %collective-permute-done.refs_4_, ...), custom_call_target="tpu_custom_call" | custom-call | tf_op jit(solution)/shard_map/image/pallas_call | solution.py:362
  16.6 0.0 copy-start
  16.6 1.3 %collective-permute-start.7 = (f32[264,128]{1,0:T(8,128)S(1)}, f32[264,128]{1,0:T(8,128)S(1)}, u32[]{:S(2)}, u32[]{:S(2)}) collective-permute-start(f32[264,128]{1,0:T(8,128)S(1)} %get-tuple-element.11), channel_id=1, source_target_pairs={{0,16},{4,20},{8,24},{12,28},{16,0},{20,4},{24,8},{28,12},{1,17},{... | collective-permute-start | bytes 405512 | tf_op jit(solution)/shard_map/ppermute | solution.py:304
  17.9 6.7 %collective-permute-done.7 = f32[264,128]{1,0:T(8,128)S(1)} collective-permute-done((f32[264,128]{1,0:T(8,128)S(1)}, f32[264,128]{1,0:T(8,128)S(1)}, u32[]{:S(2)}, u32[]{:S(2)}) %collective-permute-start.7) | collective-permute-done | bytes 135200 | tf_op jit(solution)/shard_map/ppermute | solution.py:304
  24.6 0.1 collective-permute-start.8
  24.7 5.0 %collective-permute-done.8 = f32[264,128]{1,0:T(8,128)S(1)} collective-permute-done((f32[264,128]{1,0:T(8,128)S(1)}, f32[264,128]{1,0:T(8,128)S(1)}, u32[]{:S(2)}, u32[]{:S(2)}) %collective-permute-start.8) | collective-permute-done | bytes 135200 | tf_op jit(solution)/shard_map/ppermute | solution.py:304
  29.7 0.4 collective-permute-start.9
  30.1 4.7 %collective-permute-done.9 = f32[264,128]{1,0:T(8,128)S(1)} collective-permute-done((f32[264,128]{1,0:T(8,128)S(1)}, f32[264,128]{1,0:T(8,128)S(1)}, u32[]{:S(2)}, u32[]{:S(2)}) %collective-permute-start.9) | collective-permute-done | bytes 135200 | tf_op jit(solution)/shard_map/ppermute | solution.py:304
  34.8 1.7 %collective-permute-start.13 = (f32[264,128]{1,0:T(8,128)S(1)}, f32[264,128]{1,0:T(8,128)S(1)}, u32[]{:S(2)}, u32[]{:S(2)}) collective-permute-start(f32[264,128]{1,0:T(8,128)S(1)} %add.23.share), channel_id=1, source_target_pairs={{0,2},{1,3},{2,0},{3,1},{4,6},{5,7},{6,4},{7,5},{8,10},{9,11},{10,... | collective-permute-start | bytes 405512 | tf_op jit(solution)/shard_map/ppermute | solution.py:304
  36.5 0.8 %collective-permute-start.10 = (bf16[320,512]{1,0:T(8,128)(2,1)S(1)}, bf16[320,512]{1,0:T(8,128)(2,1)S(1)}, u32[]{:S(2)}, u32[]{:S(2)}) collective-permute-start(bf16[320,512]{1,0:T(8,128)(2,1)S(1)} %get-tuple-element.14.second), channel_id=1, source_target_pairs={{0,4},{4,8},{8,12},{12,16},{16,20},{20,24},{24,28},{28,0},{1,5},{5... | collective-permute-start | bytes 983048 | tf_op jit(solution)/shard_map/ppermute | solution.py:384
  37.3 0.0 copy-start.4
  37.3 0.0 collective-permute-start.12
  37.3 3.9 %collective-permute-start.11 = (bf16[192,512]{1,0:T(8,128)(2,1)S(1)}, bf16[192,512]{1,0:T(8,128)(2,1)S(1)}, u32[]{:S(2)}, u32[]{:S(2)}) collective-permute-start(bf16[192,512]{1,0:T(8,128)(2,1)S(1)} %get-tuple-element.15.first), channel_id=1, source_target_pairs={{4,0},{8,4},{12,8},{16,12},{20,16},{24,20},{28,24},{0,28},{5,1},{9... | collective-permute-start | bytes 589832 | tf_op jit(solution)/shard_map/ppermute | solution.py:385
  41.3 0.0 collective-permute-done.13.across
  41.3 0.2 collective-permute-start.14
  41.5 0.0 copy-done.4
  41.5 0.6 %reshape.14.blocks_ref = s32[8]{0:T(128)} reshape(s32[2,4]{1,0:T(2,128)S(1)} %and_select_fusion) | data formatting | bytes 64 | tf_op jit(solution)/shard_map/reshape | solution.py:403
  42.1 0.0 collective-permute-done.12.beside
  42.1 0.5 collective-permute-done.14.opposite
  42.6 13.5 %factor.1.inverse = bf16[128,512]{1,0:T(8,128)(2,1)S(1)} custom-call(s32[8]{0:T(128)} %pad_add_fusion.refs_0_.which_ref, f32[264,128]{1,0:T(8,128)S(1)} %add.23.share, f32[264,128]{1,0:T(8,128)S(1)} %collective-permute-done.12.beside, f32[264,128]{1,0:T(8,128)S(1)} %collective-permute-done.13.across, f32[264,128]{1,0:T(8,128)S(1)} %collective-permute-done.14.opposite), custom_call_target="tpu_custom_call" | custom-call | tf_op jit(solution)/shard_map/factor/pallas_call | solution.py:388
  56.2 0.0 collective-permute-done.11.high
  56.2 0.0 collective-permute-done.10.low
  56.2 0.0 copy-done
  56.2 2.2 %project.1 = bf16[2,128,512]{2,1,0:T(8,128)(2,1)} custom-call(s32[8]{0:T(128)} %reshape.14.blocks_ref, s32[2]{0:T(128)} %counts_ref.1, bf16[320,512]{1,0:T(8,128)(2,1)S(1)} %collective-permute-done.10.low, bf16[192,512]{1,0:T(8,128)(2,1)S(1)} %get-tuple-element.15.first, bf16[320,512]{1,0:T(8,128)(2,1)S(1)} %get-tuple-element.14.second, ...), custom_call_target="tpu_custom_call" | custom-call | tf_op jit(solution)/shard_map/project/pallas_call | solution.py:406
  (4 shorter events, 0.1 us)
Async XLA Ops:
  0.0 14.5 %copy-start.1 = (bf16[512,128]{1,0:T(8,128)(2,1)S(1)}, bf16[512,128]{1,0:T(8,128)(2,1)}, u32[]{:S(2)}) copy-start(bf16[512,128]{1,0:T(8,128)(2,1)} %refs_3_.1) | copy-start | bytes 393220
  0.0 8.5 %collective-permute-start.1 = (bf16[512,128]{1,0:T(8,128)(2,1)}, bf16[512,128]{1,0:T(8,128)(2,1)S(1)}, u32[]{:S(2)}, u32[]{:S(2)}) collective-permute-start(bf16[512,128]{1,0:T(8,128)(2,1)} %refs_3_.1), channel_id=1, source_target_pairs={{0,2},{1,3},{2,0},{3,1},{4,6},{5,7},{6,4},{7,5},{8,10},{9,11},{10,... | collective-permute-start | bytes 393224 | tf_op jit(solution)/shard_map/ppermute | solution.py:304
  2.9 11.5 %collective-permute-start = (bf16[512,128]{1,0:T(8,128)(2,1)}, bf16[512,128]{1,0:T(8,128)(2,1)S(1)}, u32[]{:S(2)}, u32[]{:S(2)}) collective-permute-start(bf16[512,128]{1,0:T(8,128)(2,1)} %refs_3_.1), channel_id=1, source_target_pairs={{0,1},{1,0},{2,3},{3,2},{4,5},{5,4},{6,7},{7,6},{8,9},{9,8},{10,11... | collective-permute-start | bytes 393224 | tf_op jit(solution)/shard_map/ppermute | solution.py:304
  3.9 6.2 %collective-permute-start.3 = (bf16[144,128]{1,0:T(8,128)(2,1)S(1)}, bf16[144,128]{1,0:T(8,128)(2,1)S(1)}, u32[]{:S(2)}, u32[]{:S(2)}) collective-permute-start(bf16[144,128]{1,0:T(8,128)(2,1)S(1)} %pack.1), channel_id=1, source_target_pairs={{4,0},{8,4},{12,8},{16,12},{20,16},{24,20},{28,24},{0,28},{5,1},{9... | collective-permute-start | bytes 110600 | tf_op jit(solution)/shard_map/ppermute | solution.py:353
  8.5 6.0 %collective-permute-start.2 = (bf16[512,128]{1,0:T(8,128)(2,1)S(1)}, bf16[512,128]{1,0:T(8,128)(2,1)S(1)}, u32[]{:S(2)}, u32[]{:S(2)}) collective-permute-start(bf16[512,128]{1,0:T(8,128)(2,1)S(1)} %collective-permute-done.1.refs_5_), channel_id=1, source_target_pairs={{0,1},{1,0},{2,3},{3,2},{4,5},{5,4},{6,7},{7,6},{8,9},{9,8},{10,11... | collective-permute-start | bytes 393224 | tf_op jit(solution)/shard_map/ppermute | solution.py:304
  10.1 3.6 %collective-permute-start.6 = (bf16[144,128]{1,0:T(8,128)(2,1)S(1)}, bf16[144,128]{1,0:T(8,128)(2,1)S(1)}, u32[]{:S(2)}, u32[]{:S(2)}) collective-permute-start(bf16[144,128]{1,0:T(8,128)(2,1)S(1)} %collective-permute-done.3.refs_7_), channel_id=1, source_target_pairs={{0,3},{1,2},{2,1},{3,0},{4,7},{5,6},{6,5},{7,4},{8,11},{9,10},{10,... | collective-permute-start | bytes 110600 | tf_op jit(solution)/shard_map/ppermute | solution.py:304
  10.1 4.3 %collective-permute-start.5 = (bf16[144,128]{1,0:T(8,128)(2,1)S(1)}, bf16[144,128]{1,0:T(8,128)(2,1)S(1)}, u32[]{:S(2)}, u32[]{:S(2)}) collective-permute-start(bf16[144,128]{1,0:T(8,128)(2,1)S(1)} %collective-permute-done.3.refs_7_), channel_id=1, source_target_pairs={{0,2},{1,3},{2,0},{3,1},{4,6},{5,7},{6,4},{7,5},{8,10},{9,11},{10,... | collective-permute-start | bytes 110600 | tf_op jit(solution)/shard_map/ppermute | solution.py:304
  11.4 3.1 %collective-permute-start.4 = (bf16[144,128]{1,0:T(8,128)(2,1)S(1)}, bf16[144,128]{1,0:T(8,128)(2,1)S(1)}, u32[]{:S(2)}, u32[]{:S(2)}) collective-permute-start(bf16[144,128]{1,0:T(8,128)(2,1)S(1)} %collective-permute-done.3.refs_7_), channel_id=1, source_target_pairs={{0,1},{1,0},{2,3},{3,2},{4,5},{5,4},{6,7},{7,6},{8,9},{9,8},{10,11... | collective-permute-start | bytes 110600 | tf_op jit(solution)/shard_map/ppermute | solution.py:304
  12.0 2.5 %copy-start.3 = (f32[512]{0:T(512)S(1)}, f32[512]{0:T(512)}, u32[]{:S(2)}) copy-start(f32[512]{0:T(512)} %param.10) | copy-start | bytes 6148
  12.0 2.5 %copy-start.2 = (f32[512]{0:T(512)S(1)}, f32[512]{0:T(512)}, u32[]{:S(2)}) copy-start(f32[512]{0:T(512)} %param.11) | copy-start | bytes 6148
  16.6 39.6 %copy-start = (bf16[2,512,512]{2,1,0:T(8,128)(2,1)S(1)}, bf16[2,512,512]{2,1,0:T(8,128)(2,1)}, u32[]{:S(2)}) copy-start(bf16[2,512,512]{2,1,0:T(8,128)(2,1)} %shapes.1) | copy-start | bytes 3145732
  16.6 8.0 %collective-permute-start.7 = (f32[264,128]{1,0:T(8,128)S(1)}, f32[264,128]{1,0:T(8,128)S(1)}, u32[]{:S(2)}, u32[]{:S(2)}) collective-permute-start(f32[264,128]{1,0:T(8,128)S(1)} %get-tuple-element.11), channel_id=1, source_target_pairs={{0,16},{4,20},{8,24},{12,28},{16,0},{20,4},{24,8},{28,12},{1,17},{... | collective-permute-start | bytes 405512 | tf_op jit(solution)/shard_map/ppermute | solution.py:304
  24.6 5.1 %collective-permute-start.8 = (f32[264,128]{1,0:T(8,128)S(1)}, f32[264,128]{1,0:T(8,128)S(1)}, u32[]{:S(2)}, u32[]{:S(2)}) collective-permute-start(f32[264,128]{1,0:T(8,128)S(1)} %add.21), channel_id=1, source_target_pairs={{0,8},{4,12},{8,0},{12,4},{16,24},{20,28},{24,16},{28,20},{1,9},{5... | collective-permute-start | bytes 405512 | tf_op jit(solution)/shard_map/ppermute | solution.py:304
  29.7 5.1 %collective-permute-start.9 = (f32[264,128]{1,0:T(8,128)S(1)}, f32[264,128]{1,0:T(8,128)S(1)}, u32[]{:S(2)}, u32[]{:S(2)}) collective-permute-start(f32[264,128]{1,0:T(8,128)S(1)} %add.22), channel_id=1, source_target_pairs={{0,4},{4,0},{8,12},{12,8},{16,20},{20,16},{24,28},{28,24},{1,5},{5... | collective-permute-start | bytes 405512 | tf_op jit(solution)/shard_map/ppermute | solution.py:304
  34.8 6.4 %collective-permute-start.13 = (f32[264,128]{1,0:T(8,128)S(1)}, f32[264,128]{1,0:T(8,128)S(1)}, u32[]{:S(2)}, u32[]{:S(2)}) collective-permute-start(f32[264,128]{1,0:T(8,128)S(1)} %add.23.share), channel_id=1, source_target_pairs={{0,2},{1,3},{2,0},{3,1},{4,6},{5,7},{6,4},{7,5},{8,10},{9,11},{10,... | collective-permute-start | bytes 405512 | tf_op jit(solution)/shard_map/ppermute | solution.py:304
  36.5 19.6 %collective-permute-start.10 = (bf16[320,512]{1,0:T(8,128)(2,1)S(1)}, bf16[320,512]{1,0:T(8,128)(2,1)S(1)}, u32[]{:S(2)}, u32[]{:S(2)}) collective-permute-start(bf16[320,512]{1,0:T(8,128)(2,1)S(1)} %get-tuple-element.14.second), channel_id=1, source_target_pairs={{0,4},{4,8},{8,12},{12,16},{16,20},{20,24},{24,28},{28,0},{1,5},{5... | collective-permute-start | bytes 983048 | tf_op jit(solution)/shard_map/ppermute | solution.py:384
  37.3 4.2 %copy-start.4 = (s32[2,4]{1,0:T(2,128)S(1)}, s32[2,4]{1,0:T(2,128)}, u32[]{:S(2)}) copy-start(s32[2,4]{1,0:T(2,128)} %param.14) | copy-start | bytes 100
  37.3 4.8 %collective-permute-start.12 = (f32[264,128]{1,0:T(8,128)S(1)}, f32[264,128]{1,0:T(8,128)S(1)}, u32[]{:S(2)}, u32[]{:S(2)}) collective-permute-start(f32[264,128]{1,0:T(8,128)S(1)} %add.23.share), channel_id=1, source_target_pairs={{0,1},{1,0},{2,3},{3,2},{4,5},{5,4},{6,7},{7,6},{8,9},{9,8},{10,11... | collective-permute-start | bytes 405512 | tf_op jit(solution)/shard_map/ppermute | solution.py:304
  37.3 18.8 %collective-permute-start.11 = (bf16[192,512]{1,0:T(8,128)(2,1)S(1)}, bf16[192,512]{1,0:T(8,128)(2,1)S(1)}, u32[]{:S(2)}, u32[]{:S(2)}) collective-permute-start(bf16[192,512]{1,0:T(8,128)(2,1)S(1)} %get-tuple-element.15.first), channel_id=1, source_target_pairs={{4,0},{8,4},{12,8},{16,12},{20,16},{24,20},{28,24},{0,28},{5,1},{9... | collective-permute-start | bytes 589832 | tf_op jit(solution)/shard_map/ppermute | solution.py:385
  41.3 1.4 %collective-permute-start.14 = (f32[264,128]{1,0:T(8,128)S(1)}, f32[264,128]{1,0:T(8,128)S(1)}, u32[]{:S(2)}, u32[]{:S(2)}) collective-permute-start(f32[264,128]{1,0:T(8,128)S(1)} %collective-permute-done.13.across), channel_id=1, source_target_pairs={{0,1},{1,0},{2,3},{3,2},{4,5},{5,4},{6,7},{7,6},{8,9},{9,8},{10,11... | collective-permute-start | bytes 405512 | tf_op jit(solution)/shard_map/ppermute | solution.py:304
